TPU v7x, 32 devices: a whole 2x2x4 slice. The times are simulated.
32 devices in a mesh: seq: 16 (over z, y, core), col: 2 (over x).
Axes of the slice: x: 2, y: 2, z: 4, core: 2. Of those that a mesh axis runs over, the one named last changes fastest.
Arguments:
- tokens: bfloat16 [16384, 512], P('seq', 'col'), may hold values from -50 to 50
- cotangent: bfloat16 [16384, 512], P('seq', 'col'), may hold values from -6 to 6
- weight_in: bfloat16 [512, 4, 4, 128], P(None, None, 'col'), may hold values from -0.25 to 0.25
- weight_out: bfloat16 [4, 128, 512], P('col'), may hold values from -0.25 to 0.25
- history_ids: int32 [16384], replicated, may hold values from 0 to 7, never falling along the last dimension, each value on 1 to 4096 neighbouring positions
Outputs:
- out: bfloat16 [16384, 512], P('seq', 'col')
- grad_tokens: bfloat16 [16384, 512], P('seq', 'col')
- grad_weight_in: float32 [512, 4, 4, 128], P(None, None, 'col')
- grad_weight_out: float32 [4, 128, 512], P('col')
Inputs may be any that keep to these rules, and one draw needn't show every extreme that they name: history_ids never fall along the stream; every id occurs; each history holds 1 to 4096 tokens and one holds exactly 4096.
All inputs are finite; a program needn't handle non-finite values.
Results may differ from a plain program's by a relative error of at most 0.0092.
Values may be sent and summed in bfloat16 or wider, within the bound.
No kernel may reach another device: no remote copies, remote signals or barrier semaphores. Data moves between devices by JAX's collectives and lax.ppermute only.
A program may use at most 192 MiB of HBM per device.

v0:
```python
import math

import jax
import jax.numpy as jnp
from jax import lax
from jax.experimental import pallas as pl
from jax.experimental.pallas import tpu as pltpu
from jax.sharding import PartitionSpec as P

MAXLEN = 4096
TILE = 512

epsilon = 1e-05
head_floor = 1.0
f32 = jnp.float32
bf16 = jnp.bfloat16


def swap(block, axis, bit):
    return lax.ppermute(block, axis, [(i, i ^ bit) for i in range(lax.axis_size(axis))])


def shift(block, axis, distance):
    devices = range(lax.axis_size(axis))
    return lax.ppermute(block, axis, [(i, i + distance) for i in devices if i + distance in devices])


def layer_norm(values, offset):
    center = values - jnp.mean(values, axis=-1, keepdims=True)
    inv_std = lax.rsqrt(jnp.mean(center * center, axis=-1, keepdims=True) + offset)
    return (center * inv_std, inv_std)


def norm_back(grad_in, normed, inv_std):
    return inv_std * (
        grad_in
        - jnp.mean(grad_in, axis=-1, keepdims=True)
        - normed * jnp.mean(grad_in * normed, axis=-1, keepdims=True)
    )


NT = (((1,), (1,)), ((), ()))
TN = (((0,), (0,)), ((), ()))


def dot(a, b, dims=(((1,), (0,)), ((), ()))):
    return lax.dot_general(a, b, dims, preferred_element_type=f32)


def gate_of(inputs):
    return 0.5 + 0.5 * jnp.tanh(0.5 * inputs)


def aligned(start, size):
    return pl.ds(pl.multiple_of(start, size), size)


def project_kernel(core_ref, mine_a, mine_b, other_a, other_b, w_ref, normed_ref, slope_ref, *part_refs):
    size = 256
    count = mine_a.shape[0]
    core = core_ref[0]
    for first, second, where in ((mine_a, mine_b, core), (other_a, other_b, 1 - core)):

        def rows_step(step, carry, first=first, second=second, where=where):
            rows = aligned(step * size, size)
            into = aligned(where * count + step * size, size)
            values = jnp.concatenate([first[rows, :].astype(f32), second[rows, :].astype(f32)], axis=1)
            normed = layer_norm(values, epsilon)[0].astype(bf16)
            normed_ref[into, :] = normed
            pre = dot(normed, w_ref[...])
            gate = gate_of(pre)
            act = pre * gate
            slope_ref[into, :] = (gate + act * (1.0 - gate)).astype(bf16)
            width = part_refs[0].shape[1]
            for p, part in enumerate(part_refs):
                part[into, :] = act[:, p * width : (p + 1) * width].astype(bf16)
            return carry

        lax.fori_loop(0, count // size, rows_step, 0)


def middle_kernel(core_ref, att_ref, up_ref, slope_ref, mine_a, mine_b, other_a, other_b, w_ref, narrow_ref, gated_ref, pre_up_ref):
    size = 256
    count = mine_a.shape[0]
    half = mine_a.shape[1]
    core = core_ref[0]
    for first, second, where in ((mine_a, mine_b, core), (other_a, other_b, 1 - core)):

        def rows_step(step, carry, first=first, second=second, where=where):
            rows = aligned(step * size, size)
            into = aligned(where * count + step * size, size)
            head_normed, head_scale = layer_norm(att_ref[into, :], head_floor)
            up = up_ref[into, :].astype(f32)
            gated_ref[into, :] = (head_normed * up).astype(bf16)
            grad = dot(first[rows, :], w_ref[:, :half], NT) + dot(second[rows, :], w_ref[:, half:], NT)
            pre_up_ref[into, :] = (grad * head_normed * slope_ref[into, :].astype(f32)).astype(bf16)
            narrow_ref[into, :] = norm_back(grad * up, head_normed, head_scale).astype(bf16)
            return carry

        lax.fori_loop(0, count // size, rows_step, 0)


def outer_kernel(core_ref, gated_ref, pre_up_ref, normed_ref, mine_a, mine_b, other_a, other_b, w_ref, send_ref, keep_ref, grad_ref):
    count, half = mine_a.shape
    width = gated_ref.shape[1]
    core = core_ref[0]
    mine = aligned(core * count, count)
    other = aligned((1 - core) * count, count)
    send_ref[...] = dot(gated_ref[other, :], w_ref[...]).astype(bf16)
    keep_ref[...] = dot(gated_ref[mine, :], w_ref[...]).astype(bf16)
    grad_ref[:, :width] = dot(normed_ref[...], pre_up_ref[...], TN)
    grad_ref[:half, width:] = dot(mine_a[...], gated_ref[mine, :], TN) + dot(other_a[...], gated_ref[other, :], TN)
    grad_ref[half:, width:] = dot(mine_b[...], gated_ref[mine, :], TN) + dot(other_b[...], gated_ref[other, :], TN)


def for_tiles(low_ref, first_ref, last_ref, q_tiles, k_tiles, block_off, query_off, step):
    def query_tile(i, carry):
        start = jnp.maximum(low_ref[i] - block_off, 0)
        stop = jnp.minimum(query_off + i + 1 - block_off, k_tiles)
        rows = aligned(i * TILE, TILE)

        def key_tile(j, inner):
            cols = aligned(j * TILE, TILE)
            near = query_off + i - block_off - j
            whole = (near > 0) & (first_ref[block_off + j] == last_ref[query_off + i])

            @pl.when(whole)
            def _():
                step(rows, cols, None)

            @pl.when(jnp.logical_not(whole))
            def _():
                step(rows, cols, near * TILE)

            return inner

        lax.fori_loop(start, stop, key_tile, 0)
        return carry

    lax.fori_loop(0, q_tiles, query_tile, 0)


def forward_kernel(low_ref, first_ref, last_ref, q_ref, k_ref, v_ref, idq_ref, idk_ref, *rest, block_off, query_off, scale):
    out_ref = rest[-1]
    if len(rest) == 2:
        out_ref[...] = rest[0][...]
    else:
        out_ref[...] = jnp.zeros(out_ref.shape, f32)

    def step(rows, cols, reach):
        half = dot(q_ref[rows, :], k_ref[cols, :], NT) * (0.5 * scale)
        if reach is not None:
            pos_q = lax.broadcasted_iota(jnp.int32, (TILE, TILE), 0)
            pos_k = lax.broadcasted_iota(jnp.int32, (TILE, TILE), 1)
            ok = (idq_ref[rows, :] == idk_ref[:, cols]) & (pos_k - pos_q <= reach)
            half = jnp.where(ok, half, 0.0)
        weights = half + half * jnp.tanh(half)
        out_ref[rows, :] += dot(weights.astype(bf16), v_ref[cols, :])

    for_tiles(
        low_ref, first_ref, last_ref, q_ref.shape[0] // TILE, k_ref.shape[0] // TILE, block_off, query_off, step
    )


def backward_kernel(low_ref, first_ref, last_ref, core_ref, q_ref, g_ref, k_ref, v_ref, idq_ref, idk_ref, w_ref, slope_hbm, normed_hbm, *rest, block_off, query_off, scale, count_in):
    before = rest[:count_in]
    send_ref, keep_ref, grad_ref = rest[count_in : count_in + 3]
    if block_off != query_off:
        dq_ref = rest[count_in + 3]
    else:
        dq_ref = rest[-6]
    dk_ref, dv_ref, slope_ref, normed_ref, sems = rest[-5:]
    q_tiles = q_ref.shape[0] // TILE
    k_tiles = k_ref.shape[0] // TILE
    own = block_off == query_off
    slope_copy = pltpu.make_async_copy(slope_hbm, slope_ref, sems.at[0])
    normed_copy = pltpu.make_async_copy(normed_hbm, normed_ref, sems.at[1])
    slope_copy.start()
    normed_copy.start()
    width = k_ref.shape[1]
    if len(before) > 0:
        dq_ref[...] = before[0][...]
    else:
        dq_ref[...] = jnp.zeros(dq_ref.shape, f32)
    dk_ref[...] = jnp.zeros(dk_ref.shape, f32)
    dv_ref[...] = jnp.zeros(dv_ref.shape, f32)

    def step(rows, cols, reach):
        q = q_ref[rows, :]
        g = g_ref[rows, :]
        k = k_ref[cols, :]
        half = dot(k, q, NT) * (0.5 * scale)
        grad = dot(v_ref[cols, :], g, NT)
        if reach is not None:
            pos_k = lax.broadcasted_iota(jnp.int32, (TILE, TILE), 0)
            pos_q = lax.broadcasted_iota(jnp.int32, (TILE, TILE), 1)
            ok = (idk_ref[cols, :] == idq_ref[:, rows]) & (pos_k - pos_q <= reach)
            half = jnp.where(ok, half, 0.0)
            grad = jnp.where(ok, grad, 0.0)
        twice = (1.0 + jnp.tanh(half)).astype(bf16)
        weights = half.astype(bf16) * twice
        gate = twice * bf16(0.5)
        grad = (gate + weights * (bf16(1.0) - gate)) * grad.astype(bf16)
        dv_ref[cols, :] += dot(weights, g)
        dk_ref[cols, :] += dot(grad, q)
        dq_ref[rows, :] += dot(grad, k, TN)

    for_tiles(low_ref, first_ref, last_ref, q_tiles, k_tiles, block_off, query_off, step)
    slope_copy.wait()
    normed_copy.wait()
    core = core_ref[0]
    count = send_ref.shape[0]
    base = width if own else 0

    def narrow(grads, part):
        into = slope_ref.at[:, part * width : (part + 1) * width]
        into[...] = (grads * into[...].astype(f32)).astype(bf16)

    if own:
        slope_ref[:, :width] = before[-1][...]
        narrow(dv_ref[...], 1)
        narrow(dq_ref[...] * scale, 2)
        narrow(dk_ref[...] * scale, 3)
    else:
        narrow(dv_ref[...], 0)
        narrow(dk_ref[...] * scale, 1)
    send_ref[...] = dot(slope_ref[aligned((1 - core) * count, count), :], w_ref[...], NT).astype(bf16)
    keep_ref[...] = dot(slope_ref[aligned(core * count, count), :], w_ref[...], NT).astype(bf16)
    grads = dot(normed_ref[...], slope_ref[:, base:], TN)
    if own:
        grad_ref[:, :width] = grads[:, :width] + before[1][:, :width]
        grad_ref[:, width : 2 * width] = grads[:, width : 2 * width]
        grad_ref[:, 2 * width :] = grads[:, 2 * width :] + before[1][:, width:]
    elif len(before) > 1:
        grad_ref[...] = grads + before[1][...]
    else:
        grad_ref[...] = grads


def vmem_call(kernel, tables, arrays, outs, aliases=None, hbm=(), scratch=(), **static):
    whole = pl.BlockSpec(memory_space=pltpu.VMEM)
    table = pl.BlockSpec(memory_space=pltpu.SMEM)
    place = [pl.BlockSpec(memory_space=pl.ANY) if i in hbm else whole for i in range(len(arrays))]
    return pl.pallas_call(
        lambda *refs: kernel(*refs, **static),
        out_shape=outs,
        in_specs=[table] * len(tables) + place,
        out_specs=jax.tree.map(lambda _: whole, outs),
        input_output_aliases=aliases or {},
        scratch_shapes=list(scratch),
        compiler_params=pltpu.CompilerParams(vmem_limit_bytes=60 << 20),
    )(*tables, *arrays)


def layer(tokens, cotangent, weight_in, weight_out, history_ids):
    row_count, half_width = tokens.shape
    seq_count = lax.axis_size("seq")
    device_pos = lax.axis_index("seq")
    core = device_pos % 2
    pair = device_pos // 2
    odd = pair % 2 == 1
    block = 2 * row_count
    width = 2 * half_width
    head_size = weight_out.shape[1]
    scale = head_size ** (-0.5)
    if (MAXLEN - 2 + block) // block != 2:
        raise ValueError("reach")
    tiles = block // TILE
    core_table = core.astype(jnp.int32).reshape(1)

    def over(array, axis, bit):
        return swap(array, axis, bit)

    far = shift(tokens, "seq", 4)
    own_other = over(tokens, "col", 1)
    own_set = (tokens, own_other, over(tokens, "seq", 1), over(own_other, "seq", 1))
    near = over(jnp.where(odd, far, tokens), "seq", 2)
    far_other = over(far, "col", 1)
    far_set = (far, far_other, over(far, "seq", 1), over(far_other, "seq", 1))
    near_other = over(near, "col", 1)
    near_set = (near, near_other, over(near, "seq", 1), over(near_other, "seq", 1))
    cot_other = over(cotangent, "col", 1)
    cot_set = (cotangent, cot_other, over(cotangent, "seq", 1), over(cot_other, "seq", 1))

    flip = lax.axis_index("col") == 1
    w_in = lax.dynamic_index_in_dim(weight_in, core, 2, keepdims=False).reshape(width, 4 * head_size)
    w_in = jnp.where(flip, jnp.roll(w_in, half_width, axis=0), w_in)
    w_out = lax.dynamic_index_in_dim(weight_out, core, 0, keepdims=False)
    w_out = jnp.where(flip, jnp.roll(w_out, half_width, axis=1), w_out)
    w_kv = jnp.concatenate([w_in[:, head_size : 2 * head_size], w_in[:, 3 * head_size :]], axis=1)

    padded = jnp.concatenate([jnp.full((2 * block,), -1, jnp.int32), history_ids])
    ids = lax.dynamic_slice_in_dim(padded, pair * block, 3 * block)
    by_tile = ids.reshape(-1, TILE)
    first, last = by_tile[:, 0], by_tile[:, -1]
    low = jnp.sum((last[None, :] < first[2 * tiles :, None]).astype(jnp.int32), axis=1)
    tables = (low, first, last)
    own_ids = ids[2 * block :]

    def shape(rows, cols, dtype=bf16):
        return jax.ShapeDtypeStruct((rows, cols), dtype)

    def project(token_set, weights):
        count = weights.shape[1] // head_size
        outs = (shape(block, width), shape(block, count * head_size)) + (shape(block, head_size),) * count
        return vmem_call(project_kernel, (core_table,), (*token_set, weights), outs)

    normed_own, slope_own, up_part, value_own, query, key_own = project(own_set, w_in)
    normed_far, slope_far, value_far, key_far = project(far_set, w_kv)
    normed_near, slope_near, value_near, key_near = project(near_set, w_kv)
    keys = [key_far, key_near, key_own]
    values = [value_far, value_near, value_own]

    def forward(which, before):
        span = slice(which * block, (which + 1) * block)
        arrays = [query, keys[which], values[which], own_ids[:, None], ids[None, span]]
        aliases = {}
        if before is not None:
            aliases = {3 + len(arrays): 0}
            arrays.append(before)
        return vmem_call(
            forward_kernel,
            tables,
            arrays,
            shape(block, head_size, f32),
            aliases,
            block_off=which * tiles,
            query_off=2 * tiles,
            scale=scale,
        )

    attended = forward(2, None)
    attended = forward(0, attended)
    attended = forward(1, attended)

    grad_narrow, gated, pre_up = vmem_call(
        middle_kernel,
        (core_table,),
        (attended, up_part, slope_own[:, :head_size], *cot_set, w_out),
        (shape(block, head_size),) * 3,
    )
    out_send, out_keep, grad_early = vmem_call(
        outer_kernel,
        (core_table,),
        (gated, pre_up, normed_own, *cot_set, w_out),
        (shape(row_count, width), shape(row_count, width), shape(width, 2 * head_size, f32)),
    )

    def over_heads(send, keep):
        keep = keep.astype(f32) + over(send, "seq", 1).astype(f32)
        return keep[:, :half_width] + over(keep[:, half_width:].astype(bf16), "col", 1).astype(f32)

    def backward(which, weights, slope, normed, before):
        span = slice(which * block, (which + 1) * block)
        arrays = [query, grad_narrow, keys[which], values[which], own_ids[None, :], ids[span, None], weights, slope, normed]
        count = weights.shape[1]
        own = which == 2
        grads = count - head_size if own else count
        outs = [shape(row_count, width), shape(row_count, width), shape(width, grads, f32)]
        scratch = [
            pltpu.VMEM((block, head_size), f32),
            pltpu.VMEM((block, head_size), f32),
            pltpu.VMEM((block, count), bf16),
            pltpu.VMEM((block, width), bf16),
            pltpu.SemaphoreType.DMA((2,)),
        ]
        if own:
            scratch = [pltpu.VMEM((block, head_size), f32)] + scratch
        else:
            outs.append(shape(block, head_size, f32))
        return vmem_call(
            backward_kernel,
            (*tables, core_table),
            arrays + list(before),
            tuple(outs),
            hbm=(len(arrays) - 2, len(arrays) - 1),
            scratch=scratch,
            block_off=which * tiles,
            query_off=2 * tiles,
            scale=scale,
            count_in=len(before),
        )

    near_send, near_keep, grad_kv, grad_query = backward(1, w_kv, slope_near, normed_near, ())
    near_part = over_heads(near_send, near_keep)
    near_back = over(near_part.astype(bf16), "seq", 2).astype(f32)
    far_send, far_keep, grad_kv, grad_query = backward(0, w_kv, slope_far, normed_far, (grad_query, grad_kv))
    far_part = over_heads(far_send, far_keep) + jnp.where(odd, near_back, 0.0)
    far_back = shift(far_part.astype(bf16), "seq", -4).astype(f32)
    own_send, own_keep, grad_own = backward(2, w_in, slope_own, normed_own, (grad_query, grad_kv, pre_up))
    own_part = over_heads(own_send, own_keep)
    grad_normed = own_part + jnp.where(odd, 0.0, near_back) + far_back
    out = (tokens.astype(f32) + over_heads(out_send, out_keep)).astype(bf16)

    total = jnp.concatenate([grad_early[:, :head_size], grad_own, grad_early[:, head_size:]], axis=1)
    bits = []
    while 2 << len(bits) < seq_count:
        bits.append(2 << len(bits))
    for bit in bits:
        size = total.shape[0] // 2
        high = (device_pos & bit) // bit
        sent = lax.dynamic_slice_in_dim(total, (1 - high) * size, size).astype(bf16)
        total = lax.dynamic_slice_in_dim(total, high * size, size) + over(sent, "seq", bit).astype(f32)
    total = total.astype(bf16)
    for bit in reversed(bits):
        other = over(total, "seq", bit)
        total = jnp.where(
            (device_pos & bit) != 0,
            jnp.concatenate([other, total], axis=0),
            jnp.concatenate([total, other], axis=0),
        )

    inv_root = 1.0 / math.sqrt(row_count * seq_count)
    total = jnp.where(flip, jnp.roll(total, half_width, axis=0), total)
    both = jnp.stack([total, over(total, "seq", 1)])
    both = jnp.where(core == 0, both, both[::-1])
    grad_weight_in = both[:, :, : 4 * head_size].reshape(2, width, 4, head_size).transpose(1, 2, 0, 3)
    grad_weight_in = grad_weight_in.astype(f32) * inv_root
    grad_weight_out = both[:, :, 4 * head_size :].transpose(0, 2, 1).astype(f32) * inv_root

    own_wide = jnp.concatenate([tokens, own_other], axis=1).astype(f32)
    normed, inv_std = layer_norm(own_wide, epsilon)
    normed = normed[:, :half_width]
    sums = jnp.stack([jnp.sum(grad_normed, axis=1), jnp.sum(grad_normed * normed, axis=1)])
    sums = (sums + over(sums, "col", 1)) / width
    grad_tokens = inv_std * (grad_normed - sums[0][:, None] - normed * sums[1][:, None])
    grad_tokens = (grad_tokens + cotangent.astype(f32)).astype(bf16)
    return (out, grad_tokens, grad_weight_in, grad_weight_out)


def solution(mesh):
    placed = (
        P("seq", "col"),
        P("seq", "col"),
        P(None, None, "col", None),
        P("col", None, None),
        P(),
    )
    return jax.shard_map(
        layer,
        mesh=mesh,
        in_specs=placed,
        out_specs=(
            P("seq", "col"),
            P("seq", "col"),
            P(None, None, "col", None),
            P("col", None, None),
        ),
        check_vma=False,
    )
```

profile of v0, /device:TPU:0, one launch (start us, length us, event | category | flops | bytes accessed | tf_op | source)
XLA Modules:
  0.0 281.9 jit_solution(16323909129319965081)
XLA Ops:
  0.7 5.9 %collective-permute-start.3 = (bf16[1024,256]{1,0:T(8,128)(2,1)}, bf16[1024,256]{1,0:T(8,128)(2,1)}, u32[]{:S(2)}, u32[]{:S(2)}) collective-permute-start(bf16[1024,256]{1,0:T(8,128)(2,1)} %refs_1_.1), channel_id=1, source_target_pairs={{0,8},{2,10},{4,12},{6,14},{8,16},{10,18},{12,20},{14,22},{16,24},... | collective-permute-start | bytes 1572872 | tf_op jit(solution)/shard_map/ppermute | solution.py:25
  6.6 1.5 collective-permute-start
  8.6 0.7 pad_dynamic-slice_fusion.3
  9.3 1.1 constant_dynamic-slice_fusion
  10.4 6.8 %collective-permute-done.3.refs_1_ = bf16[1024,256]{1,0:T(8,128)(2,1)} collective-permute-done((bf16[1024,256]{1,0:T(8,128)(2,1)}, bf16[1024,256]{1,0:T(8,128)(2,1)}, u32[]{:S(2)}, u32[]{:S(2)}) %collective-permute-start.3) | collective-permute-done | bytes 524320 | tf_op jit(solution)/shard_map/ppermute | solution.py:25
  17.2 0.9 broadcast_select_fusion
  18.1 2.6 collective-permute-start.4
  20.8 1.3 copy.49
  22.9 1.6 collective-permute-start.8
  24.9 7.1 %collective-permute-done.4.refs_1_ = bf16[1024,256]{1,0:T(8,128)(2,1)} collective-permute-done((bf16[1024,256]{1,0:T(8,128)(2,1)}, bf16[1024,256]{1,0:T(8,128)(2,1)}, u32[]{:S(2)}, u32[]{:S(2)}) %collective-permute-start.4) | collective-permute-done | bytes 524320 | tf_op jit(solution)/shard_map/ppermute | solution.py:20
  32.0 1.5 collective-permute-start.5
  33.5 0.8 convert_reduce_fusion.1.refs_0_
  36.2 7.8 %collective-permute-done.8.refs_2_ = bf16[1024,256]{1,0:T(8,128)(2,1)S(1)} collective-permute-done((bf16[1024,256]{1,0:T(8,128)(2,1)}, bf16[1024,256]{1,0:T(8,128)(2,1)S(1)}, u32[]{:S(2)}, u32[]{:S(2)}) %collective-permute-start.8) | collective-permute-done | bytes 524320 | tf_op jit(solution)/shard_map/ppermute | solution.py:20
  44.6 9.4 %collective-permute-done.5.refs_2_ = bf16[1024,256]{1,0:T(8,128)(2,1)} collective-permute-done((bf16[1024,256]{1,0:T(8,128)(2,1)}, bf16[1024,256]{1,0:T(8,128)(2,1)}, u32[]{:S(2)}, u32[]{:S(2)}) %collective-permute-start.5) | collective-permute-done | bytes 524320 | tf_op jit(solution)/shard_map/ppermute | solution.py:20
  54.0 0.7 pad_dynamic-slice_fusion
  54.7 1.4 copy.43.refs_6_.refs_9_
  56.1 1.3 copy.44.refs_9_
  57.4 1.4 copy.45.refs_9_
  59.6 0.8 pad_maximum_fusion.3.refs_5_.refs_10_
  60.3 8.8 %shard_map.84 = (bf16[2048,512]{1,0:T(8,128)(2,1)}, bf16[2048,512]{1,0:T(8,128)(2,1)}, bf16[2048,128]{1,0:T(8,128)(2,1)}, bf16[2048,128]{1,0:T(8,128)(2,1)}, bf1...) custom-call(s32[1]{0:T(128)} %bitcast.refs_0_.refs_3_, bf16[1024,256]{1,0:T(8,128)(2,1)} %refs_1_.1, ...), custom_call_target="tpu_custom_call" | custom-call | tf_op jit(solution)/shard_map/pallas_call | solution.py:244
  69.2 1.9 slice.124.refs_3_
  71.1 8.9 %shard_map.87.refs_8_ = f32[2048,128]{1,0:T(8,128)} custom-call(s32[4]{0:T(128)} %convert_reduce_fusion.1.refs_0_, s32[12]{0:T(128)} %get-tuple-element.84.refs_1_, s32[12]{0:T(128)} %copy-done.21, bf16[2048,128]{1,0:T(8,128)(2,1)} %get-tuple-element.35.refs_3_.refs_4_, bf16[2048,128]{1,0:T(8,128)(2,1)} %get-tuple-element.40.refs_4_.refs_6_, ...), custom_call_target="tpu_custom_call" | custom-call | tf_op jit(solution)/shard_map/pallas_call | solution.py:244
  80.0 7.0 %shard_map.86 = (bf16[2048,512]{1,0:T(8,128)(2,1)}, bf16[2048,256]{1,0:T(8,128)(2,1)}, bf16[2048,128]{1,0:T(8,128)(2,1)}, bf16[2048,128]{1,0:T(8,128)(2,1)}) custom-call(s32[1]{0:T(128)} %bitcast.refs_0_.refs_3_, bf16[1024,256]{1,0:T(8,128)(2,1)} %collective-permute-done.3.refs_1_, bf16[1024,256]{1,0:T(8,128)(2,1)} %copy-done.14, ...), custom_call_target="tpu_custom_call" | custom-call | tf_op jit(solution)/shard_map/pallas_call | solution.py:244
  87.0 3.1 %shard_map.88.refs_8_ = f32[2048,128]{1,0:T(8,128)} custom-call(s32[4]{0:T(128)} %convert_reduce_fusion.1.refs_0_, s32[12]{0:T(128)} %get-tuple-element.84.refs_1_, s32[12]{0:T(128)} %copy-done.21, bf16[2048,128]{1,0:T(8,128)(2,1)} %get-tuple-element.35.refs_3_.refs_4_, ...), custom_call_target="tpu_custom_call", output_to_operand_aliasing={{}: (8, {})} | custom-call | tf_op jit(solution)/shard_map/pallas_call | solution.py:244
  90.2 7.0 %shard_map.85 = (bf16[2048,512]{1,0:T(8,128)(2,1)}, bf16[2048,256]{1,0:T(8,128)(2,1)}, bf16[2048,128]{1,0:T(8,128)(2,1)}, bf16[2048,128]{1,0:T(8,128)(2,1)}) custom-call(s32[1]{0:T(128)} %bitcast.refs_0_.refs_3_, bf16[1024,256]{1,0:T(8,128)(2,1)} %collective-permute-done.4.refs_1_, bf16[1024,256]{1,0:T(8,128)(2,1)} %collective-permute-done.5.refs_2_, ...), custom_call_target="tpu_custom_call" | custom-call | tf_op jit(solution)/shard_map/pallas_call | solution.py:244
  97.1 3.1 %shard_map.89.refs_1_ = f32[2048,128]{1,0:T(8,128)} custom-call(s32[4]{0:T(128)} %convert_reduce_fusion.1.refs_0_, s32[12]{0:T(128)} %get-tuple-element.84.refs_1_, s32[12]{0:T(128)} %copy-done.21, bf16[2048,128]{1,0:T(8,128)(2,1)} %get-tuple-element.35.refs_3_.refs_4_, ...), custom_call_target="tpu_custom_call", output_to_operand_aliasing={{}: (8, {})} | custom-call | tf_op jit(solution)/shard_map/pallas_call | solution.py:244
  100.3 0.8 copy-done.8
  101.3 5.9 %shard_map.90 = (bf16[2048,128]{1,0:T(8,128)(2,1)}, bf16[2048,128]{1,0:T(8,128)(2,1)}, bf16[2048,128]{1,0:T(8,128)(2,1)}) custom-call(s32[1]{0:T(128)} %bitcast.refs_0_.refs_3_, f32[2048,128]{1,0:T(8,128)} %shard_map.89.refs_1_, bf16[2048,128]{1,0:T(8,128)(2,1)} %get-tuple-element.42.refs_2_, bf16[2048,128]{1,0:T(8,128)(2,1)} %slice.124.refs_3_, ...), custom_call_target="tpu_custom_call" | custom-call | tf_op jit(solution)/shard_map/pallas_call | solution.py:244
  107.2 5.1 %shard_map.91 = (bf16[1024,512]{1,0:T(8,128)(2,1)}, bf16[1024,512]{1,0:T(8,128)(2,1)}, f32[512,256]{1,0:T(8,128)}) custom-call(s32[1]{0:T(128)} %bitcast.refs_0_.refs_3_, bf16[2048,128]{1,0:T(8,128)(2,1)} %get-tuple-element.44.refs_1_, bf16[2048,128]{1,0:T(8,128)(2,1)} %get-tuple-element.45.refs_2_.refs_15_, ...), custom_call_target="tpu_custom_call" | custom-call | tf_op jit(solution)/shard_map/pallas_call | solution.py:244
  112.3 1.1 fusion.9
  113.3 6.8 %shard_map.92 = (bf16[1024,512]{1,0:T(8,128)(2,1)}, bf16[1024,512]{1,0:T(8,128)(2,1)}, f32[512,256]{1,0:T(8,128)}, f32[2048,128]{1,0:T(8,128)}) custom-call(s32[4]{0:T(128)} %convert_reduce_fusion.1.refs_0_, s32[12]{0:T(128)} %get-tuple-element.84.refs_1_, s32[12]{0:T(128)} %copy-done.21, s32[1]{0:T(128)} %bitcast.refs_0_.refs_3_, ...), custom_call_target="tpu_custom_call" | custom-call | tf_op jit(solution)/shard_map/pallas_call | solution.py:244
  120.1 7.3 %shard_map.93 = (bf16[1024,512]{1,0:T(8,128)(2,1)}, bf16[1024,512]{1,0:T(8,128)(2,1)}, f32[512,256]{1,0:T(8,128)}, f32[2048,128]{1,0:T(8,128)}) custom-call(s32[4]{0:T(128)} %convert_reduce_fusion.1.refs_0_, s32[12]{0:T(128)} %get-tuple-element.84.refs_1_, s32[12]{0:T(128)} %copy-done.21, s32[1]{0:T(128)} %bitcast.refs_0_.refs_3_, ...), custom_call_target="tpu_custom_call" | custom-call | tf_op jit(solution)/shard_map/pallas_call | solution.py:244
  127.4 18.0 %shard_map.94 = (bf16[1024,512]{1,0:T(8,128)(2,1)}, bf16[1024,512]{1,0:T(8,128)(2,1)}, f32[512,384]{1,0:T(8,128)}) custom-call(s32[4]{0:T(128)} %convert_reduce_fusion.1.refs_0_, s32[12]{0:T(128)} %get-tuple-element.84.refs_1_, s32[12]{0:T(128)} %copy-done.21, s32[1]{0:T(128)} %bitcast.refs_0_.refs_3_, bf16[2048,128]{1,0:T(8,128)(2,1)} %get-tuple-element.35.refs_3_.refs_4_, ...), custom_call_target="tpu_custom_call" | custom-call | tf_op jit(solution)/shard_map/pallas_call | solution.py:244
  145.4 1.3 pad_maximum_fusion
  146.8 6.1 %collective-permute-start.25 = (bf16[256,640]{1,0:T(8,128)(2,1)S(1)}, bf16[256,640]{1,0:T(8,128)(2,1)S(1)}, u32[]{:S(2)}, u32[]{:S(2)}) collective-permute-start(bf16[256,640]{1,0:T(8,128)(2,1)S(1)} %dynamic-slice_convert_fusion), channel_id=1, source_target_pairs={{0,4},{2,6},{4,0},{6,2},{8,12},{10,14},{12,8},{14,10},{16,20},{18,... | collective-permute-start | bytes 983048 | tf_op jit(solution)/shard_map/ppermute | solution.py:20
  152.9 8.4 %collective-permute-done.25 = bf16[256,640]{1,0:T(8,128)(2,1)S(1)} collective-permute-done((bf16[256,640]{1,0:T(8,128)(2,1)S(1)}, bf16[256,640]{1,0:T(8,128)(2,1)S(1)}, u32[]{:S(2)}, u32[]{:S(2)}) %collective-permute-start.25) | collective-permute-done | bytes 327712 | tf_op jit(solution)/shard_map/ppermute | solution.py:20
  161.4 24.9 %collective-permute-start.26 = (bf16[128,640]{1,0:T(8,128)(2,1)S(1)}, bf16[128,640]{1,0:T(8,128)(2,1)S(1)}, u32[]{:S(2)}, u32[]{:S(2)}) collective-permute-start(bf16[128,640]{1,0:T(8,128)(2,1)S(1)} %dynamic-slice_convert_fusion.1), channel_id=1, source_target_pairs={{0,8},{2,10},{4,12},{6,14},{8,0},{10,2},{12,4},{14,6},{16,24},{18,... | collective-permute-start | bytes 491528 | tf_op jit(solution)/shard_map/ppermute | solution.py:20
  186.6 3.7 %collective-permute-done.26 = bf16[128,640]{1,0:T(8,128)(2,1)S(1)} collective-permute-done((bf16[128,640]{1,0:T(8,128)(2,1)S(1)}, bf16[128,640]{1,0:T(8,128)(2,1)S(1)}, u32[]{:S(2)}, u32[]{:S(2)}) %collective-permute-start.26) | collective-permute-done | bytes 163872 | tf_op jit(solution)/shard_map/ppermute | solution.py:20
  190.4 2.8 collective-permute-start.27
  193.2 2.6 collective-permute-done.27
  195.8 2.8 collective-permute-start.28
  199.2 2.0 collective-permute-done.28
  201.2 1.8 collective-permute-start.29
  203.1 3.6 %collective-permute-done.29 = bf16[128,640]{1,0:T(8,128)(2,1)S(1)} collective-permute-done((bf16[128,640]{1,0:T(8,128)(2,1)S(1)}, bf16[128,640]{1,0:T(8,128)(2,1)S(1)}, u32[]{:S(2)}, u32[]{:S(2)}) %collective-permute-start.29) | collective-permute-done | bytes 163872 | tf_op jit(solution)/shard_map/ppermute | solution.py:20
  206.7 0.8 collective-permute-start.30
  207.9 1.5 collective-permute-start.17
  209.8 0.8 collective-permute-start.22
  211.0 1.3 collective-permute-start.19
  212.8 0.8 collective-permute-start.15
  214.5 30.8 %collective-permute-done.19 = bf16[1024,256]{1,0:T(8,128)(2,1)S(1)} collective-permute-done((bf16[1024,256]{1,0:T(8,128)(2,1)S(1)}, bf16[1024,256]{1,0:T(8,128)(2,1)S(1)}, u32[]{:S(2)}, u32[]{:S(2)}) %collective-permute-start.19) | collective-permute-done | bytes 524320 | tf_op jit(solution)/shard_map/ppermute | solution.py:20
  245.4 1.4 collective-permute-start.20
  247.1 5.3 %collective-permute-done.15 = bf16[1024,256]{1,0:T(8,128)(2,1)S(1)} collective-permute-done((bf16[1024,256]{1,0:T(8,128)(2,1)S(1)}, bf16[1024,256]{1,0:T(8,128)(2,1)S(1)}, u32[]{:S(2)}, u32[]{:S(2)}) %collective-permute-start.15) | collective-permute-done | bytes 524320 | tf_op jit(solution)/shard_map/ppermute | solution.py:20
  252.4 1.1 fusion.6
  253.6 1.0 collective-permute-done.20
  254.9 1.3 collective-permute-start.23
  256.5 1.6 convert_multiply_fusion
  258.1 7.9 %collective-permute-done.23 = bf16[1024,256]{1,0:T(8,128)(2,1)S(1)} collective-permute-done((bf16[1024,256]{1,0:T(8,128)(2,1)S(1)}, bf16[1024,256]{1,0:T(8,128)(2,1)S(1)}, u32[]{:S(2)}, u32[]{:S(2)}) %collective-permute-start.23) | collective-permute-done | bytes 524320 | tf_op jit(solution)/shard_map/ppermute | solution.py:25
  266.0 1.3 fusion.7
  267.3 1.5 collective-permute-start.24
  268.8 0.8 multiply_bitcast_fusion
  269.6 2.9 %mul.92 = f32[2,512,4,128]{3,2,1,0:T(4,128)} reshape(f32[2,512,512]{2,1,0:T(8,128)} %convert_multiply_fusion) | data formatting | bytes 4194304 | tf_op jit(solution)/shard_map/mul | solution.py:418
  272.6 4.6 %copy.51 = f32[2,512,4,128]{3,0,2,1:T(2,128)} copy(f32[2,512,4,128]{3,2,1,0:T(4,128)} %mul.92) | data formatting | bytes 4194304 | tf_op jit(solution)/shard_map/mul | solution.py:418
  277.2 2.0 copy.48
  279.2 2.7 add_convert_fusion
  (123 shorter events, 10.0 us)
Async XLA Ops:
  0.6 8.7 %copy-start = (bf16[512,4,2,128]{3,2,1,0:T(2,128)(2,1)S(1)}, bf16[512,4,2,128]{3,2,1,0:T(2,128)(2,1)}, u32[]{:S(2)}) copy-start(bf16[512,4,2,128]{3,2,1,0:T(2,128)(2,1)} %param.7) | copy-start | bytes 3145732
  0.6 16.6 %copy-start.2 = (bf16[1024,256]{1,0:T(8,128)(2,1)S(1)}, bf16[1024,256]{1,0:T(8,128)(2,1)}, u32[]{:S(2)}) copy-start(bf16[1024,256]{1,0:T(8,128)(2,1)} %refs_1_.1) | copy-start | bytes 1572868
  0.7 16.6 %collective-permute-start.3 = (bf16[1024,256]{1,0:T(8,128)(2,1)}, bf16[1024,256]{1,0:T(8,128)(2,1)}, u32[]{:S(2)}, u32[]{:S(2)}) collective-permute-start(bf16[1024,256]{1,0:T(8,128)(2,1)} %refs_1_.1), channel_id=1, source_target_pairs={{0,8},{2,10},{4,12},{6,14},{8,16},{10,18},{12,20},{14,22},{16,24},... | collective-permute-start | bytes 1572872 | tf_op jit(solution)/shard_map/ppermute | solution.py:25
  6.6 17.8 %collective-permute-start = (bf16[1024,256]{1,0:T(8,128)(2,1)}, bf16[1024,256]{1,0:T(8,128)(2,1)S(1)}, u32[]{:S(2)}, u32[]{:S(2)}) collective-permute-start(bf16[1024,256]{1,0:T(8,128)(2,1)} %refs_1_.1), channel_id=1, source_target_pairs={{0,1},{1,0},{2,3},{3,2},{4,5},{5,4},{6,7},{7,6},{8,9},{9,8},{10,11... | collective-permute-start | bytes 1572872 | tf_op jit(solution)/shard_map/ppermute | solution.py:20
  8.1 16.4 %collective-permute-start.1 = (bf16[1024,256]{1,0:T(8,128)(2,1)}, bf16[1024,256]{1,0:T(8,128)(2,1)}, u32[]{:S(2)}, u32[]{:S(2)}) collective-permute-start(bf16[1024,256]{1,0:T(8,128)(2,1)} %refs_1_.1), channel_id=1, source_target_pairs={{0,2},{2,0},{4,6},{6,4},{8,10},{10,8},{12,14},{14,12},{16,18},{18,... | collective-permute-start | bytes 1572872 | tf_op jit(solution)/shard_map/ppermute | solution.py:20
  8.1 27.6 %collective-permute-start.11 = (bf16[1024,256]{1,0:T(8,128)(2,1)}, bf16[1024,256]{1,0:T(8,128)(2,1)}, u32[]{:S(2)}, u32[]{:S(2)}) collective-permute-start(bf16[1024,256]{1,0:T(8,128)(2,1)} %refs_4_.3), channel_id=1, source_target_pairs={{0,1},{1,0},{2,3},{3,2},{4,5},{5,4},{6,7},{7,6},{8,9},{9,8},{10,11... | collective-permute-start | bytes 1572872 | tf_op jit(solution)/shard_map/ppermute | solution.py:20
  10.4 12.4 %copy-start.16 = (bf16[2,128,512]{2,1,0:T(8,128)(2,1)S(1)}, bf16[2,128,512]{2,1,0:T(8,128)(2,1)}, u32[]{:S(2)}) copy-start(bf16[2,128,512]{2,1,0:T(8,128)(2,1)} %param.8) | copy-start | bytes 786436
  18.1 13.9 %collective-permute-start.4 = (bf16[1024,256]{1,0:T(8,128)(2,1)}, bf16[1024,256]{1,0:T(8,128)(2,1)}, u32[]{:S(2)}, u32[]{:S(2)}) collective-permute-start(bf16[1024,256]{1,0:T(8,128)(2,1)} %broadcast_select_fusion), channel_id=1, source_target_pairs={{0,4},{2,6},{4,0},{6,2},{8,12},{10,14},{12,8},{14,10},{16,20},{18,... | collective-permute-start | bytes 1572872 | tf_op jit(solution)/shard_map/ppermute | solution.py:20
  22.8 12.8 %copy-start.21 = (s32[12]{0:T(128)}, s32[12]{0:T(128)S(1)}, u32[]{:S(2)}) copy-start(s32[12]{0:T(128)S(1)} %get-tuple-element.85.refs_2_) | copy-start | bytes 148
  22.8 12.8 %copy-start.7 = (bf16[1024,256]{1,0:T(8,128)(2,1)S(1)}, bf16[1024,256]{1,0:T(8,128)(2,1)}, u32[]{:S(2)}) copy-start(bf16[1024,256]{1,0:T(8,128)(2,1)} %refs_4_.3) | copy-start | bytes 1572868
  22.9 21.2 %collective-permute-start.8 = (bf16[1024,256]{1,0:T(8,128)(2,1)}, bf16[1024,256]{1,0:T(8,128)(2,1)S(1)}, u32[]{:S(2)}, u32[]{:S(2)}) collective-permute-start(bf16[1024,256]{1,0:T(8,128)(2,1)} %collective-permute-done.3.refs_1_), channel_id=1, source_target_pairs={{0,1},{1,0},{2,3},{3,2},{4,5},{5,4},{6,7},{7,6},{8,9},{9,8},{10,11... | collective-permute-start | bytes 1572872 | tf_op jit(solution)/shard_map/ppermute | solution.py:20
  24.4 31.7 %copy-start.5 = (bf16[1024,256]{1,0:T(8,128)(2,1)}, bf16[1024,256]{1,0:T(8,128)(2,1)S(1)}, u32[]{:S(2)}) copy-start(bf16[1024,256]{1,0:T(8,128)(2,1)S(1)} %collective-permute-done.refs_2_) | copy-start | bytes 1572868
  24.4 19.6 %collective-permute-start.9 = (bf16[1024,256]{1,0:T(8,128)(2,1)}, bf16[1024,256]{1,0:T(8,128)(2,1)}, u32[]{:S(2)}, u32[]{:S(2)}) collective-permute-start(bf16[1024,256]{1,0:T(8,128)(2,1)} %collective-permute-done.3.refs_1_), channel_id=1, source_target_pairs={{0,2},{2,0},{4,6},{6,4},{8,10},{10,8},{12,14},{14,12},{16,18},{18,... | collective-permute-start | bytes 1572872 | tf_op jit(solution)/shard_map/ppermute | solution.py:20
  24.4 11.3 %collective-permute-start.2 = (bf16[1024,256]{1,0:T(8,128)(2,1)S(1)}, bf16[1024,256]{1,0:T(8,128)(2,1)}, u32[]{:S(2)}, u32[]{:S(2)}) collective-permute-start(bf16[1024,256]{1,0:T(8,128)(2,1)S(1)} %collective-permute-done.refs_2_), channel_id=1, source_target_pairs={{0,2},{2,0},{4,6},{6,4},{8,10},{10,8},{12,14},{14,12},{16,18},{18,... | collective-permute-start | bytes 1572872 | tf_op jit(solution)/shard_map/ppermute | solution.py:20
  32.0 21.9 %collective-permute-start.5 = (bf16[1024,256]{1,0:T(8,128)(2,1)}, bf16[1024,256]{1,0:T(8,128)(2,1)}, u32[]{:S(2)}, u32[]{:S(2)}) collective-permute-start(bf16[1024,256]{1,0:T(8,128)(2,1)} %collective-permute-done.4.refs_1_), channel_id=1, source_target_pairs={{0,1},{1,0},{2,3},{3,2},{4,5},{5,4},{6,7},{7,6},{8,9},{9,8},{10,11... | collective-permute-start | bytes 1572872 | tf_op jit(solution)/shard_map/ppermute | solution.py:20
  35.5 23.4 %copy-start.17 = (bf16[128,256]{1,0:T(8,128)(2,1)S(1)}, bf16[128,256]{1,0:T(8,128)(2,1)}, u32[]{:S(2)}) copy-start(bf16[128,256]{1,0:T(8,128)(2,1)} %get-tuple-element.99) | copy-start | bytes 196612
  35.6 23.9 %copy-start.4 = (bf16[512,512]{1,0:T(8,128)(2,1)}, bf16[512,512]{1,0:T(8,128)(2,1)S(1)}, u32[]{:S(2)}) copy-start(bf16[512,512]{1,0:T(8,128)(2,1)S(1)} %maximum_select_fusion.4.refs_5_.refs_10_) | copy-start | bytes 1572868
  35.6 64.6 %collective-permute-start.12 = (bf16[1024,256]{1,0:T(8,128)(2,1)S(1)}, bf16[1024,256]{1,0:T(8,128)(2,1)S(1)}, u32[]{:S(2)}, u32[]{:S(2)}) collective-permute-start(bf16[1024,256]{1,0:T(8,128)(2,1)S(1)} %copy-done.7), channel_id=1, source_target_pairs={{0,2},{2,0},{4,6},{6,4},{8,10},{10,8},{12,14},{14,12},{16,18},{18,... | collective-permute-start | bytes 1572872 | tf_op jit(solution)/shard_map/ppermute | solution.py:20
  35.7 64.6 %collective-permute-start.13 = (bf16[1024,256]{1,0:T(8,128)(2,1)}, bf16[1024,256]{1,0:T(8,128)(2,1)S(1)}, u32[]{:S(2)}, u32[]{:S(2)}) collective-permute-start(bf16[1024,256]{1,0:T(8,128)(2,1)} %collective-permute-done.11.refs_5_), channel_id=1, source_target_pairs={{0,2},{2,0},{4,6},{6,4},{8,10},{10,8},{12,14},{14,12},{16,18},{18,... | collective-permute-start | bytes 1572872 | tf_op jit(solution)/shard_map/ppermute | solution.py:20
  44.0 15.5 %copy-start.14 = (bf16[1024,256]{1,0:T(8,128)(2,1)}, bf16[1024,256]{1,0:T(8,128)(2,1)S(1)}, u32[]{:S(2)}) copy-start(bf16[1024,256]{1,0:T(8,128)(2,1)S(1)} %collective-permute-done.8.refs_2_) | copy-start | bytes 1572868
  44.0 46.1 %collective-permute-start.6 = (bf16[1024,256]{1,0:T(8,128)(2,1)}, bf16[1024,256]{1,0:T(8,128)(2,1)}, u32[]{:S(2)}, u32[]{:S(2)}) collective-permute-start(bf16[1024,256]{1,0:T(8,128)(2,1)} %collective-permute-done.4.refs_1_), channel_id=1, source_target_pairs={{0,2},{2,0},{4,6},{6,4},{8,10},{10,8},{12,14},{14,12},{16,18},{18,... | collective-permute-start | bytes 1572872 | tf_op jit(solution)/shard_map/ppermute | solution.py:20
  44.1 36.0 %collective-permute-start.10 = (bf16[1024,256]{1,0:T(8,128)(2,1)S(1)}, bf16[1024,256]{1,0:T(8,128)(2,1)}, u32[]{:S(2)}, u32[]{:S(2)}) collective-permute-start(bf16[1024,256]{1,0:T(8,128)(2,1)S(1)} %collective-permute-done.8.refs_2_), channel_id=1, source_target_pairs={{0,2},{2,0},{4,6},{6,4},{8,10},{10,8},{12,14},{14,12},{16,18},{18,... | collective-permute-start | bytes 1572872 | tf_op jit(solution)/shard_map/ppermute | solution.py:20
  54.0 36.2 %collective-permute-start.7 = (bf16[1024,256]{1,0:T(8,128)(2,1)}, bf16[1024,256]{1,0:T(8,128)(2,1)}, u32[]{:S(2)}, u32[]{:S(2)}) collective-permute-start(bf16[1024,256]{1,0:T(8,128)(2,1)} %collective-permute-done.5.refs_2_), channel_id=1, source_target_pairs={{0,2},{2,0},{4,6},{6,4},{8,10},{10,8},{12,14},{14,12},{16,18},{18,... | collective-permute-start | bytes 1572872 | tf_op jit(solution)/shard_map/ppermute | solution.py:20
  54.7 5.7 %copy-start.15 = (s32[2048]{0:T(1024)}, s32[2048]{0:T(1024)S(1)}, u32[]{:S(2)}) copy-start(s32[2048]{0:T(1024)S(1)} %get-tuple-element.102) | copy-start | bytes 24580
  54.7 5.7 %copy-start.19 = (s32[2048]{0:T(1024)}, s32[2048]{0:T(1024)S(1)}, u32[]{:S(2)}) copy-start(s32[2048]{0:T(1024)S(1)} %get-tuple-element.103) | copy-start | bytes 24580
  54.7 5.7 %copy-start.20 = (s32[2048]{0:T(1024)}, s32[2048]{0:T(1024)S(1)}, u32[]{:S(2)}) copy-start(s32[2048]{0:T(1024)S(1)} %get-tuple-element.101) | copy-start | bytes 24580
  56.1 2.8 copy-start.18
  100.3 0.8 copy-start.8
  100.3 1.0 copy-start.9
  145.4 40.9 %copy-start.3 = (bf16[1024,256]{1,0:T(8,128)(2,1)S(1)}, bf16[1024,256]{1,0:T(8,128)(2,1)}, u32[]{:S(2)}) copy-start(bf16[1024,256]{1,0:T(8,128)(2,1)} %refs_1_.1) | copy-start | bytes 1572868
  145.4 40.9 %copy-start.6 = (bf16[1024,256]{1,0:T(8,128)(2,1)S(1)}, bf16[1024,256]{1,0:T(8,128)(2,1)}, u32[]{:S(2)}) copy-start(bf16[1024,256]{1,0:T(8,128)(2,1)} %copy-done.5) | copy-start | bytes 1572868
  146.8 14.5 %collective-permute-start.25 = (bf16[256,640]{1,0:T(8,128)(2,1)S(1)}, bf16[256,640]{1,0:T(8,128)(2,1)S(1)}, u32[]{:S(2)}, u32[]{:S(2)}) collective-permute-start(bf16[256,640]{1,0:T(8,128)(2,1)S(1)} %dynamic-slice_convert_fusion), channel_id=1, source_target_pairs={{0,4},{2,6},{4,0},{6,2},{8,12},{10,14},{12,8},{14,10},{16,20},{18,... | collective-permute-start | bytes 983048 | tf_op jit(solution)/shard_map/ppermute | solution.py:20
  161.4 28.9 %collective-permute-start.26 = (bf16[128,640]{1,0:T(8,128)(2,1)S(1)}, bf16[128,640]{1,0:T(8,128)(2,1)S(1)}, u32[]{:S(2)}, u32[]{:S(2)}) collective-permute-start(bf16[128,640]{1,0:T(8,128)(2,1)S(1)} %dynamic-slice_convert_fusion.1), channel_id=1, source_target_pairs={{0,8},{2,10},{4,12},{6,14},{8,0},{10,2},{12,4},{14,6},{16,24},{18,... | collective-permute-start | bytes 491528 | tf_op jit(solution)/shard_map/ppermute | solution.py:20
  186.5 12.6 %copy-start.23 = (bf16[1024,512]{1,0:T(8,128)(2,1)S(1)}, bf16[1024,512]{1,0:T(8,128)(2,1)}, u32[]{:S(2)}) copy-start(bf16[1024,512]{1,0:T(8,128)(2,1)} %get-tuple-element.61) | copy-start | bytes 3145732
  186.5 21.0 %collective-permute-start.16 = (bf16[1024,512]{1,0:T(8,128)(2,1)}, bf16[1024,512]{1,0:T(8,128)(2,1)S(1)}, u32[]{:S(2)}, u32[]{:S(2)}) collective-permute-start(bf16[1024,512]{1,0:T(8,128)(2,1)} %get-tuple-element.59), channel_id=1, source_target_pairs={{0,2},{2,0},{4,6},{6,4},{8,10},{10,8},{12,14},{14,12},{16,18},{18,... | collective-permute-start | bytes 3145736 | tf_op jit(solution)/shard_map/ppermute | solution.py:20
  190.3 12.7 %copy-start.22 = (bf16[1024,512]{1,0:T(8,128)(2,1)S(1)}, bf16[1024,512]{1,0:T(8,128)(2,1)}, u32[]{:S(2)}) copy-start(bf16[1024,512]{1,0:T(8,128)(2,1)} %get-tuple-element.48) | copy-start | bytes 3145732
  190.4 5.4 %collective-permute-start.27 = (bf16[64,640]{1,0:T(8,128)(2,1)S(1)}, bf16[64,640]{1,0:T(8,128)(2,1)S(1)}, u32[]{:S(2)}, u32[]{:S(2)}) collective-permute-start(bf16[64,640]{1,0:T(8,128)(2,1)S(1)} %dynamic-slice_convert_fusion.2), channel_id=1, source_target_pairs={{0,16},{2,18},{4,20},{6,22},{8,24},{10,26},{12,28},{14,30},{16,0},... | collective-permute-start | bytes 245768 | tf_op jit(solution)/shard_map/ppermute | solution.py:20
  193.2 16.2 %collective-permute-start.21 = (bf16[1024,512]{1,0:T(8,128)(2,1)}, bf16[1024,512]{1,0:T(8,128)(2,1)S(1)}, u32[]{:S(2)}, u32[]{:S(2)}) collective-permute-start(bf16[1024,512]{1,0:T(8,128)(2,1)} %get-tuple-element.63), channel_id=1, source_target_pairs={{0,2},{2,0},{4,6},{6,4},{8,10},{10,8},{12,14},{14,12},{16,18},{18,... | collective-permute-start | bytes 3145736 | tf_op jit(solution)/shard_map/ppermute | solution.py:20
  195.8 11.7 %copy-start.13 = (bf16[1024,512]{1,0:T(8,128)(2,1)S(1)}, bf16[1024,512]{1,0:T(8,128)(2,1)}, u32[]{:S(2)}) copy-start(bf16[1024,512]{1,0:T(8,128)(2,1)} %get-tuple-element.58) | copy-start | bytes 3145732
  195.8 5.4 %collective-permute-start.28 = (bf16[64,640]{1,0:T(8,128)(2,1)S(1)}, bf16[64,640]{1,0:T(8,128)(2,1)S(1)}, u32[]{:S(2)}, u32[]{:S(2)}) collective-permute-start(bf16[64,640]{1,0:T(8,128)(2,1)S(1)} %add_convert_fusion.1), channel_id=1, source_target_pairs={{0,16},{2,18},{4,20},{6,22},{8,24},{10,26},{12,28},{14,30},{16,0},... | collective-permute-start | bytes 245768 | tf_op jit(solution)/shard_map/ppermute | solution.py:20
  199.1 11.5 %collective-permute-start.18 = (bf16[1024,512]{1,0:T(8,128)(2,1)S(1)}, bf16[1024,512]{1,0:T(8,128)(2,1)S(1)}, u32[]{:S(2)}, u32[]{:S(2)}) collective-permute-start(bf16[1024,512]{1,0:T(8,128)(2,1)S(1)} %copy-done.23), channel_id=1, source_target_pairs={{0,2},{2,0},{4,6},{6,4},{8,10},{10,8},{12,14},{14,12},{16,18},{18,... | collective-permute-start | bytes 3145736 | tf_op jit(solution)/shard_map/ppermute | solution.py:20
  201.2 5.4 %collective-permute-start.29 = (bf16[128,640]{1,0:T(8,128)(2,1)S(1)}, bf16[128,640]{1,0:T(8,128)(2,1)S(1)}, u32[]{:S(2)}, u32[]{:S(2)}) collective-permute-start(bf16[128,640]{1,0:T(8,128)(2,1)S(1)} %maximum_select_fusion.6), channel_id=1, source_target_pairs={{0,8},{2,10},{4,12},{6,14},{8,0},{10,2},{12,4},{14,6},{16,24},{18,... | collective-permute-start | bytes 491528 | tf_op jit(solution)/shard_map/ppermute | solution.py:20
  203.1 9.3 %collective-permute-start.14 = (bf16[1024,512]{1,0:T(8,128)(2,1)S(1)}, bf16[1024,512]{1,0:T(8,128)(2,1)S(1)}, u32[]{:S(2)}, u32[]{:S(2)}) collective-permute-start(bf16[1024,512]{1,0:T(8,128)(2,1)S(1)} %copy-done.22), channel_id=1, source_target_pairs={{0,2},{2,0},{4,6},{6,4},{8,10},{10,8},{12,14},{14,12},{16,18},{18,... | collective-permute-start | bytes 3145736 | tf_op jit(solution)/shard_map/ppermute | solution.py:20
  206.7 7.1 %collective-permute-start.30 = (bf16[256,640]{1,0:T(8,128)(2,1)S(1)}, bf16[256,640]{1,0:T(8,128)(2,1)S(1)}, u32[]{:S(2)}, u32[]{:S(2)}) collective-permute-start(bf16[256,640]{1,0:T(8,128)(2,1)S(1)} %maximum_select_fusion.5), channel_id=1, source_target_pairs={{0,4},{2,6},{4,0},{6,2},{8,12},{10,14},{12,8},{14,10},{16,20},{18,... | collective-permute-start | bytes 983048 | tf_op jit(solution)/shard_map/ppermute | solution.py:20
  207.5 1.9 copy-start.12
  207.9 50.2 %collective-permute-start.17 = (bf16[1024,256]{1,0:T(8,128)(2,1)S(1)}, bf16[1024,256]{1,0:T(8,128)(2,1)S(1)}, u32[]{:S(2)}, u32[]{:S(2)}) collective-permute-start(bf16[1024,256]{1,0:T(8,128)(2,1)S(1)} %slice.200), channel_id=1, source_target_pairs={{0,1},{1,0},{2,3},{3,2},{4,5},{5,4},{6,7},{7,6},{8,9},{9,8},{10,11... | collective-permute-start | bytes 1572872 | tf_op jit(solution)/shard_map/ppermute | solution.py:20
  209.4 1.2 copy-start.11
  209.8 43.8 %collective-permute-start.22 = (bf16[1024,256]{1,0:T(8,128)(2,1)S(1)}, bf16[1024,256]{1,0:T(8,128)(2,1)S(1)}, u32[]{:S(2)}, u32[]{:S(2)}) collective-permute-start(bf16[1024,256]{1,0:T(8,128)(2,1)S(1)} %slice.198), channel_id=1, source_target_pairs={{0,1},{1,0},{2,3},{3,2},{4,5},{5,4},{6,7},{7,6},{8,9},{9,8},{10,11... | collective-permute-start | bytes 1572872 | tf_op jit(solution)/shard_map/ppermute | solution.py:20
  210.6 1.7 copy-start.10
  211.0 34.2 %collective-permute-start.19 = (bf16[1024,256]{1,0:T(8,128)(2,1)S(1)}, bf16[1024,256]{1,0:T(8,128)(2,1)S(1)}, u32[]{:S(2)}, u32[]{:S(2)}) collective-permute-start(bf16[1024,256]{1,0:T(8,128)(2,1)S(1)} %slice.199), channel_id=1, source_target_pairs={{0,1},{1,0},{2,3},{3,2},{4,5},{5,4},{6,7},{7,6},{8,9},{9,8},{10,11... | collective-permute-start | bytes 1572872 | tf_op jit(solution)/shard_map/ppermute | solution.py:20
  212.8 39.7 %collective-permute-start.15 = (bf16[1024,256]{1,0:T(8,128)(2,1)S(1)}, bf16[1024,256]{1,0:T(8,128)(2,1)S(1)}, u32[]{:S(2)}, u32[]{:S(2)}) collective-permute-start(bf16[1024,256]{1,0:T(8,128)(2,1)S(1)} %slice.201), channel_id=1, source_target_pairs={{0,1},{1,0},{2,3},{3,2},{4,5},{5,4},{6,7},{7,6},{8,9},{9,8},{10,11... | collective-permute-start | bytes 1572872 | tf_op jit(solution)/shard_map/ppermute | solution.py:20
  214.4 39.1 %collective-permute-start.31 = (bf16[512,640]{1,0:T(8,128)(2,1)S(1)}, bf16[512,640]{1,0:T(8,128)(2,1)S(1)}, u32[]{:S(2)}, u32[]{:S(2)}) collective-permute-start(bf16[512,640]{1,0:T(8,128)(2,1)S(1)} %maximum_select_fusion.3), channel_id=1, source_target_pairs={{0,2},{2,0},{4,6},{6,4},{8,10},{10,8},{12,14},{14,12},{16,18},{18,... | collective-permute-start | bytes 1966088 | tf_op jit(solution)/shard_map/ppermute | solution.py:20
  245.4 9.2 %collective-permute-start.20 = (bf16[1024,256]{1,0:T(8,128)(2,1)S(1)}, bf16[1024,256]{1,0:T(8,128)(2,1)S(1)}, u32[]{:S(2)}, u32[]{:S(2)}) collective-permute-start(bf16[1024,256]{1,0:T(8,128)(2,1)S(1)} %fusion.4), channel_id=1, source_target_pairs={{0,4},{2,6},{4,0},{6,2},{8,12},{10,14},{12,8},{14,10},{16,20},{18,... | collective-permute-start | bytes 1572872 | tf_op jit(solution)/shard_map/ppermute | solution.py:20
  254.9 11.1 %collective-permute-start.23 = (bf16[1024,256]{1,0:T(8,128)(2,1)S(1)}, bf16[1024,256]{1,0:T(8,128)(2,1)S(1)}, u32[]{:S(2)}, u32[]{:S(2)}) collective-permute-start(bf16[1024,256]{1,0:T(8,128)(2,1)S(1)} %fusion.3), channel_id=1, source_target_pairs={{8,0},{10,2},{12,4},{14,6},{16,8},{18,10},{20,12},{22,14},{24,16},... | collective-permute-start | bytes 1572872 | tf_op jit(solution)/shard_map/ppermute | solution.py:25
  267.3 11.9 %collective-permute-start.24 = (f32[2,1024]{1,0:T(2,128)S(1)}, f32[2,1024]{1,0:T(2,128)S(1)}, u32[]{:S(2)}, u32[]{:S(2)}) collective-permute-start(f32[2,1024]{1,0:T(2,128)S(1)} %pad_maximum_fusion.4), channel_id=1, source_target_pairs={{0,1},{1,0},{2,3},{3,2},{4,5},{5,4},{6,7},{7,6},{8,9},{9,8},{10,11... | collective-permute-start | bytes 24584 | tf_op jit(solution)/shard_map/ppermute | solution.py:20
  272.6 9.4 %copy-start.1 = (bf16[512,4,2,128]{3,2,1,0:T(2,128)(2,1)S(1)}, bf16[512,4,2,128]{3,2,1,0:T(2,128)(2,1)}, u32[]{:S(2)}) copy-start(bf16[512,4,2,128]{3,2,1,0:T(2,128)(2,1)} %param.7) | copy-start | bytes 3145732
where the time goes:
time: 283 us; the launch traced here: 282 us
  waiting for transfers between devices  96.7 us (34%)
  Pallas kernels  81 us (29%)
  starting transfers between devices  63.2 us (22%)
  local copies, waits for them, and re-layouts  24 us (8%)
  other arithmetic  15.7 us (6%)
    ppermute x30, waiting for transfers between devices, swap(): lax.ppermute(block, axis, [(i, i ^ bit) for i in range(lax.axis_size(axis...  82 us
    pallas_call x11, Pallas kernels, vmem_call(): pl.pallas_call(lambda *refs: kernel(*refs, **static), out_shape=outs, in_...  81 us
    ppermute x30, starting transfers between devices, swap(): lax.ppermute(block, axis, [(i, i ^ bit) for i in range(lax.axis_size(axis...  56 us
    ppermute x2, waiting for transfers between devices, shift(): lax.ppermute(block, axis, [(i, i + distance) for i in devices if i + dist...  14.7 us
    mul x2, local copies, waits for them, and re-layouts, layer(): grad_weight_in = grad_weight_in.astype(f32) * inv_root  7.53 us
    ppermute x2, starting transfers between devices, shift(): lax.ppermute(block, axis, [(i, i + distance) for i in devices if i + dist...  7.2 us
  transfers between devices with their start and end apart: 32, of which 14 were waited for; matrix products, arithmetic and copies ran while one was open for 11% of the time, Pallas kernels for 13%

commit v1 on v0

--- a/solution.py
+++ b/solution.py
@@ -93,7 +93,7 @@
             up = up_ref[into, :].astype(f32)
             gated_ref[into, :] = (head_normed * up).astype(bf16)
             grad = dot(first[rows, :], w_ref[:, :half], NT) + dot(second[rows, :], w_ref[:, half:], NT)
-            pre_up_ref[into, :] = (grad * head_normed * slope_ref[into, :].astype(f32)).astype(bf16)
+            pre_up_ref[into, :] = (grad * head_normed * slope_ref[into, : up.shape[1]].astype(f32)).astype(bf16)
             narrow_ref[into, :] = norm_back(grad * up, head_normed, head_scale).astype(bf16)
             return carry
 
@@ -117,20 +117,18 @@
     def query_tile(i, carry):
         start = jnp.maximum(low_ref[i] - block_off, 0)
         stop = jnp.minimum(query_off + i + 1 - block_off, k_tiles)
-        rows = aligned(i * TILE, TILE)
 
         def key_tile(j, inner):
-            cols = aligned(j * TILE, TILE)
             near = query_off + i - block_off - j
             whole = (near > 0) & (first_ref[block_off + j] == last_ref[query_off + i])
 
             @pl.when(whole)
             def _():
-                step(rows, cols, None)
+                step(i, j, None)
 
             @pl.when(jnp.logical_not(whole))
             def _():
-                step(rows, cols, near * TILE)
+                step(i, j, near * TILE)
 
             return inner
 
@@ -140,20 +138,22 @@
     lax.fori_loop(0, q_tiles, query_tile, 0)
 
 
-def forward_kernel(low_ref, first_ref, last_ref, q_ref, k_ref, v_ref, idq_ref, idk_ref, *rest, block_off, query_off, scale):
+def forward_kernel(low_ref, first_ref, last_ref, q_ref, k_ref, v_ref, col_ref, row_ref, *rest, block_off, query_off, scale):
     out_ref = rest[-1]
     if len(rest) == 2:
         out_ref[...] = rest[0][...]
     else:
         out_ref[...] = jnp.zeros(out_ref.shape, f32)
 
-    def step(rows, cols, reach):
+    def step(i, j, reach):
+        rows, cols = aligned(i * TILE, TILE), aligned(j * TILE, TILE)
         half = dot(q_ref[rows, :], k_ref[cols, :], NT) * (0.5 * scale)
         if reach is not None:
             pos_q = lax.broadcasted_iota(jnp.int32, (TILE, TILE), 0)
             pos_k = lax.broadcasted_iota(jnp.int32, (TILE, TILE), 1)
-            ok = (idq_ref[rows, :] == idk_ref[:, cols]) & (pos_k - pos_q <= reach)
-            half = jnp.where(ok, half, 0.0)
+            id_q = col_ref[aligned((query_off + i) * TILE, TILE), :]
+            id_k = row_ref[:, aligned((block_off + j) * TILE, TILE)]
+            half = jnp.where((id_q == id_k) & (pos_k - pos_q <= reach), half, 0.0)
         weights = half + half * jnp.tanh(half)
         out_ref[rows, :] += dot(weights.astype(bf16), v_ref[cols, :])
 
@@ -162,30 +162,19 @@
     )
 
 
-def backward_kernel(low_ref, first_ref, last_ref, core_ref, q_ref, g_ref, k_ref, v_ref, idq_ref, idk_ref, w_ref, slope_hbm, normed_hbm, *rest, block_off, query_off, scale, count_in):
-    before = rest[:count_in]
-    send_ref, keep_ref, grad_ref = rest[count_in : count_in + 3]
-    if block_off != query_off:
-        dq_ref = rest[count_in + 3]
-    else:
-        dq_ref = rest[-6]
-    dk_ref, dv_ref, slope_ref, normed_ref, sems = rest[-5:]
-    q_tiles = q_ref.shape[0] // TILE
-    k_tiles = k_ref.shape[0] // TILE
+def backward_kernel(low_ref, first_ref, last_ref, core_ref, q_ref, g_ref, k_ref, v_ref, col_ref, row_ref, w_ref, slope_ref, *rest, block_off, query_off, scale):
     own = block_off == query_off
-    slope_copy = pltpu.make_async_copy(slope_hbm, slope_ref, sems.at[0])
-    normed_copy = pltpu.make_async_copy(normed_hbm, normed_ref, sems.at[1])
-    slope_copy.start()
-    normed_copy.start()
+    *before, send_ref, keep_ref, grads_ref, dq_ref, dk_ref, dv_ref = rest
     width = k_ref.shape[1]
-    if len(before) > 0:
+    if before:
         dq_ref[...] = before[0][...]
     else:
         dq_ref[...] = jnp.zeros(dq_ref.shape, f32)
     dk_ref[...] = jnp.zeros(dk_ref.shape, f32)
     dv_ref[...] = jnp.zeros(dv_ref.shape, f32)
 
-    def step(rows, cols, reach):
+    def step(i, j, reach):
+        rows, cols = aligned(i * TILE, TILE), aligned(j * TILE, TILE)
         q = q_ref[rows, :]
         g = g_ref[rows, :]
         k = k_ref[cols, :]
@@ -194,7 +183,9 @@
         if reach is not None:
             pos_k = lax.broadcasted_iota(jnp.int32, (TILE, TILE), 0)
             pos_q = lax.broadcasted_iota(jnp.int32, (TILE, TILE), 1)
-            ok = (idk_ref[cols, :] == idq_ref[:, rows]) & (pos_k - pos_q <= reach)
+            id_k = col_ref[aligned((block_off + j) * TILE, TILE), :]
+            id_q = row_ref[:, aligned((query_off + i) * TILE, TILE)]
+            ok = (id_k == id_q) & (pos_k - pos_q <= reach)
             half = jnp.where(ok, half, 0.0)
             grad = jnp.where(ok, grad, 0.0)
         twice = (1.0 + jnp.tanh(half)).astype(bf16)
@@ -205,50 +196,73 @@
         dk_ref[cols, :] += dot(grad, q)
         dq_ref[rows, :] += dot(grad, k, TN)
 
+    q_tiles = q_ref.shape[0] // TILE
+    k_tiles = k_ref.shape[0] // TILE
     for_tiles(low_ref, first_ref, last_ref, q_tiles, k_tiles, block_off, query_off, step)
-    slope_copy.wait()
-    normed_copy.wait()
-    core = core_ref[0]
-    count = send_ref.shape[0]
-    base = width if own else 0
 
     def narrow(grads, part):
-        into = slope_ref.at[:, part * width : (part + 1) * width]
-        into[...] = (grads * into[...].astype(f32)).astype(bf16)
+        into = slice(part * width, (part + 1) * width)
+        grads_ref[:, into] = (grads * slope_ref[:, into].astype(f32)).astype(bf16)
 
     if own:
-        slope_ref[:, :width] = before[-1][...]
+        grads_ref[:, :width] = before[1][...]
         narrow(dv_ref[...], 1)
         narrow(dq_ref[...] * scale, 2)
         narrow(dk_ref[...] * scale, 3)
     else:
         narrow(dv_ref[...], 0)
         narrow(dk_ref[...] * scale, 1)
-    send_ref[...] = dot(slope_ref[aligned((1 - core) * count, count), :], w_ref[...], NT).astype(bf16)
-    keep_ref[...] = dot(slope_ref[aligned(core * count, count), :], w_ref[...], NT).astype(bf16)
-    grads = dot(normed_ref[...], slope_ref[:, base:], TN)
-    if own:
-        grad_ref[:, :width] = grads[:, :width] + before[1][:, :width]
-        grad_ref[:, width : 2 * width] = grads[:, width : 2 * width]
-        grad_ref[:, 2 * width :] = grads[:, 2 * width :] + before[1][:, width:]
-    elif len(before) > 1:
-        grad_ref[...] = grads + before[1][...]
-    else:
-        grad_ref[...] = grads
-
-
-def vmem_call(kernel, tables, arrays, outs, aliases=None, hbm=(), scratch=(), **static):
+    core = core_ref[0]
+    count = send_ref.shape[0]
+    send_ref[...] = dot(grads_ref[aligned((1 - core) * count, count), :], w_ref[...], NT).astype(bf16)
+    keep_ref[...] = dot(grads_ref[aligned(core * count, count), :], w_ref[...], NT).astype(bf16)
+
+
+def weight_kernel(normed_ref, grads_ref, *rest):
+    *before, out_ref = rest
+    grads = dot(normed_ref[...], grads_ref[...], TN)
+    out_ref[...] = grads + before[0][...] if before else grads
+
+
+def weight_own_kernel(high_ref, normed_ref, grads_ref, early_ref, kv_ref, send_ref, keep_ref, sum_ref):
+    width = kv_ref.shape[1] // 2
+    size = send_ref.shape[0]
+    sum_ref[:, width : 4 * width] = dot(normed_ref[...], grads_ref[:, width:], TN)
+    sum_ref[:, width : 2 * width] += kv_ref[:, :width]
+    sum_ref[:, 3 * width : 4 * width] += kv_ref[:, width:]
+    sum_ref[:, :width] = early_ref[:, :width]
+    sum_ref[:, 4 * width :] = early_ref[:, width:]
+    high = high_ref[0]
+    send_ref[...] = sum_ref[aligned((1 - high) * size, size), :].astype(bf16)
+    keep_ref[...] = sum_ref[aligned(high * size, size), :]
+
+
+def assemble_kernel(place_ref, mine_ref, other_ref, in_ref, out_ref, *, scale):
+    core, flip = place_ref[0], place_ref[1]
+    width = out_ref.shape[1]
+    half = mine_ref.shape[0] // 2
+    for ref, head in ((mine_ref, core), (other_ref, 1 - core)):
+        for part in range(2):
+            where = (part + flip) % 2
+            rows = slice(part * half, (part + 1) * half)
+            for p in range(4):
+                piece = ref[rows, p * width : (p + 1) * width].astype(f32) * scale
+                in_ref[pl.ds(where * (half * 8) + 2 * p + head, half, stride=8), :] = piece
+            piece = ref[rows, 4 * width :].astype(f32) * scale
+            out_ref[head, :, aligned(where * half, half)] = piece.T
+
+
+def vmem_call(kernel, tables, arrays, outs, aliases=None, scratch=(), **static):
     whole = pl.BlockSpec(memory_space=pltpu.VMEM)
     table = pl.BlockSpec(memory_space=pltpu.SMEM)
-    place = [pl.BlockSpec(memory_space=pl.ANY) if i in hbm else whole for i in range(len(arrays))]
     return pl.pallas_call(
         lambda *refs: kernel(*refs, **static),
         out_shape=outs,
-        in_specs=[table] * len(tables) + place,
+        in_specs=[table] * len(tables) + [whole] * len(arrays),
         out_specs=jax.tree.map(lambda _: whole, outs),
         input_output_aliases=aliases or {},
         scratch_shapes=list(scratch),
-        compiler_params=pltpu.CompilerParams(vmem_limit_bytes=60 << 20),
+        compiler_params=pltpu.CompilerParams(vmem_limit_bytes=16 << 20),
     )(*tables, *arrays)
 
 
@@ -295,7 +309,7 @@
     first, last = by_tile[:, 0], by_tile[:, -1]
     low = jnp.sum((last[None, :] < first[2 * tiles :, None]).astype(jnp.int32), axis=1)
     tables = (low, first, last)
-    own_ids = ids[2 * block :]
+    id_col, id_row = ids[:, None], ids[None, :]
 
     def shape(rows, cols, dtype=bf16):
         return jax.ShapeDtypeStruct((rows, cols), dtype)
@@ -312,8 +326,7 @@
     values = [value_far, value_near, value_own]
 
     def forward(which, before):
-        span = slice(which * block, (which + 1) * block)
-        arrays = [query, keys[which], values[which], own_ids[:, None], ids[None, span]]
+        arrays = [query, keys[which], values[which], id_col, id_row]
         aliases = {}
         if before is not None:
             aliases = {3 + len(arrays): 0}
@@ -336,7 +349,7 @@
     grad_narrow, gated, pre_up = vmem_call(
         middle_kernel,
         (core_table,),
-        (attended, up_part, slope_own[:, :head_size], *cot_set, w_out),
+        (attended, up_part, slope_own, *cot_set, w_out),
         (shape(block, head_size),) * 3,
     )
     out_send, out_keep, grad_early = vmem_call(
@@ -350,57 +363,59 @@
         keep = keep.astype(f32) + over(send, "seq", 1).astype(f32)
         return keep[:, :half_width] + over(keep[:, half_width:].astype(bf16), "col", 1).astype(f32)
 
-    def backward(which, weights, slope, normed, before):
-        span = slice(which * block, (which + 1) * block)
-        arrays = [query, grad_narrow, keys[which], values[which], own_ids[None, :], ids[span, None], weights, slope, normed]
-        count = weights.shape[1]
-        own = which == 2
-        grads = count - head_size if own else count
-        outs = [shape(row_count, width), shape(row_count, width), shape(width, grads, f32)]
-        scratch = [
-            pltpu.VMEM((block, head_size), f32),
-            pltpu.VMEM((block, head_size), f32),
-            pltpu.VMEM((block, count), bf16),
-            pltpu.VMEM((block, width), bf16),
-            pltpu.SemaphoreType.DMA((2,)),
-        ]
-        if own:
-            scratch = [pltpu.VMEM((block, head_size), f32)] + scratch
-        else:
-            outs.append(shape(block, head_size, f32))
+    def backward(which, weights, slope, before):
+        arrays = [query, grad_narrow, keys[which], values[which], id_col, id_row, weights, slope, *before]
+        outs = (
+            shape(row_count, width),
+            shape(row_count, width),
+            shape(block, weights.shape[1]),
+            shape(block, head_size, f32),
+        )
         return vmem_call(
             backward_kernel,
             (*tables, core_table),
-            arrays + list(before),
-            tuple(outs),
-            hbm=(len(arrays) - 2, len(arrays) - 1),
-            scratch=scratch,
+            arrays,
+            outs,
+            {4 + 8: 3} if before else None,
+            scratch=[pltpu.VMEM((block, head_size), f32)] * 2,
             block_off=which * tiles,
             query_off=2 * tiles,
             scale=scale,
-            count_in=len(before),
         )
 
-    near_send, near_keep, grad_kv, grad_query = backward(1, w_kv, slope_near, normed_near, ())
+    kv_shape = shape(width, 2 * head_size, f32)
+    near_send, near_keep, near_grads, grad_query = backward(1, w_kv, slope_near, ())
+    grad_kv = vmem_call(weight_kernel, (), (normed_near, near_grads), kv_shape)
     near_part = over_heads(near_send, near_keep)
     near_back = over(near_part.astype(bf16), "seq", 2).astype(f32)
-    far_send, far_keep, grad_kv, grad_query = backward(0, w_kv, slope_far, normed_far, (grad_query, grad_kv))
+    far_send, far_keep, far_grads, grad_query = backward(0, w_kv, slope_far, (grad_query,))
+    grad_kv = vmem_call(weight_kernel, (), (normed_far, far_grads, grad_kv), kv_shape)
     far_part = over_heads(far_send, far_keep) + jnp.where(odd, near_back, 0.0)
     far_back = shift(far_part.astype(bf16), "seq", -4).astype(f32)
-    own_send, own_keep, grad_own = backward(2, w_in, slope_own, normed_own, (grad_query, grad_kv, pre_up))
+    own_send, own_keep, own_grads, _ = backward(2, w_in, slope_own, (grad_query, pre_up))
     own_part = over_heads(own_send, own_keep)
     grad_normed = own_part + jnp.where(odd, 0.0, near_back) + far_back
     out = (tokens.astype(f32) + over_heads(out_send, out_keep)).astype(bf16)
 
-    total = jnp.concatenate([grad_early[:, :head_size], grad_own, grad_early[:, head_size:]], axis=1)
     bits = []
     while 2 << len(bits) < seq_count:
         bits.append(2 << len(bits))
+    high = ((device_pos // bits[0]) % 2).astype(jnp.int32).reshape(1)
+    half_shape = (half_width, 5 * head_size)
+    sent, total = vmem_call(
+        weight_own_kernel,
+        (high,),
+        (normed_own, own_grads, grad_early, grad_kv),
+        (shape(*half_shape), shape(*half_shape, f32)),
+        scratch=[pltpu.VMEM((width, 5 * head_size), f32)],
+    )
     for bit in bits:
-        size = total.shape[0] // 2
-        high = (device_pos & bit) // bit
-        sent = lax.dynamic_slice_in_dim(total, (1 - high) * size, size).astype(bf16)
-        total = lax.dynamic_slice_in_dim(total, high * size, size) + over(sent, "seq", bit).astype(f32)
+        if bit != bits[0]:
+            size = total.shape[0] // 2
+            side = (device_pos & bit) // bit
+            sent = lax.dynamic_slice_in_dim(total, (1 - side) * size, size).astype(bf16)
+            total = lax.dynamic_slice_in_dim(total, side * size, size)
+        total = total + over(sent, "seq", bit).astype(f32)
     total = total.astype(bf16)
     for bit in reversed(bits):
         other = over(total, "seq", bit)
@@ -410,13 +425,15 @@
             jnp.concatenate([total, other], axis=0),
         )
 
-    inv_root = 1.0 / math.sqrt(row_count * seq_count)
-    total = jnp.where(flip, jnp.roll(total, half_width, axis=0), total)
-    both = jnp.stack([total, over(total, "seq", 1)])
-    both = jnp.where(core == 0, both, both[::-1])
-    grad_weight_in = both[:, :, : 4 * head_size].reshape(2, width, 4, head_size).transpose(1, 2, 0, 3)
-    grad_weight_in = grad_weight_in.astype(f32) * inv_root
-    grad_weight_out = both[:, :, 4 * head_size :].transpose(0, 2, 1).astype(f32) * inv_root
+    place = jnp.stack([core, lax.axis_index("col")]).astype(jnp.int32)
+    grad_weight_in, grad_weight_out = vmem_call(
+        assemble_kernel,
+        (place,),
+        (total, over(total, "seq", 1)),
+        (shape(8 * width, head_size, f32), jax.ShapeDtypeStruct((2, head_size, width), f32)),
+        scale=1.0 / math.sqrt(row_count * seq_count),
+    )
+    grad_weight_in = grad_weight_in.reshape(width, 4, 2, head_size)
 
     own_wide = jnp.concatenate([tokens, own_other], axis=1).astype(f32)
     normed, inv_std = layer_norm(own_wide, epsilon)

time: 283 us -> 222 us (0.78)
  waiting for transfers between devices: 96.7 us -> 67 us
  Pallas kernels: 81 us -> 55.8 us
  other arithmetic: 15.7 us -> 11 us
  local copies, waits for them, and re-layouts: 24 us -> 19.9 us
    pallas_call x11 -> x15, Pallas kernels: 81 us -> 55.8 us  [vmem_call(): pl.pallas_call(lambda *refs: kernel(*refs, **static), out_shape=outs, in_...]
    ppermute x30, waiting for transfers between devices: 82 us -> 59.6 us  [swap(): lax.ppermute(block, axis, [(i, i ^ bit) for i in range(lax.axis_size(axis...]
    mul x2 -> x0, local copies, waits for them, and re-layouts: 7.53 us -> none  [layer(): grad_weight_in = grad_weight_in.astype(f32) * inv_root]
    ppermute x2, waiting for transfers between devices: 14.7 us -> 7.38 us  [shift(): lax.ppermute(block, axis, [(i, i + distance) for i in devices if i + dist...]
    unnamed x50 -> x63, local copies, waits for them, and re-layouts: 4.44 us -> 11.7 us
    slice x3 -> x0, local copies, waits for them, and re-layouts: 3.66 us -> none  [the longest x1 1.89 us: layer(): slope_own[:, :head_size]]
    ppermute x30, starting transfers between devices: 56 us -> 59.5 us  [swap(): lax.ppermute(block, axis, [(i, i ^ bit) for i in range(lax.axis_size(axis...]
    broadcast_in_dim x3 -> x1, local copies, waits for them, and re-layouts: 4.11 us -> 1.06 us  [layer(): id_col, id_row = (ids[:, None], ids[None, :])]
  transfers between devices with their start and end apart: 32 -> 32, of which waited for: 14 -> 13; matrix products, arithmetic and copies ran while one was open for 11% -> 9% of each run, Pallas kernels for 13% -> 12%
where the time goes in v1:
time: 222 us; the launch traced here: 221 us
  waiting for transfers between devices  67 us (30%)
  starting transfers between devices  65.9 us (30%)
  Pallas kernels  55.8 us (25%)
  local copies, waits for them, and re-layouts  19.9 us (9%)
  other arithmetic  11 us (5%)
    ppermute x30, waiting for transfers between devices, swap(): lax.ppermute(block, axis, [(i, i ^ bit) for i in range(lax.axis_size(axis...  59.6 us
    ppermute x30, starting transfers between devices, swap(): lax.ppermute(block, axis, [(i, i ^ bit) for i in range(lax.axis_size(axis...  59.5 us
    pallas_call x15, Pallas kernels, vmem_call(): pl.pallas_call(lambda *refs: kernel(*refs, **static), out_shape=outs, in_...  55.8 us
    unnamed x63, local copies, waits for them, and re-layouts  11.7 us
    ppermute x2, waiting for transfers between devices, shift(): lax.ppermute(block, axis, [(i, i + distance) for i in devices if i + dist...  7.38 us
    ppermute x2, starting transfers between devices, shift(): lax.ppermute(block, axis, [(i, i + distance) for i in devices if i + dist...  6.41 us
  transfers between devices with their start and end apart: 32, of which 13 were waited for; matrix products, arithmetic and copies ran while one was open for 9% of the time, Pallas kernels for 12%

profile of v1, /device:TPU:0, one launch (start us, length us, event | category | flops | bytes accessed | tf_op | source)
XLA Modules:
  0.0 220.9 jit_solution(2704206162087190529)
XLA Ops:
  0.7 5.1 %collective-permute-start.3 = (bf16[1024,256]{1,0:T(8,128)(2,1)}, bf16[1024,256]{1,0:T(8,128)(2,1)S(1)}, u32[]{:S(2)}, u32[]{:S(2)}) collective-permute-start(bf16[1024,256]{1,0:T(8,128)(2,1)} %refs_1_.1), channel_id=1, source_target_pairs={{0,8},{2,10},{4,12},{6,14},{8,16},{10,18},{12,20},{14,22},{16,24},... | collective-permute-start | bytes 1572872 | tf_op jit(solution)/shard_map/ppermute | solution.py:25
  5.8 1.6 collective-permute-start
  7.9 2.1 constant_dynamic-slice_fusion
  10.0 7.3 %collective-permute-done.3.refs_1_ = bf16[1024,256]{1,0:T(8,128)(2,1)S(1)} collective-permute-done((bf16[1024,256]{1,0:T(8,128)(2,1)}, bf16[1024,256]{1,0:T(8,128)(2,1)S(1)}, u32[]{:S(2)}, u32[]{:S(2)}) %collective-permute-start.3) | collective-permute-done | bytes 524320 | tf_op jit(solution)/shard_map/ppermute | solution.py:25
  17.3 0.9 broadcast_select_fusion
  18.2 1.5 collective-permute-start.4
  19.7 2.3 %copy.43 = bf16[512,4,1,128]{0,3,1,2:T(8,128)(2,1)S(1)} copy(bf16[512,4,1,128]{3,2,1,0:T(2,128)(2,1)} %constant_dynamic-slice_fusion) | data formatting | bytes 1048576
  22.3 0.7 dynamic-slice_bitcast_fusion
  23.0 1.6 collective-permute-start.8
  25.1 6.2 %collective-permute-done.4.refs_1_ = bf16[1024,256]{1,0:T(8,128)(2,1)} collective-permute-done((bf16[1024,256]{1,0:T(8,128)(2,1)}, bf16[1024,256]{1,0:T(8,128)(2,1)}, u32[]{:S(2)}, u32[]{:S(2)}) %collective-permute-start.4) | collective-permute-done | bytes 524320 | tf_op jit(solution)/shard_map/ppermute | solution.py:20
  31.3 1.5 collective-permute-start.5
  33.1 0.8 copy.35
  34.1 1.5 fusion.11
  35.7 1.9 maximum_select_fusion.1.refs_5_.refs_10_
  37.6 0.8 copy-done.20
  38.8 4.6 %collective-permute-done.8.refs_2_ = bf16[1024,256]{1,0:T(8,128)(2,1)} collective-permute-done((bf16[1024,256]{1,0:T(8,128)(2,1)S(1)}, bf16[1024,256]{1,0:T(8,128)(2,1)}, u32[]{:S(2)}, u32[]{:S(2)}) %collective-permute-start.8) | collective-permute-done | bytes 524320 | tf_op jit(solution)/shard_map/ppermute | solution.py:20
  43.5 0.8 copy-done.18
  44.8 8.5 %collective-permute-done.5.refs_2_ = bf16[1024,256]{1,0:T(8,128)(2,1)} collective-permute-done((bf16[1024,256]{1,0:T(8,128)(2,1)}, bf16[1024,256]{1,0:T(8,128)(2,1)}, u32[]{:S(2)}, u32[]{:S(2)}) %collective-permute-start.5) | collective-permute-done | bytes 524320 | tf_op jit(solution)/shard_map/ppermute | solution.py:20
  53.5 1.1 copy.39.refs_6_.refs_8_
  54.5 0.9 maximum_select_fusion.4.refs_8_
  55.4 1.0 fusion.9
  56.5 1.0 copy-done.3
  57.5 1.0 copy-done.5
  58.5 1.0 copy-done.8
  59.6 1.0 copy-done.21
  60.6 5.8 %shard_map.84 = (bf16[2048,512]{1,0:T(8,128)(2,1)S(1)}, bf16[2048,512]{1,0:T(8,128)(2,1)S(1)}, bf16[2048,128]{1,0:T(8,128)(2,1)S(1)}, bf16[2048,128]{1,0:T(8,128...) custom-call(s32[1]{0:T(128)} %bitcast.refs_0_.refs_3_, bf16[1024,256]{1,0:T(8,128)(2,1)S(1)} %copy-done.3, ...), custom_call_target="tpu_custom_call" | custom-call | tf_op jit(solution)/shard_map/pallas_call | solution.py:258
  66.5 6.9 %shard_map.87.refs_8_ = f32[2048,128]{1,0:T(8,128)S(1)} custom-call(s32[4]{0:T(128)S(1)} %convert_reduce_fusion.1.refs_0_, s32[12]{0:T(128)S(1)} %get-tuple-element.76.refs_1_, s32[12]{0:T(128)S(1)} %get-tuple-element.77.refs_2_, bf16[2048,128]{1,0:T(8,128)(2,1)S(1)} %get-tuple-element.39.refs_3_.refs_4_, ...), custom_call_target="tpu_custom_call" | custom-call | tf_op jit(solution)/shard_map/pallas_call | solution.py:258
  73.4 4.6 %shard_map.86 = (bf16[2048,512]{1,0:T(8,128)(2,1)S(1)}, bf16[2048,256]{1,0:T(8,128)(2,1)S(1)}, bf16[2048,128]{1,0:T(8,128)(2,1)S(1)}, bf16[2048,128]{1,0:T(8,128)(2,1)S(1)}) custom-call(s32[1]{0:T(128)} %bitcast.refs_0_.refs_3_, bf16[1024,256]{1,0:T(8,128)(2,1)S(1)} %copy-done.11, bf16[1024,256]{1,0:T(8,128)(2,1)} %collective-permute-done.8.refs_2_, ...), custom_call_target="tpu_custom_call" | custom-call | tf_op jit(solution)/shard_map/pallas_call | solution.py:258
  78.0 0.7 shard_map.88.refs_8_
  78.8 4.9 %shard_map.85 = (bf16[2048,512]{1,0:T(8,128)(2,1)S(1)}, bf16[2048,256]{1,0:T(8,128)(2,1)S(1)}, bf16[2048,128]{1,0:T(8,128)(2,1)S(1)}, bf16[2048,128]{1,0:T(8,128)(2,1)S(1)}) custom-call(s32[1]{0:T(128)} %bitcast.refs_0_.refs_3_, bf16[1024,256]{1,0:T(8,128)(2,1)} %collective-permute-done.4.refs_1_, bf16[1024,256]{1,0:T(8,128)(2,1)} %collective-permute-done.5.refs_2_, ...), custom_call_target="tpu_custom_call" | custom-call | tf_op jit(solution)/shard_map/pallas_call | solution.py:258
  83.8 0.8 shard_map.89.refs_1_
  84.6 4.3 %shard_map.90 = (bf16[2048,128]{1,0:T(8,128)(2,1)S(1)}, bf16[2048,128]{1,0:T(8,128)(2,1)S(1)}, bf16[2048,128]{1,0:T(8,128)(2,1)S(1)}) custom-call(s32[1]{0:T(128)} %bitcast.refs_0_.refs_3_, f32[2048,128]{1,0:T(8,128)S(1)} %shard_map.89.refs_1_, bf16[2048,128]{1,0:T(8,128)(2,1)S(1)} %get-tuple-element.46.refs_2_, ...), custom_call_target="tpu_custom_call" | custom-call | tf_op jit(solution)/shard_map/pallas_call | solution.py:258
  88.8 2.2 shard_map.92
  91.0 1.0 copy-done.27
  92.0 0.7 shard_map.95.refs_2_
  92.8 2.1 shard_map.93
  94.9 1.0 copy-done.14
  95.9 1.0 copy-done.26
  96.9 14.0 %shard_map.94 = (bf16[1024,512]{1,0:T(8,128)(2,1)S(1)}, bf16[1024,512]{1,0:T(8,128)(2,1)S(1)}, bf16[2048,512]{1,0:T(8,128)(2,1)S(1)}, f32[2048,128]{1,0:T(8,128)S(1)}) custom-call(s32[4]{0:T(128)S(1)} %convert_reduce_fusion.1.refs_0_, s32[12]{0:T(128)S(1)} %get-tuple-element.76.refs_1_, ...), custom_call_target="tpu_custom_call", output_to_operand_aliasing={{3}: (12, {})} | custom-call | tf_op jit(solution)/shard_map/pallas_call | solution.py:258
  110.9 0.7 shard_map.96.refs_4_
  112.2 3.3 %shard_map.91 = (bf16[1024,512]{1,0:T(8,128)(2,1)S(1)}, bf16[1024,512]{1,0:T(8,128)(2,1)S(1)}, f32[512,256]{1,0:T(8,128)S(1)}) custom-call(s32[1]{0:T(128)} %bitcast.refs_0_.refs_3_, bf16[2048,128]{1,0:T(8,128)(2,1)S(1)} %get-tuple-element.48.refs_1_, bf16[2048,128]{1,0:T(8,128)(2,1)S(1)} %get-tuple-element.49.refs_2_.refs_13_, ...), custom_call_target="tpu_custom_call" | custom-call | tf_op jit(solution)/shard_map/pallas_call | solution.py:258
  115.5 2.1 shard_map.97
  117.6 7.6 %collective-permute-start.25 = (bf16[256,640]{1,0:T(8,128)(2,1)}, bf16[256,640]{1,0:T(8,128)(2,1)S(1)}, u32[]{:S(2)}, u32[]{:S(2)}) collective-permute-start(bf16[256,640]{1,0:T(8,128)(2,1)} %get-tuple-element.71), channel_id=1, source_target_pairs={{0,4},{2,6},{4,0},{6,2},{8,12},{10,14},{12,8},{14,10},{16,20},{18,... | collective-permute-start | bytes 983048 | tf_op jit(solution)/shard_map/ppermute | solution.py:20
  126.1 7.7 %collective-permute-done.25 = bf16[256,640]{1,0:T(8,128)(2,1)S(1)} collective-permute-done((bf16[256,640]{1,0:T(8,128)(2,1)}, bf16[256,640]{1,0:T(8,128)(2,1)S(1)}, u32[]{:S(2)}, u32[]{:S(2)}) %collective-permute-start.25) | collective-permute-done | bytes 327712 | tf_op jit(solution)/shard_map/ppermute | solution.py:20
  134.0 27.4 %collective-permute-start.26 = (bf16[128,640]{1,0:T(8,128)(2,1)S(1)}, bf16[128,640]{1,0:T(8,128)(2,1)S(1)}, u32[]{:S(2)}, u32[]{:S(2)}) collective-permute-start(bf16[128,640]{1,0:T(8,128)(2,1)S(1)} %dynamic-slice_convert_fusion), channel_id=1, source_target_pairs={{0,8},{2,10},{4,12},{6,14},{8,0},{10,2},{12,4},{14,6},{16,24},{18,... | collective-permute-start | bytes 491528 | tf_op jit(solution)/shard_map/ppermute | solution.py:20
  162.5 2.9 %collective-permute-done.26 = bf16[128,640]{1,0:T(8,128)(2,1)S(1)} collective-permute-done((bf16[128,640]{1,0:T(8,128)(2,1)S(1)}, bf16[128,640]{1,0:T(8,128)(2,1)S(1)}, u32[]{:S(2)}, u32[]{:S(2)}) %collective-permute-start.26) | collective-permute-done | bytes 163872 | tf_op jit(solution)/shard_map/ppermute | solution.py:20
  165.5 2.8 %collective-permute-start.27 = (bf16[64,640]{1,0:T(8,128)(2,1)S(1)}, bf16[64,640]{1,0:T(8,128)(2,1)S(1)}, u32[]{:S(2)}, u32[]{:S(2)}) collective-permute-start(bf16[64,640]{1,0:T(8,128)(2,1)S(1)} %dynamic-slice_convert_fusion.1), channel_id=1, source_target_pairs={{0,16},{2,18},{4,20},{6,22},{8,24},{10,26},{12,28},{14,30},{16,0},... | collective-permute-start | bytes 245768 | tf_op jit(solution)/shard_map/ppermute | solution.py:20
  168.7 1.6 collective-permute-start.19
  170.9 2.8 %collective-permute-start.28 = (bf16[64,640]{1,0:T(8,128)(2,1)S(1)}, bf16[64,640]{1,0:T(8,128)(2,1)S(1)}, u32[]{:S(2)}, u32[]{:S(2)}) collective-permute-start(bf16[64,640]{1,0:T(8,128)(2,1)S(1)} %add_convert_fusion.1), channel_id=1, source_target_pairs={{0,16},{2,18},{4,20},{6,22},{8,24},{10,26},{12,28},{14,30},{16,0},... | collective-permute-start | bytes 245768 | tf_op jit(solution)/shard_map/ppermute | solution.py:20
  174.1 1.6 collective-permute-start.22
  175.7 7.9 %collective-permute-done.19 = bf16[1024,256]{1,0:T(8,128)(2,1)S(1)} collective-permute-done((bf16[1024,256]{1,0:T(8,128)(2,1)S(1)}, bf16[1024,256]{1,0:T(8,128)(2,1)S(1)}, u32[]{:S(2)}, u32[]{:S(2)}) %collective-permute-start.19) | collective-permute-done | bytes 524320 | tf_op jit(solution)/shard_map/ppermute | solution.py:20
  183.7 0.6 collective-permute-start.20
  185.2 1.6 collective-permute-start.17
  186.7 8.1 %collective-permute-done.22 = bf16[1024,256]{1,0:T(8,128)(2,1)S(1)} collective-permute-done((bf16[1024,256]{1,0:T(8,128)(2,1)S(1)}, bf16[1024,256]{1,0:T(8,128)(2,1)S(1)}, u32[]{:S(2)}, u32[]{:S(2)}) %collective-permute-start.22) | collective-permute-done | bytes 524320 | tf_op jit(solution)/shard_map/ppermute | solution.py:20
  195.0 1.3 collective-permute-start.23
  197.4 1.6 collective-permute-start.15
  199.0 4.5 %collective-permute-done.30 = bf16[256,640]{1,0:T(8,128)(2,1)S(1)} collective-permute-done((bf16[256,640]{1,0:T(8,128)(2,1)S(1)}, bf16[256,640]{1,0:T(8,128)(2,1)S(1)}, u32[]{:S(2)}, u32[]{:S(2)}) %collective-permute-start.30) | collective-permute-done | bytes 327712 | tf_op jit(solution)/shard_map/ppermute | solution.py:20
  203.9 2.1 collective-permute-done.17
  206.1 0.8 fusion.7
  206.9 1.6 collective-permute-start.24
  208.5 6.4 %collective-permute-done.15 = bf16[1024,256]{1,0:T(8,128)(2,1)S(1)} collective-permute-done((bf16[1024,256]{1,0:T(8,128)(2,1)S(1)}, bf16[1024,256]{1,0:T(8,128)(2,1)S(1)}, u32[]{:S(2)}, u32[]{:S(2)}) %collective-permute-start.15) | collective-permute-done | bytes 524320 | tf_op jit(solution)/shard_map/ppermute | solution.py:20
  214.9 1.0 fusion.6
  215.9 2.6 %shard_map.98 = (f32[4096,128]{1,0:T(8,128)}, f32[2,128,512]{2,1,0:T(8,128)}) custom-call(s32[2]{0:T(128)S(1)} %pad_add_fusion.refs_0_, bf16[512,640]{1,0:T(8,128)(2,1)S(1)} %maximum_select_fusion.refs_1_, bf16[512,640]{1,0:T(8,128)(2,1)S(1)} %collective-permute-done.31.refs_2_), custom_call_target="tpu_custom_call" | custom-call | tf_op jit(solution)/shard_map/pallas_call | solution.py:258
  218.6 2.3 %add_convert_fusion = bf16[1024,256]{1,0:T(8,128)(2,1)} fusion(bf16[1024,256]{1,0:T(8,128)(2,1)} %refs_4_.3, f32[1024,256]{1,0:T(8,128)S(1)} %get-tuple-element.78, f32[1024,512]{1,0:T(8,128)S(1)} %get-tuple-element.79, f32[1024]{0:T(1024)S(1)} %bitcast.32, f32[1024]{0:T(1024)S(1)} %bitcast.31, f32[1024]{0:T(1024)S(1)} %add_rsqrt_fusion), kind=kLoop, calls=%fused_computation.26 | loop fusion | flops 2097152 | bytes 3158016 | tf_op jit(solution)/shard_map/convert_element_type | solution.py:444
  (125 shorter events, 10.0 us)
Async XLA Ops:
  0.6 7.3 %copy-start = (bf16[512,4,2,128]{3,2,1,0:T(2,128)(2,1)S(1)}, bf16[512,4,2,128]{3,2,1,0:T(2,128)(2,1)}, u32[]{:S(2)}) copy-start(bf16[512,4,2,128]{3,2,1,0:T(2,128)(2,1)} %param.7) | copy-start | bytes 3145732
  0.6 16.6 %copy-start.2 = (bf16[1024,256]{1,0:T(8,128)(2,1)S(1)}, bf16[1024,256]{1,0:T(8,128)(2,1)}, u32[]{:S(2)}) copy-start(bf16[1024,256]{1,0:T(8,128)(2,1)} %refs_1_.1) | copy-start | bytes 1572868
  0.7 19.1 %copy-start.30 = (s32[16384]{0:T(1024)S(1)}, s32[16384]{0:T(1024)}, u32[]{:S(2)}) copy-start(s32[16384]{0:T(1024)} %param.9) | copy-start | bytes 196612
  0.7 16.6 %collective-permute-start.3 = (bf16[1024,256]{1,0:T(8,128)(2,1)}, bf16[1024,256]{1,0:T(8,128)(2,1)S(1)}, u32[]{:S(2)}, u32[]{:S(2)}) collective-permute-start(bf16[1024,256]{1,0:T(8,128)(2,1)} %refs_1_.1), channel_id=1, source_target_pairs={{0,8},{2,10},{4,12},{6,14},{8,16},{10,18},{12,20},{14,22},{16,24},... | collective-permute-start | bytes 1572872 | tf_op jit(solution)/shard_map/ppermute | solution.py:25
  5.8 18.8 %collective-permute-start = (bf16[1024,256]{1,0:T(8,128)(2,1)}, bf16[1024,256]{1,0:T(8,128)(2,1)S(1)}, u32[]{:S(2)}, u32[]{:S(2)}) collective-permute-start(bf16[1024,256]{1,0:T(8,128)(2,1)} %refs_1_.1), channel_id=1, source_target_pairs={{0,1},{1,0},{2,3},{3,2},{4,5},{5,4},{6,7},{7,6},{8,9},{9,8},{10,11... | collective-permute-start | bytes 1572872 | tf_op jit(solution)/shard_map/ppermute | solution.py:20
  7.4 17.3 %collective-permute-start.1 = (bf16[1024,256]{1,0:T(8,128)(2,1)}, bf16[1024,256]{1,0:T(8,128)(2,1)}, u32[]{:S(2)}, u32[]{:S(2)}) collective-permute-start(bf16[1024,256]{1,0:T(8,128)(2,1)} %refs_1_.1), channel_id=1, source_target_pairs={{0,2},{2,0},{4,6},{6,4},{8,10},{10,8},{12,14},{14,12},{16,18},{18,... | collective-permute-start | bytes 1572872 | tf_op jit(solution)/shard_map/ppermute | solution.py:20
  7.4 30.2 %collective-permute-start.11 = (bf16[1024,256]{1,0:T(8,128)(2,1)}, bf16[1024,256]{1,0:T(8,128)(2,1)}, u32[]{:S(2)}, u32[]{:S(2)}) collective-permute-start(bf16[1024,256]{1,0:T(8,128)(2,1)} %refs_4_.3), channel_id=1, source_target_pairs={{0,1},{1,0},{2,3},{3,2},{4,5},{5,4},{6,7},{7,6},{8,9},{9,8},{10,11... | collective-permute-start | bytes 1572872 | tf_op jit(solution)/shard_map/ppermute | solution.py:20
  9.9 12.3 %copy-start.28 = (bf16[2,128,512]{2,1,0:T(8,128)(2,1)S(1)}, bf16[2,128,512]{2,1,0:T(8,128)(2,1)}, u32[]{:S(2)}) copy-start(bf16[2,128,512]{2,1,0:T(8,128)(2,1)} %param.8) | copy-start | bytes 786436
  17.3 7.3 %copy-start.10 = (bf16[1024,256]{1,0:T(8,128)(2,1)}, bf16[1024,256]{1,0:T(8,128)(2,1)S(1)}, u32[]{:S(2)}) copy-start(bf16[1024,256]{1,0:T(8,128)(2,1)S(1)} %collective-permute-done.3.refs_1_) | copy-start | bytes 1572868
  18.2 13.1 %collective-permute-start.4 = (bf16[1024,256]{1,0:T(8,128)(2,1)}, bf16[1024,256]{1,0:T(8,128)(2,1)}, u32[]{:S(2)}, u32[]{:S(2)}) collective-permute-start(bf16[1024,256]{1,0:T(8,128)(2,1)} %broadcast_select_fusion), channel_id=1, source_target_pairs={{0,4},{2,6},{4,0},{6,2},{8,12},{10,14},{12,8},{14,10},{16,20},{18,... | collective-permute-start | bytes 1572872 | tf_op jit(solution)/shard_map/ppermute | solution.py:20
  23.0 20.4 %collective-permute-start.8 = (bf16[1024,256]{1,0:T(8,128)(2,1)S(1)}, bf16[1024,256]{1,0:T(8,128)(2,1)}, u32[]{:S(2)}, u32[]{:S(2)}) collective-permute-start(bf16[1024,256]{1,0:T(8,128)(2,1)S(1)} %collective-permute-done.3.refs_1_), channel_id=1, source_target_pairs={{0,1},{1,0},{2,3},{3,2},{4,5},{5,4},{6,7},{7,6},{8,9},{9,8},{10,11... | collective-permute-start | bytes 1572872 | tf_op jit(solution)/shard_map/ppermute | solution.py:20
  24.6 28.9 %copy-start.7 = (bf16[1024,256]{1,0:T(8,128)(2,1)}, bf16[1024,256]{1,0:T(8,128)(2,1)S(1)}, u32[]{:S(2)}) copy-start(bf16[1024,256]{1,0:T(8,128)(2,1)S(1)} %collective-permute-done.refs_2_) | copy-start | bytes 1572868
  24.6 18.9 %collective-permute-start.9 = (bf16[1024,256]{1,0:T(8,128)(2,1)S(1)}, bf16[1024,256]{1,0:T(8,128)(2,1)S(1)}, u32[]{:S(2)}, u32[]{:S(2)}) collective-permute-start(bf16[1024,256]{1,0:T(8,128)(2,1)S(1)} %collective-permute-done.3.refs_1_), channel_id=1, source_target_pairs={{0,2},{2,0},{4,6},{6,4},{8,10},{10,8},{12,14},{14,12},{16,18},{18,... | collective-permute-start | bytes 1572872 | tf_op jit(solution)/shard_map/ppermute | solution.py:20
  24.7 12.9 %collective-permute-start.2 = (bf16[1024,256]{1,0:T(8,128)(2,1)S(1)}, bf16[1024,256]{1,0:T(8,128)(2,1)S(1)}, u32[]{:S(2)}, u32[]{:S(2)}) collective-permute-start(bf16[1024,256]{1,0:T(8,128)(2,1)S(1)} %collective-permute-done.refs_2_), channel_id=1, source_target_pairs={{0,2},{2,0},{4,6},{6,4},{8,10},{10,8},{12,14},{14,12},{16,18},{18,... | collective-permute-start | bytes 1572872 | tf_op jit(solution)/shard_map/ppermute | solution.py:20
  31.3 21.9 %collective-permute-start.5 = (bf16[1024,256]{1,0:T(8,128)(2,1)}, bf16[1024,256]{1,0:T(8,128)(2,1)}, u32[]{:S(2)}, u32[]{:S(2)}) collective-permute-start(bf16[1024,256]{1,0:T(8,128)(2,1)} %collective-permute-done.4.refs_1_), channel_id=1, source_target_pairs={{0,1},{1,0},{2,3},{3,2},{4,5},{5,4},{6,7},{7,6},{8,9},{9,8},{10,11... | collective-permute-start | bytes 1572872 | tf_op jit(solution)/shard_map/ppermute | solution.py:20
  37.5 17.0 %copy-start.29 = (bf16[2,128,512]{2,1,0:T(8,128)(2,1)S(1)}, bf16[2,128,512]{2,1,0:T(8,128)(2,1)}, u32[]{:S(2)}) copy-start(bf16[2,128,512]{2,1,0:T(8,128)(2,1)} %param.8) | copy-start | bytes 786436
  37.5 47.0 %collective-permute-start.12 = (bf16[1024,256]{1,0:T(8,128)(2,1)}, bf16[1024,256]{1,0:T(8,128)(2,1)}, u32[]{:S(2)}, u32[]{:S(2)}) collective-permute-start(bf16[1024,256]{1,0:T(8,128)(2,1)} %refs_4_.3), channel_id=1, source_target_pairs={{0,2},{2,0},{4,6},{6,4},{8,10},{10,8},{12,14},{14,12},{16,18},{18,... | collective-permute-start | bytes 1572872 | tf_op jit(solution)/shard_map/ppermute | solution.py:20
  37.6 0.8 copy-start.20
  38.4 46.2 %collective-permute-start.13 = (bf16[1024,256]{1,0:T(8,128)(2,1)}, bf16[1024,256]{1,0:T(8,128)(2,1)}, u32[]{:S(2)}, u32[]{:S(2)}) collective-permute-start(bf16[1024,256]{1,0:T(8,128)(2,1)} %collective-permute-done.11.refs_5_), channel_id=1, source_target_pairs={{0,2},{2,0},{4,6},{6,4},{8,10},{10,8},{12,14},{14,12},{16,18},{18,... | collective-permute-start | bytes 1572872 | tf_op jit(solution)/shard_map/ppermute | solution.py:20
  43.4 35.4 %collective-permute-start.6 = (bf16[1024,256]{1,0:T(8,128)(2,1)}, bf16[1024,256]{1,0:T(8,128)(2,1)}, u32[]{:S(2)}, u32[]{:S(2)}) collective-permute-start(bf16[1024,256]{1,0:T(8,128)(2,1)} %collective-permute-done.4.refs_1_), channel_id=1, source_target_pairs={{0,2},{2,0},{4,6},{6,4},{8,10},{10,8},{12,14},{14,12},{16,18},{18,... | collective-permute-start | bytes 1572872 | tf_op jit(solution)/shard_map/ppermute | solution.py:20
  43.5 0.8 copy-start.18
  44.2 29.1 %collective-permute-start.10 = (bf16[1024,256]{1,0:T(8,128)(2,1)}, bf16[1024,256]{1,0:T(8,128)(2,1)}, u32[]{:S(2)}, u32[]{:S(2)}) collective-permute-start(bf16[1024,256]{1,0:T(8,128)(2,1)} %collective-permute-done.8.refs_2_), channel_id=1, source_target_pairs={{0,2},{2,0},{4,6},{6,4},{8,10},{10,8},{12,14},{14,12},{16,18},{18,... | collective-permute-start | bytes 1572872 | tf_op jit(solution)/shard_map/ppermute | solution.py:20
  53.3 25.5 %collective-permute-start.7 = (bf16[1024,256]{1,0:T(8,128)(2,1)}, bf16[1024,256]{1,0:T(8,128)(2,1)}, u32[]{:S(2)}, u32[]{:S(2)}) collective-permute-start(bf16[1024,256]{1,0:T(8,128)(2,1)} %collective-permute-done.5.refs_2_), channel_id=1, source_target_pairs={{0,2},{2,0},{4,6},{6,4},{8,10},{10,8},{12,14},{14,12},{16,18},{18,... | collective-permute-start | bytes 1572872 | tf_op jit(solution)/shard_map/ppermute | solution.py:20
  56.5 1.0 copy-start.3
  57.5 1.0 copy-start.5
  58.5 1.0 copy-start.8
  59.6 1.0 copy-start.21
  66.5 6.9 %copy-start.11 = (bf16[1024,256]{1,0:T(8,128)(2,1)S(1)}, bf16[1024,256]{1,0:T(8,128)(2,1)}, u32[]{:S(2)}) copy-start(bf16[1024,256]{1,0:T(8,128)(2,1)} %copy-done.10) | copy-start | bytes 1572868
  66.5 6.9 %copy-start.19 = (bf16[1024,256]{1,0:T(8,128)(2,1)S(1)}, bf16[1024,256]{1,0:T(8,128)(2,1)}, u32[]{:S(2)}) copy-start(bf16[1024,256]{1,0:T(8,128)(2,1)} %copy-done.18) | copy-start | bytes 1572868
  91.0 1.0 copy-start.27
  91.0 1.7 copy-start.16
  92.8 4.1 %copy-start.6 = (bf16[512,512]{1,0:T(8,128)(2,1)S(1)}, bf16[512,512]{1,0:T(8,128)(2,1)}, u32[]{:S(2)}) copy-start(bf16[512,512]{1,0:T(8,128)(2,1)} %maximum_select_fusion.1.refs_5_.refs_10_) | copy-start | bytes 1572868
  94.9 1.0 copy-start.14
  95.9 1.0 copy-start.26
  110.9 1.0 copy-start.12
  110.9 1.3 copy-start.24
  115.5 2.1 copy-start.22
  115.5 9.8 %copy-start.4 = (bf16[1024,256]{1,0:T(8,128)(2,1)S(1)}, bf16[1024,256]{1,0:T(8,128)(2,1)}, u32[]{:S(2)}) copy-start(bf16[1024,256]{1,0:T(8,128)(2,1)} %refs_1_.1) | copy-start | bytes 1572868
  115.5 9.8 %copy-start.9 = (bf16[1024,256]{1,0:T(8,128)(2,1)S(1)}, bf16[1024,256]{1,0:T(8,128)(2,1)}, u32[]{:S(2)}) copy-start(bf16[1024,256]{1,0:T(8,128)(2,1)} %copy-done.7) | copy-start | bytes 1572868
  117.6 16.2 %collective-permute-start.25 = (bf16[256,640]{1,0:T(8,128)(2,1)}, bf16[256,640]{1,0:T(8,128)(2,1)S(1)}, u32[]{:S(2)}, u32[]{:S(2)}) collective-permute-start(bf16[256,640]{1,0:T(8,128)(2,1)} %get-tuple-element.71), channel_id=1, source_target_pairs={{0,4},{2,6},{4,0},{6,2},{8,12},{10,14},{12,8},{14,10},{16,20},{18,... | collective-permute-start | bytes 983048 | tf_op jit(solution)/shard_map/ppermute | solution.py:20
  125.6 42.7 %collective-permute-start.18 = (bf16[1024,512]{1,0:T(8,128)(2,1)}, bf16[1024,512]{1,0:T(8,128)(2,1)S(1)}, u32[]{:S(2)}, u32[]{:S(2)}) collective-permute-start(bf16[1024,512]{1,0:T(8,128)(2,1)} %copy-done.27), channel_id=1, source_target_pairs={{0,2},{2,0},{4,6},{6,4},{8,10},{10,8},{12,14},{14,12},{16,18},{18,... | collective-permute-start | bytes 3145736 | tf_op jit(solution)/shard_map/ppermute | solution.py:20
  125.9 47.9 %collective-permute-start.21 = (bf16[1024,512]{1,0:T(8,128)(2,1)}, bf16[1024,512]{1,0:T(8,128)(2,1)S(1)}, u32[]{:S(2)}, u32[]{:S(2)}) collective-permute-start(bf16[1024,512]{1,0:T(8,128)(2,1)} %copy-done.26), channel_id=1, source_target_pairs={{0,2},{2,0},{4,6},{6,4},{8,10},{10,8},{12,14},{14,12},{16,18},{18,... | collective-permute-start | bytes 3145736 | tf_op jit(solution)/shard_map/ppermute | solution.py:20
  133.9 28.0 %copy-start.25 = (bf16[1024,512]{1,0:T(8,128)(2,1)S(1)}, bf16[1024,512]{1,0:T(8,128)(2,1)}, u32[]{:S(2)}) copy-start(bf16[1024,512]{1,0:T(8,128)(2,1)} %copy-done.24) | copy-start | bytes 3145732
  133.9 28.1 %copy-start.23 = (bf16[1024,512]{1,0:T(8,128)(2,1)S(1)}, bf16[1024,512]{1,0:T(8,128)(2,1)}, u32[]{:S(2)}) copy-start(bf16[1024,512]{1,0:T(8,128)(2,1)} %copy-done.22) | copy-start | bytes 3145732
  134.0 34.3 %copy-start.17 = (bf16[1024,512]{1,0:T(8,128)(2,1)S(1)}, bf16[1024,512]{1,0:T(8,128)(2,1)}, u32[]{:S(2)}) copy-start(bf16[1024,512]{1,0:T(8,128)(2,1)} %copy-done.16) | copy-start | bytes 3145732
  134.0 31.4 %collective-permute-start.26 = (bf16[128,640]{1,0:T(8,128)(2,1)S(1)}, bf16[128,640]{1,0:T(8,128)(2,1)S(1)}, u32[]{:S(2)}, u32[]{:S(2)}) collective-permute-start(bf16[128,640]{1,0:T(8,128)(2,1)S(1)} %dynamic-slice_convert_fusion), channel_id=1, source_target_pairs={{0,8},{2,10},{4,12},{6,14},{8,0},{10,2},{12,4},{14,6},{16,24},{18,... | collective-permute-start | bytes 491528 | tf_op jit(solution)/shard_map/ppermute | solution.py:20
  161.9 22.8 %collective-permute-start.16 = (bf16[1024,512]{1,0:T(8,128)(2,1)S(1)}, bf16[1024,512]{1,0:T(8,128)(2,1)S(1)}, u32[]{:S(2)}, u32[]{:S(2)}) collective-permute-start(bf16[1024,512]{1,0:T(8,128)(2,1)S(1)} %copy-done.25), channel_id=1, source_target_pairs={{0,2},{2,0},{4,6},{6,4},{8,10},{10,8},{12,14},{14,12},{16,18},{18,... | collective-permute-start | bytes 3145736 | tf_op jit(solution)/shard_map/ppermute | solution.py:20
  162.0 35.0 %collective-permute-start.14 = (bf16[1024,512]{1,0:T(8,128)(2,1)S(1)}, bf16[1024,512]{1,0:T(8,128)(2,1)S(1)}, u32[]{:S(2)}, u32[]{:S(2)}) collective-permute-start(bf16[1024,512]{1,0:T(8,128)(2,1)S(1)} %copy-done.23), channel_id=1, source_target_pairs={{0,2},{2,0},{4,6},{6,4},{8,10},{10,8},{12,14},{14,12},{16,18},{18,... | collective-permute-start | bytes 3145736 | tf_op jit(solution)/shard_map/ppermute | solution.py:20
  165.5 5.4 %collective-permute-start.27 = (bf16[64,640]{1,0:T(8,128)(2,1)S(1)}, bf16[64,640]{1,0:T(8,128)(2,1)S(1)}, u32[]{:S(2)}, u32[]{:S(2)}) collective-permute-start(bf16[64,640]{1,0:T(8,128)(2,1)S(1)} %dynamic-slice_convert_fusion.1), channel_id=1, source_target_pairs={{0,16},{2,18},{4,20},{6,22},{8,24},{10,26},{12,28},{14,30},{16,0},... | collective-permute-start | bytes 245768 | tf_op jit(solution)/shard_map/ppermute | solution.py:20
  168.3 5.4 %copy-start.15 = (bf16[1024,512]{1,0:T(8,128)(2,1)S(1)}, bf16[1024,512]{1,0:T(8,128)(2,1)}, u32[]{:S(2)}) copy-start(bf16[1024,512]{1,0:T(8,128)(2,1)} %copy-done.14) | copy-start | bytes 3145732
  168.7 14.9 %collective-permute-start.19 = (bf16[1024,256]{1,0:T(8,128)(2,1)S(1)}, bf16[1024,256]{1,0:T(8,128)(2,1)S(1)}, u32[]{:S(2)}, u32[]{:S(2)}) collective-permute-start(bf16[1024,256]{1,0:T(8,128)(2,1)S(1)} %slice.145), channel_id=1, source_target_pairs={{0,1},{1,0},{2,3},{3,2},{4,5},{5,4},{6,7},{7,6},{8,9},{9,8},{10,11... | collective-permute-start | bytes 1572872 | tf_op jit(solution)/shard_map/ppermute | solution.py:20
  170.9 13.5 %collective-permute-start.28 = (bf16[64,640]{1,0:T(8,128)(2,1)S(1)}, bf16[64,640]{1,0:T(8,128)(2,1)S(1)}, u32[]{:S(2)}, u32[]{:S(2)}) collective-permute-start(bf16[64,640]{1,0:T(8,128)(2,1)S(1)} %add_convert_fusion.1), channel_id=1, source_target_pairs={{0,16},{2,18},{4,20},{6,22},{8,24},{10,26},{12,28},{14,30},{16,0},... | collective-permute-start | bytes 245768 | tf_op jit(solution)/shard_map/ppermute | solution.py:20
  174.0 10.7 %copy-start.13 = (bf16[1024,512]{1,0:T(8,128)(2,1)S(1)}, bf16[1024,512]{1,0:T(8,128)(2,1)}, u32[]{:S(2)}) copy-start(bf16[1024,512]{1,0:T(8,128)(2,1)} %copy-done.12) | copy-start | bytes 3145732
  174.1 20.7 %collective-permute-start.22 = (bf16[1024,256]{1,0:T(8,128)(2,1)S(1)}, bf16[1024,256]{1,0:T(8,128)(2,1)S(1)}, u32[]{:S(2)}, u32[]{:S(2)}) collective-permute-start(bf16[1024,256]{1,0:T(8,128)(2,1)S(1)} %slice.144), channel_id=1, source_target_pairs={{0,1},{1,0},{2,3},{3,2},{4,5},{5,4},{6,7},{7,6},{8,9},{9,8},{10,11... | collective-permute-start | bytes 1572872 | tf_op jit(solution)/shard_map/ppermute | solution.py:20
  183.7 11.0 %collective-permute-start.20 = (bf16[1024,256]{1,0:T(8,128)(2,1)S(1)}, bf16[1024,256]{1,0:T(8,128)(2,1)S(1)}, u32[]{:S(2)}, u32[]{:S(2)}) collective-permute-start(bf16[1024,256]{1,0:T(8,128)(2,1)S(1)} %fusion.4), channel_id=1, source_target_pairs={{0,4},{2,6},{4,0},{6,2},{8,12},{10,14},{12,8},{14,10},{16,20},{18,... | collective-permute-start | bytes 1572872 | tf_op jit(solution)/shard_map/ppermute | solution.py:20
  184.4 11.9 %collective-permute-start.29 = (bf16[128,640]{1,0:T(8,128)(2,1)S(1)}, bf16[128,640]{1,0:T(8,128)(2,1)S(1)}, u32[]{:S(2)}, u32[]{:S(2)}) collective-permute-start(bf16[128,640]{1,0:T(8,128)(2,1)S(1)} %maximum_select_fusion.3), channel_id=1, source_target_pairs={{0,8},{2,10},{4,12},{6,14},{8,0},{10,2},{12,4},{14,6},{16,24},{18,... | collective-permute-start | bytes 491528 | tf_op jit(solution)/shard_map/ppermute | solution.py:20
  185.2 20.8 %collective-permute-start.17 = (bf16[1024,256]{1,0:T(8,128)(2,1)S(1)}, bf16[1024,256]{1,0:T(8,128)(2,1)S(1)}, u32[]{:S(2)}, u32[]{:S(2)}) collective-permute-start(bf16[1024,256]{1,0:T(8,128)(2,1)S(1)} %slice.146), channel_id=1, source_target_pairs={{0,1},{1,0},{2,3},{3,2},{4,5},{5,4},{6,7},{7,6},{8,9},{9,8},{10,11... | collective-permute-start | bytes 1572872 | tf_op jit(solution)/shard_map/ppermute | solution.py:20
  195.0 11.1 %collective-permute-start.23 = (bf16[1024,256]{1,0:T(8,128)(2,1)S(1)}, bf16[1024,256]{1,0:T(8,128)(2,1)S(1)}, u32[]{:S(2)}, u32[]{:S(2)}) collective-permute-start(bf16[1024,256]{1,0:T(8,128)(2,1)S(1)} %fusion.3), channel_id=1, source_target_pairs={{8,0},{10,2},{12,4},{14,6},{16,8},{18,10},{20,12},{22,14},{24,16},... | collective-permute-start | bytes 1572872 | tf_op jit(solution)/shard_map/ppermute | solution.py:25
  196.4 7.1 %collective-permute-start.30 = (bf16[256,640]{1,0:T(8,128)(2,1)S(1)}, bf16[256,640]{1,0:T(8,128)(2,1)S(1)}, u32[]{:S(2)}, u32[]{:S(2)}) collective-permute-start(bf16[256,640]{1,0:T(8,128)(2,1)S(1)} %maximum_select_fusion.2), channel_id=1, source_target_pairs={{0,4},{2,6},{4,0},{6,2},{8,12},{10,14},{12,8},{14,10},{16,20},{18,... | collective-permute-start | bytes 983048 | tf_op jit(solution)/shard_map/ppermute | solution.py:20
  197.4 17.4 %collective-permute-start.15 = (bf16[1024,256]{1,0:T(8,128)(2,1)S(1)}, bf16[1024,256]{1,0:T(8,128)(2,1)S(1)}, u32[]{:S(2)}, u32[]{:S(2)}) collective-permute-start(bf16[1024,256]{1,0:T(8,128)(2,1)S(1)} %slice.147), channel_id=1, source_target_pairs={{0,1},{1,0},{2,3},{3,2},{4,5},{5,4},{6,7},{7,6},{8,9},{9,8},{10,11... | collective-permute-start | bytes 1572872 | tf_op jit(solution)/shard_map/ppermute | solution.py:20
  203.8 12.1 %collective-permute-start.31 = (bf16[512,640]{1,0:T(8,128)(2,1)S(1)}, bf16[512,640]{1,0:T(8,128)(2,1)S(1)}, u32[]{:S(2)}, u32[]{:S(2)}) collective-permute-start(bf16[512,640]{1,0:T(8,128)(2,1)S(1)} %maximum_select_fusion.refs_1_), channel_id=1, source_target_pairs={{0,2},{2,0},{4,6},{6,4},{8,10},{10,8},{12,14},{14,12},{16,18},{18,... | collective-permute-start | bytes 1966088 | tf_op jit(solution)/shard_map/ppermute | solution.py:20
  206.9 11.6 %collective-permute-start.24 = (f32[2,1024]{1,0:T(2,128)S(1)}, f32[2,1024]{1,0:T(2,128)S(1)}, u32[]{:S(2)}, u32[]{:S(2)}) collective-permute-start(f32[2,1024]{1,0:T(2,128)S(1)} %pad_maximum_fusion.2), channel_id=1, source_target_pairs={{0,1},{1,0},{2,3},{3,2},{4,5},{5,4},{6,7},{7,6},{8,9},{9,8},{10,11... | collective-permute-start | bytes 24584 | tf_op jit(solution)/shard_map/ppermute | solution.py:20
  214.9 6.0 %copy-start.1 = (bf16[512,4,2,128]{3,2,1,0:T(2,128)(2,1)S(1)}, bf16[512,4,2,128]{3,2,1,0:T(2,128)(2,1)}, u32[]{:S(2)}) copy-start(bf16[512,4,2,128]{3,2,1,0:T(2,128)(2,1)} %param.7) | copy-start | bytes 3145732

commit v2 on v1

--- a/solution.py
+++ b/solution.py
@@ -69,11 +69,12 @@
             normed_ref[into, :] = normed
             pre = dot(normed, w_ref[...])
             gate = gate_of(pre)
-            act = pre * gate
-            slope_ref[into, :] = (gate + act * (1.0 - gate)).astype(bf16)
+            act = (pre * gate).astype(bf16)
+            gate = gate.astype(bf16)
+            slope_ref[into, :] = gate + act * (bf16(1.0) - gate)
             width = part_refs[0].shape[1]
             for p, part in enumerate(part_refs):
-                part[into, :] = act[:, p * width : (p + 1) * width].astype(bf16)
+                part[into, :] = act[:, p * width : (p + 1) * width]
             return carry
 
         lax.fori_loop(0, count // size, rows_step, 0)
@@ -200,18 +201,19 @@
     k_tiles = k_ref.shape[0] // TILE
     for_tiles(low_ref, first_ref, last_ref, q_tiles, k_tiles, block_off, query_off, step)
 
-    def narrow(grads, part):
-        into = slice(part * width, (part + 1) * width)
-        grads_ref[:, into] = (grads * slope_ref[:, into].astype(f32)).astype(bf16)
-
     if own:
         grads_ref[:, :width] = before[1][...]
-        narrow(dv_ref[...], 1)
-        narrow(dq_ref[...] * scale, 2)
-        narrow(dk_ref[...] * scale, 3)
-    else:
-        narrow(dv_ref[...], 0)
-        narrow(dk_ref[...] * scale, 1)
+    parts = ((1, dv_ref), (2, dq_ref), (3, dk_ref)) if own else ((0, dv_ref), (1, dk_ref))
+
+    def narrow(step, carry):
+        rows = aligned(step * 256, 256)
+        for part, ref in parts:
+            into = slice(part * width, (part + 1) * width)
+            grads = ref[rows, :] if ref is dv_ref else ref[rows, :] * scale
+            grads_ref[rows, into] = (grads * slope_ref[rows, into].astype(f32)).astype(bf16)
+        return carry
+
+    lax.fori_loop(0, dk_ref.shape[0] // 256, narrow, 0)
     core = core_ref[0]
     count = send_ref.shape[0]
     send_ref[...] = dot(grads_ref[aligned((1 - core) * count, count), :], w_ref[...], NT).astype(bf16)
@@ -219,37 +221,48 @@
 
 
 def weight_kernel(normed_ref, grads_ref, *rest):
-    *before, out_ref = rest
     grads = dot(normed_ref[...], grads_ref[...], TN)
-    out_ref[...] = grads + before[0][...] if before else grads
-
-
-def weight_own_kernel(high_ref, normed_ref, grads_ref, early_ref, kv_ref, send_ref, keep_ref, sum_ref):
+    rest[-1][...] = grads if len(rest) == 1 else grads + rest[0][...]
+
+
+def weight_own_kernel(side_ref, normed_ref, grads_ref, early_ref, kv_ref, send_ref, keep_ref, sum_ref):
     width = kv_ref.shape[1] // 2
-    size = send_ref.shape[0]
     sum_ref[:, width : 4 * width] = dot(normed_ref[...], grads_ref[:, width:], TN)
     sum_ref[:, width : 2 * width] += kv_ref[:, :width]
     sum_ref[:, 3 * width : 4 * width] += kv_ref[:, width:]
     sum_ref[:, :width] = early_ref[:, :width]
     sum_ref[:, 4 * width :] = early_ref[:, width:]
-    high = high_ref[0]
-    send_ref[...] = sum_ref[aligned((1 - high) * size, size), :].astype(bf16)
-    keep_ref[...] = sum_ref[aligned(high * size, size), :]
-
-
-def assemble_kernel(place_ref, mine_ref, other_ref, in_ref, out_ref, *, scale):
-    core, flip = place_ref[0], place_ref[1]
-    width = out_ref.shape[1]
-    half = mine_ref.shape[0] // 2
+    side = side_ref[0]
+    size = send_ref.shape[0]
+    send_ref[...] = sum_ref[aligned((1 - side) * size, size), :].astype(bf16)
+    keep_ref[...] = sum_ref[aligned(side * size, size), :]
+
+
+def last_kernel(kept_ref, received_ref, out_ref):
+    out_ref[...] = (kept_ref[...] + received_ref[...].astype(f32)).astype(bf16)
+
+
+def halve_kernel(side_ref, kept_ref, received_ref, send_ref, keep_ref):
+    side = side_ref[0]
+    size = send_ref.shape[0]
+    other, mine = aligned((1 - side) * size, size), aligned(side * size, size)
+    send_ref[...] = (kept_ref[other, :] + received_ref[other, :].astype(f32)).astype(bf16)
+    keep_ref[...] = kept_ref[mine, :] + received_ref[mine, :].astype(f32)
+
+
+def assemble_kernel(place_ref, mine_ref, other_ref, in_ref, out_ref, turned_ref, *, scale, blocks):
+    core, place = place_ref[0], place_ref[1]
+    width = turned_ref.shape[1]
+    size = mine_ref.shape[0] // blocks
     for ref, head in ((mine_ref, core), (other_ref, 1 - core)):
-        for part in range(2):
-            where = (part + flip) % 2
-            rows = slice(part * half, (part + 1) * half)
+        for i in range(blocks):
+            rows = slice(i * size, (i + 1) * size)
+            true = jnp.bitwise_xor(i, place) * size
             for p in range(4):
                 piece = ref[rows, p * width : (p + 1) * width].astype(f32) * scale
-                in_ref[pl.ds(where * (half * 8) + 2 * p + head, half, stride=8), :] = piece
-            piece = ref[rows, 4 * width :].astype(f32) * scale
-            out_ref[head, :, aligned(where * half, half)] = piece.T
+                in_ref[pl.ds(true * 8 + 2 * p + head, size, stride=8), :] = piece
+            turned_ref[aligned(true, size), :] = ref[rows, 4 * width :].astype(f32) * scale
+        out_ref[head] = turned_ref[...].T
 
 
 def vmem_call(kernel, tables, arrays, outs, aliases=None, scratch=(), **static):
@@ -285,17 +298,6 @@
     def over(array, axis, bit):
         return swap(array, axis, bit)
 
-    far = shift(tokens, "seq", 4)
-    own_other = over(tokens, "col", 1)
-    own_set = (tokens, own_other, over(tokens, "seq", 1), over(own_other, "seq", 1))
-    near = over(jnp.where(odd, far, tokens), "seq", 2)
-    far_other = over(far, "col", 1)
-    far_set = (far, far_other, over(far, "seq", 1), over(far_other, "seq", 1))
-    near_other = over(near, "col", 1)
-    near_set = (near, near_other, over(near, "seq", 1), over(near_other, "seq", 1))
-    cot_other = over(cotangent, "col", 1)
-    cot_set = (cotangent, cot_other, over(cotangent, "seq", 1), over(cot_other, "seq", 1))
-
     flip = lax.axis_index("col") == 1
     w_in = lax.dynamic_index_in_dim(weight_in, core, 2, keepdims=False).reshape(width, 4 * head_size)
     w_in = jnp.where(flip, jnp.roll(w_in, half_width, axis=0), w_in)
@@ -311,6 +313,13 @@
     tables = (low, first, last)
     id_col, id_row = ids[:, None], ids[None, :]
 
+    far = shift(tokens, "seq", 4)
+    own_other = over(tokens, "col", 1)
+    own_other, w_in, w_kv, w_out, id_col, id_row, tables = lax.optimization_barrier(
+        (own_other, w_in, w_kv, w_out, id_col, id_row, tables)
+    )
+    own_set = (tokens, own_other, over(tokens, "seq", 1), over(own_other, "seq", 1))
+
     def shape(rows, cols, dtype=bf16):
         return jax.ShapeDtypeStruct((rows, cols), dtype)
 
@@ -320,6 +329,14 @@
         return vmem_call(project_kernel, (core_table,), (*token_set, weights), outs)
 
     normed_own, slope_own, up_part, value_own, query, key_own = project(own_set, w_in)
+    near = over(jnp.where(odd, far, tokens), "seq", 2)
+    far_other = over(far, "col", 1)
+    far_set = (far, far_other, over(lax.optimization_barrier((far, query))[0], "seq", 1), over(far_other, "seq", 1))
+    near_other = over(near, "col", 1)
+    near_set = (near, near_other, over(near, "seq", 1), over(near_other, "seq", 1))
+    cot_other = over(cotangent, "col", 1)
+    cot_set = (cotangent, cot_other, over(cotangent, "seq", 1), over(cot_other, "seq", 1))
+
     normed_far, slope_far, value_far, key_far = project(far_set, w_kv)
     normed_near, slope_near, value_near, key_near = project(near_set, w_kv)
     keys = [key_far, key_near, key_own]
@@ -400,38 +417,44 @@
     bits = []
     while 2 << len(bits) < seq_count:
         bits.append(2 << len(bits))
-    high = ((device_pos // bits[0]) % 2).astype(jnp.int32).reshape(1)
-    half_shape = (half_width, 5 * head_size)
-    sent, total = vmem_call(
+    sides = [((device_pos // bit) % 2).astype(jnp.int32) for bit in bits]
+    lanes = 5 * head_size
+    size = half_width
+    sent, kept = vmem_call(
         weight_own_kernel,
-        (high,),
+        (sides[0].reshape(1),),
         (normed_own, own_grads, grad_early, grad_kv),
-        (shape(*half_shape), shape(*half_shape, f32)),
-        scratch=[pltpu.VMEM((width, 5 * head_size), f32)],
-    )
-    for bit in bits:
-        if bit != bits[0]:
-            size = total.shape[0] // 2
-            side = (device_pos & bit) // bit
-            sent = lax.dynamic_slice_in_dim(total, (1 - side) * size, size).astype(bf16)
-            total = lax.dynamic_slice_in_dim(total, side * size, size)
-        total = total + over(sent, "seq", bit).astype(f32)
-    total = total.astype(bf16)
-    for bit in reversed(bits):
-        other = over(total, "seq", bit)
-        total = jnp.where(
-            (device_pos & bit) != 0,
-            jnp.concatenate([other, total], axis=0),
-            jnp.concatenate([total, other], axis=0),
-        )
-
-    place = jnp.stack([core, lax.axis_index("col")]).astype(jnp.int32)
+        (shape(size, lanes), shape(size, lanes, f32)),
+        scratch=[pltpu.VMEM((width, lanes), f32)],
+    )
+    for i, bit in enumerate(bits):
+        received = over(sent, "seq", bit)
+        if i + 1 < len(bits):
+            size = size // 2
+            sent, kept = vmem_call(
+                halve_kernel,
+                (sides[i + 1].reshape(1),),
+                (kept, received),
+                (shape(size, lanes), shape(size, lanes, f32)),
+            )
+        else:
+            total = vmem_call(last_kernel, (), (kept, received), shape(size, lanes))
+    for i, bit in reversed(list(enumerate(bits))):
+        total = jnp.concatenate([total, over(total, "seq", bit)], axis=0)
+
+    blocks = 1 << len(bits)
+    block_place = lax.axis_index("col") * (blocks // 2)
+    for i, side in enumerate(sides):
+        block_place = block_place ^ (side << (len(bits) - 1 - i))
+    place = jnp.stack([core, block_place]).astype(jnp.int32)
     grad_weight_in, grad_weight_out = vmem_call(
         assemble_kernel,
         (place,),
         (total, over(total, "seq", 1)),
         (shape(8 * width, head_size, f32), jax.ShapeDtypeStruct((2, head_size, width), f32)),
+        scratch=[pltpu.VMEM((width, head_size), f32)],
         scale=1.0 / math.sqrt(row_count * seq_count),
+        blocks=blocks,
     )
     grad_weight_in = grad_weight_in.reshape(width, 4, 2, head_size)
 

time: 222 us -> 220 us (level)
  starting transfers between devices: 65.9 us -> 58.4 us
  waiting for transfers between devices: 67 us -> 70.5 us
    ppermute x30, waiting for transfers between devices: 59.6 us -> 68.1 us  [swap(): lax.ppermute(block, axis, [(i, i ^ bit) for i in range(lax.axis_size(axis...]
    ppermute x30, starting transfers between devices: 59.5 us -> 53.6 us  [swap(): lax.ppermute(block, axis, [(i, i ^ bit) for i in range(lax.axis_size(axis...]
    ppermute x2, waiting for transfers between devices: 7.38 us -> 2.4 us  [shift(): lax.ppermute(block, axis, [(i, i + distance) for i in devices if i + dist...]
    unnamed x63 -> x75, local copies, waits for them, and re-layouts: 11.7 us -> 15.8 us
    add x4, other arithmetic: 1.25 us -> 4.02 us  [over_heads(): keep = keep.astype(f32) + over(send, 'seq', 1).astype(f32)]
    pallas_call x15 -> x18, Pallas kernels: 55.8 us -> 55.4 us  [vmem_call(): pl.pallas_call(lambda *refs: kernel(*refs, **static), out_shape=outs, in_...]
  transfers between devices with their start and end apart: 32 -> 32, of which waited for: 13 -> 11; matrix products, arithmetic and copies ran while one was open for 9% -> 8% of each run, Pallas kernels for 12% -> 22%
where the time goes in v2:
time: 220 us
  waiting for transfers between devices  70.5 us (32%)
  starting transfers between devices  58.4 us (27%)
  Pallas kernels  55.4 us (25%)
  local copies, waits for them, and re-layouts  21.5 us (10%)
  other arithmetic  12.5 us (6%)
    ppermute x30, waiting for transfers between devices, swap(): lax.ppermute(block, axis, [(i, i ^ bit) for i in range(lax.axis_size(axis...  68.1 us
    pallas_call x18, Pallas kernels, vmem_call(): pl.pallas_call(lambda *refs: kernel(*refs, **static), out_shape=outs, in_...  55.4 us
    ppermute x30, starting transfers between devices, swap(): lax.ppermute(block, axis, [(i, i ^ bit) for i in range(lax.axis_size(axis...  53.6 us
    unnamed x75, local copies, waits for them, and re-layouts  15.8 us
    ppermute x2, starting transfers between devices, shift(): lax.ppermute(block, axis, [(i, i + distance) for i in devices if i + dist...  4.8 us
  transfers between devices with their start and end apart: 32, of which 11 were waited for; matrix products, arithmetic and copies ran while one was open for 8% of the time, Pallas kernels for 22%

profile of v2, /device:TPU:0, one launch (start us, length us, event | category | flops | bytes accessed | tf_op | source)
XLA Modules:
  0.0 219.5 jit_solution(142832919076310022)
XLA Ops:
  0.6 3.0 %collective-permute-start = (bf16[1024,256]{1,0:T(8,128)(2,1)}, bf16[1024,256]{1,0:T(8,128)(2,1)S(1)}, u32[]{:S(2)}, u32[]{:S(2)}) collective-permute-start(bf16[1024,256]{1,0:T(8,128)(2,1)} %refs_1_.1), channel_id=1, source_target_pairs={{0,1},{1,0},{2,3},{3,2},{4,5},{5,4},{6,7},{7,6},{8,9},{9,8},{10,11... | collective-permute-start | bytes 1572872 | tf_op jit(solution)/shard_map/ppermute | solution.py:20
  3.7 3.5 %collective-permute-start.3 = (bf16[1024,256]{1,0:T(8,128)(2,1)}, bf16[1024,256]{1,0:T(8,128)(2,1)S(1)}, u32[]{:S(2)}, u32[]{:S(2)}) collective-permute-start(bf16[1024,256]{1,0:T(8,128)(2,1)} %refs_1_.1), channel_id=1, source_target_pairs={{0,8},{2,10},{4,12},{6,14},{8,16},{10,18},{12,20},{14,22},{16,24},... | collective-permute-start | bytes 1572872 | tf_op jit(solution)/shard_map/ppermute | solution.py:25
  7.2 0.7 pad_dynamic-slice_fusion
  8.3 2.1 constant_dynamic-slice_fusion
  10.3 2.3 %copy.43 = bf16[512,4,1,128]{0,3,1,2:T(8,128)(2,1)S(1)} copy(bf16[512,4,1,128]{3,2,1,0:T(2,128)(2,1)} %constant_dynamic-slice_fusion) | data formatting | bytes 1048576
  12.9 0.8 copy.35
  13.9 1.1 maximum_select_fusion.refs_5_.refs_10_
  15.3 1.6 maximum_select_fusion.1.refs_8_
  17.0 2.3 %collective-permute-done.3.refs_1_ = bf16[1024,256]{1,0:T(8,128)(2,1)S(1)} collective-permute-done((bf16[1024,256]{1,0:T(8,128)(2,1)}, bf16[1024,256]{1,0:T(8,128)(2,1)S(1)}, u32[]{:S(2)}, u32[]{:S(2)}) %collective-permute-start.3) | collective-permute-done | bytes 524320 | tf_op jit(solution)/shard_map/ppermute | solution.py:25
  19.4 1.6 collective-permute-start.4
  21.0 0.6 collective-permute-start.8
  21.6 1.5 collective-permute-start.11
  23.1 10.0 %collective-permute-done.4.refs_1_ = bf16[1024,256]{1,0:T(8,128)(2,1)} collective-permute-done((bf16[1024,256]{1,0:T(8,128)(2,1)S(1)}, bf16[1024,256]{1,0:T(8,128)(2,1)}, u32[]{:S(2)}, u32[]{:S(2)}) %collective-permute-start.4) | collective-permute-done | bytes 524320 | tf_op jit(solution)/shard_map/ppermute | solution.py:20
  33.6 4.6 %shard_map.84 = (bf16[2048,512]{1,0:T(8,128)(2,1)S(1)}, bf16[2048,512]{1,0:T(8,128)(2,1)S(1)}, bf16[2048,128]{1,0:T(8,128)(2,1)S(1)}, bf16[2048,128]{1,0:T(8,128...) custom-call(s32[1]{0:T(128)} %bitcast.refs_0_.refs_3_, bf16[1024,256]{1,0:T(8,128)(2,1)S(1)} %copy-done.5, ...), custom_call_target="tpu_custom_call" | custom-call | tf_op jit(solution)/shard_map/pallas_call | solution.py:271
  38.2 0.8 copy-done.2
  39.0 1.3 copy-done.7
  40.3 1.3 copy-done.9
  41.6 0.8 copy-done.15
  42.4 0.9 copy-done.18
  43.3 0.8 copy-done.29
  44.7 13.2 %collective-permute-done.5.refs_2_ = bf16[1024,256]{1,0:T(8,128)(2,1)} collective-permute-done((bf16[1024,256]{1,0:T(8,128)(2,1)}, bf16[1024,256]{1,0:T(8,128)(2,1)}, u32[]{:S(2)}, u32[]{:S(2)}) %collective-permute-start.5) | collective-permute-done | bytes 524320 | tf_op jit(solution)/shard_map/ppermute | solution.py:20
  58.4 0.8 copy-done.31
  59.2 1.0 copy.39.refs_6_.refs_8_
  60.3 1.0 copy-done.3
  61.3 1.0 copy-done.16
  62.3 1.0 copy-done.19
  63.4 6.8 %shard_map.87.refs_8_ = f32[2048,128]{1,0:T(8,128)S(1)} custom-call(s32[4]{0:T(128)S(1)} %convert_reduce_fusion.1.refs_0_, s32[12]{0:T(128)S(1)} %get-tuple-element.54.refs_1_, s32[12]{0:T(128)S(1)} %get-tuple-element.55.refs_2_, bf16[2048,128]{1,0:T(8,128)(2,1)S(1)} %copy-done.3, bf16[2048,128]{1,0:T(8,128)(2,1)S(1)} %copy-done.19, ...), custom_call_target="tpu_custom_call" | custom-call | tf_op jit(solution)/shard_map/pallas_call | solution.py:271
  70.3 4.7 %shard_map.86 = (bf16[2048,512]{1,0:T(8,128)(2,1)S(1)}, bf16[2048,256]{1,0:T(8,128)(2,1)S(1)}, bf16[2048,128]{1,0:T(8,128)(2,1)S(1)}, bf16[2048,128]{1,0:T(8,128)(2,1)S(1)}) custom-call(s32[1]{0:T(128)} %bitcast.refs_0_.refs_3_, bf16[1024,256]{1,0:T(8,128)(2,1)S(1)} %copy-done.22, bf16[1024,256]{1,0:T(8,128)(2,1)} %collective-permute-done.8.refs_2_, ...), custom_call_target="tpu_custom_call" | custom-call | tf_op jit(solution)/shard_map/pallas_call | solution.py:271
  75.0 0.7 shard_map.88.refs_8_
  75.7 4.9 %shard_map.85 = (bf16[2048,512]{1,0:T(8,128)(2,1)S(1)}, bf16[2048,256]{1,0:T(8,128)(2,1)S(1)}, bf16[2048,128]{1,0:T(8,128)(2,1)S(1)}, bf16[2048,128]{1,0:T(8,128)(2,1)S(1)}) custom-call(s32[1]{0:T(128)} %bitcast.refs_0_.refs_3_, bf16[1024,256]{1,0:T(8,128)(2,1)} %collective-permute-done.4.refs_1_, bf16[1024,256]{1,0:T(8,128)(2,1)} %collective-permute-done.5.refs_2_, ...), custom_call_target="tpu_custom_call" | custom-call | tf_op jit(solution)/shard_map/pallas_call | solution.py:271
  80.7 0.8 shard_map.89.refs_1_
  81.5 0.8 copy-done.10
  82.4 4.1 %shard_map.90 = (bf16[2048,128]{1,0:T(8,128)(2,1)S(1)}, bf16[2048,128]{1,0:T(8,128)(2,1)S(1)}, bf16[2048,128]{1,0:T(8,128)(2,1)S(1)}) custom-call(s32[1]{0:T(128)} %bitcast.refs_0_.refs_3_, f32[2048,128]{1,0:T(8,128)S(1)} %shard_map.89.refs_1_, bf16[2048,128]{1,0:T(8,128)(2,1)S(1)} %copy-done.30, bf16[2048,512]{1,0:T(8,128)(2,1)S(1)} %copy-done.10, ...), custom_call_target="tpu_custom_call" | custom-call | tf_op jit(solution)/shard_map/pallas_call | solution.py:271
  86.5 2.8 %shard_map.92 = (bf16[1024,512]{1,0:T(8,128)(2,1)}, bf16[1024,512]{1,0:T(8,128)(2,1)S(1)}, bf16[2048,256]{1,0:T(8,128)(2,1)S(1)}, f32[2048,128]{1,0:T(8,128)S(1)}) custom-call(s32[4]{0:T(128)S(1)} %convert_reduce_fusion.1.refs_0_, s32[12]{0:T(128)S(1)} %get-tuple-element.54.refs_1_, s32[12]{0:T(128)S(1)} %get-tuple-element.55.refs_2_, ...), custom_call_target="tpu_custom_call" | custom-call | tf_op jit(solution)/shard_map/pallas_call | solution.py:271
  89.8 0.8 shard_map.95.refs_2_
  90.6 2.7 %shard_map.93 = (bf16[1024,512]{1,0:T(8,128)(2,1)}, bf16[1024,512]{1,0:T(8,128)(2,1)S(1)}, bf16[2048,256]{1,0:T(8,128)(2,1)S(1)}, f32[2048,128]{1,0:T(8,128)S(1)}) custom-call(s32[4]{0:T(128)S(1)} %convert_reduce_fusion.1.refs_0_, s32[12]{0:T(128)S(1)} %get-tuple-element.54.refs_1_, ...), custom_call_target="tpu_custom_call", output_to_operand_aliasing={{3}: (12, {})} | custom-call | tf_op jit(solution)/shard_map/pallas_call | solution.py:271
  93.3 1.0 copy-done.26
  94.3 13.7 %shard_map.94 = (bf16[1024,512]{1,0:T(8,128)(2,1)S(1)}, bf16[1024,512]{1,0:T(8,128)(2,1)S(1)}, bf16[2048,512]{1,0:T(8,128)(2,1)S(1)}, f32[2048,128]{1,0:T(8,128)S(1)}) custom-call(s32[4]{0:T(128)S(1)} %convert_reduce_fusion.1.refs_0_, s32[12]{0:T(128)S(1)} %get-tuple-element.54.refs_1_, ...), custom_call_target="tpu_custom_call", output_to_operand_aliasing={{3}: (12, {})} | custom-call | tf_op jit(solution)/shard_map/pallas_call | solution.py:271
  108.0 0.7 shard_map.96.refs_4_
  109.4 1.0 copy-done.8
  110.4 3.3 %shard_map.91 = (bf16[1024,512]{1,0:T(8,128)(2,1)S(1)}, bf16[1024,512]{1,0:T(8,128)(2,1)S(1)}, f32[512,256]{1,0:T(8,128)S(1)}) custom-call(s32[1]{0:T(128)} %bitcast.refs_0_.refs_3_, bf16[2048,128]{1,0:T(8,128)(2,1)S(1)} %get-tuple-element.72.refs_1_, bf16[2048,128]{1,0:T(8,128)(2,1)S(1)} %get-tuple-element.73.refs_2_.refs_13_, ...), custom_call_target="tpu_custom_call" | custom-call | tf_op jit(solution)/shard_map/pallas_call | solution.py:271
  113.7 2.1 shard_map.97
  115.9 5.8 %collective-permute-start.25 = (bf16[256,640]{1,0:T(8,128)(2,1)}, bf16[256,640]{1,0:T(8,128)(2,1)S(1)}, u32[]{:S(2)}, u32[]{:S(2)}) collective-permute-start(bf16[256,640]{1,0:T(8,128)(2,1)} %get-tuple-element.95), channel_id=1, source_target_pairs={{0,4},{2,6},{4,0},{6,2},{8,12},{10,14},{12,8},{14,10},{16,20},{18,... | collective-permute-start | bytes 983048 | tf_op jit(solution)/shard_map/ppermute | solution.py:20
  121.9 8.0 %collective-permute-done.25.refs_2_ = bf16[256,640]{1,0:T(8,128)(2,1)S(1)} collective-permute-done((bf16[256,640]{1,0:T(8,128)(2,1)}, bf16[256,640]{1,0:T(8,128)(2,1)S(1)}, u32[]{:S(2)}, u32[]{:S(2)}) %collective-permute-start.25) | collective-permute-done | bytes 327712 | tf_op jit(solution)/shard_map/ppermute | solution.py:20
  130.0 29.2 %collective-permute-start.26 = (bf16[128,640]{1,0:T(8,128)(2,1)S(1)}, bf16[128,640]{1,0:T(8,128)(2,1)S(1)}, u32[]{:S(2)}, u32[]{:S(2)}) collective-permute-start(bf16[128,640]{1,0:T(8,128)(2,1)S(1)} %get-tuple-element.97), channel_id=1, source_target_pairs={{0,8},{2,10},{4,12},{6,14},{8,0},{10,2},{12,4},{14,6},{16,24},{18,... | collective-permute-start | bytes 491528 | tf_op jit(solution)/shard_map/ppermute | solution.py:20
  159.2 3.7 %collective-permute-done.26.refs_2_ = bf16[128,640]{1,0:T(8,128)(2,1)S(1)} collective-permute-done((bf16[128,640]{1,0:T(8,128)(2,1)S(1)}, bf16[128,640]{1,0:T(8,128)(2,1)S(1)}, u32[]{:S(2)}, u32[]{:S(2)}) %collective-permute-start.26) | collective-permute-done | bytes 163872 | tf_op jit(solution)/shard_map/ppermute | solution.py:20
  163.0 2.8 %collective-permute-start.27 = (bf16[64,640]{1,0:T(8,128)(2,1)S(1)}, bf16[64,640]{1,0:T(8,128)(2,1)S(1)}, u32[]{:S(2)}, u32[]{:S(2)}) collective-permute-start(bf16[64,640]{1,0:T(8,128)(2,1)S(1)} %get-tuple-element.99), channel_id=1, source_target_pairs={{0,16},{2,18},{4,20},{6,22},{8,24},{10,26},{12,28},{14,30},{16,0},... | collective-permute-start | bytes 245768 | tf_op jit(solution)/shard_map/ppermute | solution.py:20
  165.8 1.8 convert_add_fusion.1
  167.7 0.6 collective-permute-start.19
  169.0 2.2 %collective-permute-start.28 = (bf16[64,640]{1,0:T(8,128)(2,1)S(1)}, bf16[64,640]{1,0:T(8,128)(2,1)S(1)}, u32[]{:S(2)}, u32[]{:S(2)}) collective-permute-start(bf16[64,640]{1,0:T(8,128)(2,1)S(1)} %shard_map.100), channel_id=1, source_target_pairs={{0,16},{2,18},{4,20},{6,22},{8,24},{10,26},{12,28},{14,30},{16,0},... | collective-permute-start | bytes 245768 | tf_op jit(solution)/shard_map/ppermute | solution.py:20
  171.2 1.5 convert_add_fusion
  173.4 9.2 %collective-permute-done.19 = bf16[1024,256]{1,0:T(8,128)(2,1)S(1)} collective-permute-done((bf16[1024,256]{1,0:T(8,128)(2,1)S(1)}, bf16[1024,256]{1,0:T(8,128)(2,1)S(1)}, u32[]{:S(2)}, u32[]{:S(2)}) %collective-permute-start.19) | collective-permute-done | bytes 524320 | tf_op jit(solution)/shard_map/ppermute | solution.py:20
  182.8 0.6 collective-permute-start.20
  184.8 9.0 %collective-permute-done.22 = bf16[1024,256]{1,0:T(8,128)(2,1)S(1)} collective-permute-done((bf16[1024,256]{1,0:T(8,128)(2,1)S(1)}, bf16[1024,256]{1,0:T(8,128)(2,1)S(1)}, u32[]{:S(2)}, u32[]{:S(2)}) %collective-permute-start.22) | collective-permute-done | bytes 524320 | tf_op jit(solution)/shard_map/ppermute | solution.py:20
  194.1 1.3 collective-permute-start.23
  195.4 0.6 collective-permute-start.30
  196.4 0.6 collective-permute-start.15
  197.0 5.5 %collective-permute-done.30 = bf16[256,640]{1,0:T(8,128)(2,1)S(1)} collective-permute-done((bf16[256,640]{1,0:T(8,128)(2,1)S(1)}, bf16[256,640]{1,0:T(8,128)(2,1)S(1)}, u32[]{:S(2)}, u32[]{:S(2)}) %collective-permute-start.30) | collective-permute-done | bytes 327712 | tf_op jit(solution)/shard_map/ppermute | solution.py:20
  202.7 2.4 %collective-permute-done.17 = bf16[1024,256]{1,0:T(8,128)(2,1)S(1)} collective-permute-done((bf16[1024,256]{1,0:T(8,128)(2,1)S(1)}, bf16[1024,256]{1,0:T(8,128)(2,1)S(1)}, u32[]{:S(2)}, u32[]{:S(2)}) %collective-permute-start.17) | collective-permute-done | bytes 524320 | tf_op jit(solution)/shard_map/ppermute | solution.py:20
  205.1 0.7 fusion.7
  206.5 7.1 %collective-permute-done.15 = bf16[1024,256]{1,0:T(8,128)(2,1)S(1)} collective-permute-done((bf16[1024,256]{1,0:T(8,128)(2,1)S(1)}, bf16[1024,256]{1,0:T(8,128)(2,1)S(1)}, u32[]{:S(2)}, u32[]{:S(2)}) %collective-permute-start.15) | collective-permute-done | bytes 524320 | tf_op jit(solution)/shard_map/ppermute | solution.py:20
  213.6 1.0 fusion.6
  214.7 2.5 %shard_map.101 = (f32[4096,128]{1,0:T(8,128)}, f32[2,128,512]{2,1,0:T(8,128)}) custom-call(s32[2]{0:T(128)S(1)} %pad_add_fusion.refs_0_, bf16[512,640]{1,0:T(8,128)(2,1)S(1)} %pad_maximum_fusion.1.refs_1_, bf16[512,640]{1,0:T(8,128)(2,1)S(1)} %collective-permute-done.31.refs_2_), custom_call_target="tpu_custom_call" | custom-call | tf_op jit(solution)/shard_map/pallas_call | solution.py:271
  217.2 2.3 %add_convert_fusion = bf16[1024,256]{1,0:T(8,128)(2,1)} fusion(bf16[1024,256]{1,0:T(8,128)(2,1)} %refs_4_.3, f32[1024,256]{1,0:T(8,128)S(1)} %get-tuple-element.106, f32[1024,512]{1,0:T(8,128)S(1)} %get-tuple-element.107, f32[1024]{0:T(1024)S(1)} %bitcast.34, f32[1024]{0:T(1024)S(1)} %bitcast.33, f32[1024]{0:T(1024)S(1)} %add_rsqrt_fusion), kind=kLoop, calls=%fused_computation.26 | loop fusion | flops 2097152 | bytes 3158016 | tf_op jit(solution)/shard_map/convert_element_type | solution.py:467
  (135 shorter events, 8.8 us)
Async XLA Ops:
  0.6 7.6 %copy-start = (bf16[512,4,2,128]{3,2,1,0:T(2,128)(2,1)S(1)}, bf16[512,4,2,128]{3,2,1,0:T(2,128)(2,1)}, u32[]{:S(2)}) copy-start(bf16[512,4,2,128]{3,2,1,0:T(2,128)(2,1)} %param.7) | copy-start | bytes 3145732
  0.6 20.3 %collective-permute-start = (bf16[1024,256]{1,0:T(8,128)(2,1)}, bf16[1024,256]{1,0:T(8,128)(2,1)S(1)}, u32[]{:S(2)}, u32[]{:S(2)}) collective-permute-start(bf16[1024,256]{1,0:T(8,128)(2,1)} %refs_1_.1), channel_id=1, source_target_pairs={{0,1},{1,0},{2,3},{3,2},{4,5},{5,4},{6,7},{7,6},{8,9},{9,8},{10,11... | collective-permute-start | bytes 1572872 | tf_op jit(solution)/shard_map/ppermute | solution.py:20
  3.7 29.9 %collective-permute-start.1 = (bf16[1024,256]{1,0:T(8,128)(2,1)}, bf16[1024,256]{1,0:T(8,128)(2,1)S(1)}, u32[]{:S(2)}, u32[]{:S(2)}) collective-permute-start(bf16[1024,256]{1,0:T(8,128)(2,1)} %refs_1_.1), channel_id=1, source_target_pairs={{0,2},{2,0},{4,6},{6,4},{8,10},{10,8},{12,14},{14,12},{16,18},{18,... | collective-permute-start | bytes 1572872 | tf_op jit(solution)/shard_map/ppermute | solution.py:20
  3.7 15.6 %collective-permute-start.3 = (bf16[1024,256]{1,0:T(8,128)(2,1)}, bf16[1024,256]{1,0:T(8,128)(2,1)S(1)}, u32[]{:S(2)}, u32[]{:S(2)}) collective-permute-start(bf16[1024,256]{1,0:T(8,128)(2,1)} %refs_1_.1), channel_id=1, source_target_pairs={{0,8},{2,10},{4,12},{6,14},{8,16},{10,18},{12,20},{14,22},{16,24},... | collective-permute-start | bytes 1572872 | tf_op jit(solution)/shard_map/ppermute | solution.py:25
  13.7 5.6 %copy-start.5 = (bf16[1024,256]{1,0:T(8,128)(2,1)S(1)}, bf16[1024,256]{1,0:T(8,128)(2,1)}, u32[]{:S(2)}) copy-start(bf16[1024,256]{1,0:T(8,128)(2,1)} %refs_1_.1) | copy-start | bytes 1572868
  13.9 1.2 copy-start.36
  15.1 23.1 %copy-start.11 = (bf16[512,512]{1,0:T(8,128)(2,1)}, bf16[512,512]{1,0:T(8,128)(2,1)S(1)}, u32[]{:S(2)}) copy-start(bf16[512,512]{1,0:T(8,128)(2,1)S(1)} %maximum_select_fusion.refs_5_.refs_10_) | copy-start | bytes 1572868
  19.3 24.8 %copy-start.21 = (bf16[1024,256]{1,0:T(8,128)(2,1)}, bf16[1024,256]{1,0:T(8,128)(2,1)S(1)}, u32[]{:S(2)}) copy-start(bf16[1024,256]{1,0:T(8,128)(2,1)S(1)} %collective-permute-done.3.refs_1_) | copy-start | bytes 1572868
  19.4 13.6 %collective-permute-start.4 = (bf16[1024,256]{1,0:T(8,128)(2,1)S(1)}, bf16[1024,256]{1,0:T(8,128)(2,1)}, u32[]{:S(2)}, u32[]{:S(2)}) collective-permute-start(bf16[1024,256]{1,0:T(8,128)(2,1)S(1)} %broadcast_select_fusion), channel_id=1, source_target_pairs={{0,4},{2,6},{4,0},{6,2},{8,12},{10,14},{12,8},{14,10},{16,20},{18,... | collective-permute-start | bytes 1572872 | tf_op jit(solution)/shard_map/ppermute | solution.py:20
  21.0 37.4 %copy-start.13 = (bf16[1024,256]{1,0:T(8,128)(2,1)}, bf16[1024,256]{1,0:T(8,128)(2,1)S(1)}, u32[]{:S(2)}) copy-start(bf16[1024,256]{1,0:T(8,128)(2,1)S(1)} %collective-permute-done.refs_2_) | copy-start | bytes 1572868
  21.0 12.6 %collective-permute-start.2 = (bf16[1024,256]{1,0:T(8,128)(2,1)S(1)}, bf16[1024,256]{1,0:T(8,128)(2,1)S(1)}, u32[]{:S(2)}, u32[]{:S(2)}) collective-permute-start(bf16[1024,256]{1,0:T(8,128)(2,1)S(1)} %collective-permute-done.refs_2_), channel_id=1, source_target_pairs={{0,2},{2,0},{4,6},{6,4},{8,10},{10,8},{12,14},{14,12},{16,18},{18,... | collective-permute-start | bytes 1572872 | tf_op jit(solution)/shard_map/ppermute | solution.py:20
  21.0 23.2 %collective-permute-start.8 = (bf16[1024,256]{1,0:T(8,128)(2,1)S(1)}, bf16[1024,256]{1,0:T(8,128)(2,1)}, u32[]{:S(2)}, u32[]{:S(2)}) collective-permute-start(bf16[1024,256]{1,0:T(8,128)(2,1)S(1)} %collective-permute-done.3.refs_1_), channel_id=1, source_target_pairs={{0,1},{1,0},{2,3},{3,2},{4,5},{5,4},{6,7},{7,6},{8,9},{9,8},{10,11... | collective-permute-start | bytes 1572872 | tf_op jit(solution)/shard_map/ppermute | solution.py:20
  21.6 36.3 %collective-permute-start.11 = (bf16[1024,256]{1,0:T(8,128)(2,1)}, bf16[1024,256]{1,0:T(8,128)(2,1)}, u32[]{:S(2)}, u32[]{:S(2)}) collective-permute-start(bf16[1024,256]{1,0:T(8,128)(2,1)} %refs_4_.3), channel_id=1, source_target_pairs={{0,1},{1,0},{2,3},{3,2},{4,5},{5,4},{6,7},{7,6},{8,9},{9,8},{10,11... | collective-permute-start | bytes 1572872 | tf_op jit(solution)/shard_map/ppermute | solution.py:20
  33.0 24.9 %collective-permute-start.5 = (bf16[1024,256]{1,0:T(8,128)(2,1)}, bf16[1024,256]{1,0:T(8,128)(2,1)}, u32[]{:S(2)}, u32[]{:S(2)}) collective-permute-start(bf16[1024,256]{1,0:T(8,128)(2,1)} %collective-permute-done.4.refs_1_), channel_id=1, source_target_pairs={{0,1},{1,0},{2,3},{3,2},{4,5},{5,4},{6,7},{7,6},{8,9},{9,8},{10,11... | collective-permute-start | bytes 1572872 | tf_op jit(solution)/shard_map/ppermute | solution.py:20
  39.0 1.3 copy-start.7
  40.3 1.3 copy-start.9
  44.1 14.3 %collective-permute-start.9 = (bf16[1024,256]{1,0:T(8,128)(2,1)S(1)}, bf16[1024,256]{1,0:T(8,128)(2,1)S(1)}, u32[]{:S(2)}, u32[]{:S(2)}) collective-permute-start(bf16[1024,256]{1,0:T(8,128)(2,1)S(1)} %collective-permute-done.3.refs_1_), channel_id=1, source_target_pairs={{0,2},{2,0},{4,6},{6,4},{8,10},{10,8},{12,14},{14,12},{16,18},{18,... | collective-permute-start | bytes 1572872 | tf_op jit(solution)/shard_map/ppermute | solution.py:20
  44.1 26.1 %collective-permute-start.10 = (bf16[1024,256]{1,0:T(8,128)(2,1)}, bf16[1024,256]{1,0:T(8,128)(2,1)}, u32[]{:S(2)}, u32[]{:S(2)}) collective-permute-start(bf16[1024,256]{1,0:T(8,128)(2,1)} %collective-permute-done.8.refs_2_), channel_id=1, source_target_pairs={{0,2},{2,0},{4,6},{6,4},{8,10},{10,8},{12,14},{14,12},{16,18},{18,... | collective-permute-start | bytes 1572872 | tf_op jit(solution)/shard_map/ppermute | solution.py:20
  44.6 31.1 %collective-permute-start.6 = (bf16[1024,256]{1,0:T(8,128)(2,1)}, bf16[1024,256]{1,0:T(8,128)(2,1)}, u32[]{:S(2)}, u32[]{:S(2)}) collective-permute-start(bf16[1024,256]{1,0:T(8,128)(2,1)} %collective-permute-done.4.refs_1_), channel_id=1, source_target_pairs={{0,2},{2,0},{4,6},{6,4},{8,10},{10,8},{12,14},{14,12},{16,18},{18,... | collective-permute-start | bytes 1572872 | tf_op jit(solution)/shard_map/ppermute | solution.py:20
  57.9 17.8 %collective-permute-start.7 = (bf16[1024,256]{1,0:T(8,128)(2,1)}, bf16[1024,256]{1,0:T(8,128)(2,1)}, u32[]{:S(2)}, u32[]{:S(2)}) collective-permute-start(bf16[1024,256]{1,0:T(8,128)(2,1)} %collective-permute-done.5.refs_2_), channel_id=1, source_target_pairs={{0,2},{2,0},{4,6},{6,4},{8,10},{10,8},{12,14},{14,12},{16,18},{18,... | collective-permute-start | bytes 1572872 | tf_op jit(solution)/shard_map/ppermute | solution.py:20
  57.9 23.6 %collective-permute-start.12 = (bf16[1024,256]{1,0:T(8,128)(2,1)}, bf16[1024,256]{1,0:T(8,128)(2,1)}, u32[]{:S(2)}, u32[]{:S(2)}) collective-permute-start(bf16[1024,256]{1,0:T(8,128)(2,1)} %refs_4_.3), channel_id=1, source_target_pairs={{0,2},{2,0},{4,6},{6,4},{8,10},{10,8},{12,14},{14,12},{16,18},{18,... | collective-permute-start | bytes 1572872 | tf_op jit(solution)/shard_map/ppermute | solution.py:20
  59.2 22.3 %collective-permute-start.13 = (bf16[1024,256]{1,0:T(8,128)(2,1)}, bf16[1024,256]{1,0:T(8,128)(2,1)}, u32[]{:S(2)}, u32[]{:S(2)}) collective-permute-start(bf16[1024,256]{1,0:T(8,128)(2,1)} %collective-permute-done.11.refs_5_), channel_id=1, source_target_pairs={{0,2},{2,0},{4,6},{6,4},{8,10},{10,8},{12,14},{14,12},{16,18},{18,... | collective-permute-start | bytes 1572872 | tf_op jit(solution)/shard_map/ppermute | solution.py:20
  60.3 1.0 copy-start.3
  61.3 1.0 copy-start.16
  62.3 1.0 copy-start.19
  63.4 6.8 %copy-start.22 = (bf16[1024,256]{1,0:T(8,128)(2,1)S(1)}, bf16[1024,256]{1,0:T(8,128)(2,1)}, u32[]{:S(2)}) copy-start(bf16[1024,256]{1,0:T(8,128)(2,1)} %copy-done.21) | copy-start | bytes 1572868
  63.4 6.9 %copy-start.32 = (bf16[1024,256]{1,0:T(8,128)(2,1)S(1)}, bf16[1024,256]{1,0:T(8,128)(2,1)}, u32[]{:S(2)}) copy-start(bf16[1024,256]{1,0:T(8,128)(2,1)} %copy-done.31) | copy-start | bytes 1572868
  70.2 4.7 %copy-start.4 = (bf16[2048,128]{1,0:T(8,128)(2,1)S(1)}, bf16[2048,128]{1,0:T(8,128)(2,1)}, u32[]{:S(2)}) copy-start(bf16[2048,128]{1,0:T(8,128)(2,1)} %copy-done.2) | copy-start | bytes 1572868
  80.7 1.6 copy-start.10
  80.7 1.6 copy-start.23
  80.7 1.7 copy-start.30
  89.3 1.3 copy-start.28
  89.3 76.4 %collective-permute-start.18 = (bf16[1024,512]{1,0:T(8,128)(2,1)}, bf16[1024,512]{1,0:T(8,128)(2,1)}, u32[]{:S(2)}, u32[]{:S(2)}) collective-permute-start(bf16[1024,512]{1,0:T(8,128)(2,1)} %get-tuple-element.85), channel_id=1, source_target_pairs={{0,2},{2,0},{4,6},{6,4},{8,10},{10,8},{12,14},{14,12},{16,18},{18,... | collective-permute-start | bytes 3145736 | tf_op jit(solution)/shard_map/ppermute | solution.py:20
  90.6 3.7 %copy-start.12 = (bf16[512,512]{1,0:T(8,128)(2,1)S(1)}, bf16[512,512]{1,0:T(8,128)(2,1)}, u32[]{:S(2)}) copy-start(bf16[512,512]{1,0:T(8,128)(2,1)} %copy-done.11) | copy-start | bytes 1572868
  90.6 3.7 %copy-start.17 = (bf16[2048,128]{1,0:T(8,128)(2,1)S(1)}, bf16[2048,128]{1,0:T(8,128)(2,1)}, u32[]{:S(2)}) copy-start(bf16[2048,128]{1,0:T(8,128)(2,1)} %copy-done.15) | copy-start | bytes 1572868
  90.6 3.7 %copy-start.20 = (bf16[2048,128]{1,0:T(8,128)(2,1)S(1)}, bf16[2048,128]{1,0:T(8,128)(2,1)}, u32[]{:S(2)}) copy-start(bf16[2048,128]{1,0:T(8,128)(2,1)} %copy-done.18) | copy-start | bytes 1572868
  93.3 1.0 copy-start.26
  108.0 1.1 copy-start.24
  108.0 1.4 copy-start.35
  108.0 2.3 %copy-start.8 = (bf16[2048,512]{1,0:T(8,128)(2,1)S(1)}, bf16[2048,512]{1,0:T(8,128)(2,1)}, u32[]{:S(2)}) copy-start(bf16[2048,512]{1,0:T(8,128)(2,1)} %copy-done.7) | copy-start | bytes 6291460
  113.7 2.1 copy-start.33
  113.7 8.0 %copy-start.6 = (bf16[1024,256]{1,0:T(8,128)(2,1)S(1)}, bf16[1024,256]{1,0:T(8,128)(2,1)}, u32[]{:S(2)}) copy-start(bf16[1024,256]{1,0:T(8,128)(2,1)} %refs_1_.1) | copy-start | bytes 1572868
  113.7 8.0 %copy-start.14 = (bf16[1024,256]{1,0:T(8,128)(2,1)S(1)}, bf16[1024,256]{1,0:T(8,128)(2,1)}, u32[]{:S(2)}) copy-start(bf16[1024,256]{1,0:T(8,128)(2,1)} %copy-done.13) | copy-start | bytes 1572868
  115.9 14.0 %collective-permute-start.25 = (bf16[256,640]{1,0:T(8,128)(2,1)}, bf16[256,640]{1,0:T(8,128)(2,1)S(1)}, u32[]{:S(2)}, u32[]{:S(2)}) collective-permute-start(bf16[256,640]{1,0:T(8,128)(2,1)} %get-tuple-element.95), channel_id=1, source_target_pairs={{0,4},{2,6},{4,0},{6,2},{8,12},{10,14},{12,8},{14,10},{16,20},{18,... | collective-permute-start | bytes 983048 | tf_op jit(solution)/shard_map/ppermute | solution.py:20
  121.6 49.6 %collective-permute-start.21 = (bf16[1024,512]{1,0:T(8,128)(2,1)}, bf16[1024,512]{1,0:T(8,128)(2,1)}, u32[]{:S(2)}, u32[]{:S(2)}) collective-permute-start(bf16[1024,512]{1,0:T(8,128)(2,1)} %get-tuple-element.87), channel_id=1, source_target_pairs={{0,2},{2,0},{4,6},{6,4},{8,10},{10,8},{12,14},{14,12},{16,18},{18,... | collective-permute-start | bytes 3145736 | tf_op jit(solution)/shard_map/ppermute | solution.py:20
  130.0 33.0 %collective-permute-start.26 = (bf16[128,640]{1,0:T(8,128)(2,1)S(1)}, bf16[128,640]{1,0:T(8,128)(2,1)S(1)}, u32[]{:S(2)}, u32[]{:S(2)}) collective-permute-start(bf16[128,640]{1,0:T(8,128)(2,1)S(1)} %get-tuple-element.97), channel_id=1, source_target_pairs={{0,8},{2,10},{4,12},{6,14},{8,0},{10,2},{12,4},{14,6},{16,24},{18,... | collective-permute-start | bytes 491528 | tf_op jit(solution)/shard_map/ppermute | solution.py:20
  159.2 24.6 %collective-permute-start.16 = (bf16[1024,512]{1,0:T(8,128)(2,1)}, bf16[1024,512]{1,0:T(8,128)(2,1)S(1)}, u32[]{:S(2)}, u32[]{:S(2)}) collective-permute-start(bf16[1024,512]{1,0:T(8,128)(2,1)} %copy-done.35), channel_id=1, source_target_pairs={{0,2},{2,0},{4,6},{6,4},{8,10},{10,8},{12,14},{14,12},{16,18},{18,... | collective-permute-start | bytes 3145736 | tf_op jit(solution)/shard_map/ppermute | solution.py:20
  163.0 6.0 %collective-permute-start.27 = (bf16[64,640]{1,0:T(8,128)(2,1)S(1)}, bf16[64,640]{1,0:T(8,128)(2,1)S(1)}, u32[]{:S(2)}, u32[]{:S(2)}) collective-permute-start(bf16[64,640]{1,0:T(8,128)(2,1)S(1)} %get-tuple-element.99), channel_id=1, source_target_pairs={{0,16},{2,18},{4,20},{6,22},{8,24},{10,26},{12,28},{14,30},{16,0},... | collective-permute-start | bytes 245768 | tf_op jit(solution)/shard_map/ppermute | solution.py:20
  167.6 1.2 copy-start.34
  167.6 3.6 %copy-start.27 = (bf16[1024,512]{1,0:T(8,128)(2,1)S(1)}, bf16[1024,512]{1,0:T(8,128)(2,1)}, u32[]{:S(2)}) copy-start(bf16[1024,512]{1,0:T(8,128)(2,1)} %copy-done.26) | copy-start | bytes 3145732
  167.7 14.9 %collective-permute-start.19 = (bf16[1024,256]{1,0:T(8,128)(2,1)S(1)}, bf16[1024,256]{1,0:T(8,128)(2,1)S(1)}, u32[]{:S(2)}, u32[]{:S(2)}) collective-permute-start(bf16[1024,256]{1,0:T(8,128)(2,1)S(1)} %slice.145), channel_id=1, source_target_pairs={{0,1},{1,0},{2,3},{3,2},{4,5},{5,4},{6,7},{7,6},{8,9},{9,8},{10,11... | collective-permute-start | bytes 1572872 | tf_op jit(solution)/shard_map/ppermute | solution.py:20
  168.9 27.2 %collective-permute-start.14 = (bf16[1024,512]{1,0:T(8,128)(2,1)S(1)}, bf16[1024,512]{1,0:T(8,128)(2,1)S(1)}, u32[]{:S(2)}, u32[]{:S(2)}) collective-permute-start(bf16[1024,512]{1,0:T(8,128)(2,1)S(1)} %copy-done.34), channel_id=1, source_target_pairs={{0,2},{2,0},{4,6},{6,4},{8,10},{10,8},{12,14},{14,12},{16,18},{18,... | collective-permute-start | bytes 3145736 | tf_op jit(solution)/shard_map/ppermute | solution.py:20
  169.0 14.5 %collective-permute-start.28 = (bf16[64,640]{1,0:T(8,128)(2,1)S(1)}, bf16[64,640]{1,0:T(8,128)(2,1)S(1)}, u32[]{:S(2)}, u32[]{:S(2)}) collective-permute-start(bf16[64,640]{1,0:T(8,128)(2,1)S(1)} %shard_map.100), channel_id=1, source_target_pairs={{0,16},{2,18},{4,20},{6,22},{8,24},{10,26},{12,28},{14,30},{16,0},... | collective-permute-start | bytes 245768 | tf_op jit(solution)/shard_map/ppermute | solution.py:20
  172.8 11.1 %copy-start.25 = (bf16[1024,512]{1,0:T(8,128)(2,1)S(1)}, bf16[1024,512]{1,0:T(8,128)(2,1)}, u32[]{:S(2)}) copy-start(bf16[1024,512]{1,0:T(8,128)(2,1)} %copy-done.24) | copy-start | bytes 3145732
  172.8 21.0 %collective-permute-start.22 = (bf16[1024,256]{1,0:T(8,128)(2,1)S(1)}, bf16[1024,256]{1,0:T(8,128)(2,1)S(1)}, u32[]{:S(2)}, u32[]{:S(2)}) collective-permute-start(bf16[1024,256]{1,0:T(8,128)(2,1)S(1)} %slice.144), channel_id=1, source_target_pairs={{0,1},{1,0},{2,3},{3,2},{4,5},{5,4},{6,7},{7,6},{8,9},{9,8},{10,11... | collective-permute-start | bytes 1572872 | tf_op jit(solution)/shard_map/ppermute | solution.py:20
  182.8 11.0 %collective-permute-start.20 = (bf16[1024,256]{1,0:T(8,128)(2,1)S(1)}, bf16[1024,256]{1,0:T(8,128)(2,1)S(1)}, u32[]{:S(2)}, u32[]{:S(2)}) collective-permute-start(bf16[1024,256]{1,0:T(8,128)(2,1)S(1)} %fusion.4), channel_id=1, source_target_pairs={{0,4},{2,6},{4,0},{6,2},{8,12},{10,14},{12,8},{14,10},{16,20},{18,... | collective-permute-start | bytes 1572872 | tf_op jit(solution)/shard_map/ppermute | solution.py:20
  183.5 11.9 %collective-permute-start.29 = (bf16[128,640]{1,0:T(8,128)(2,1)S(1)}, bf16[128,640]{1,0:T(8,128)(2,1)S(1)}, u32[]{:S(2)}, u32[]{:S(2)}) collective-permute-start(bf16[128,640]{1,0:T(8,128)(2,1)S(1)} %pad_maximum_fusion.4), channel_id=1, source_target_pairs={{0,8},{2,10},{4,12},{6,14},{8,0},{10,2},{12,4},{14,6},{16,24},{18,... | collective-permute-start | bytes 491528 | tf_op jit(solution)/shard_map/ppermute | solution.py:20
  184.2 20.8 %collective-permute-start.17 = (bf16[1024,256]{1,0:T(8,128)(2,1)S(1)}, bf16[1024,256]{1,0:T(8,128)(2,1)S(1)}, u32[]{:S(2)}, u32[]{:S(2)}) collective-permute-start(bf16[1024,256]{1,0:T(8,128)(2,1)S(1)} %slice.146), channel_id=1, source_target_pairs={{0,1},{1,0},{2,3},{3,2},{4,5},{5,4},{6,7},{7,6},{8,9},{9,8},{10,11... | collective-permute-start | bytes 1572872 | tf_op jit(solution)/shard_map/ppermute | solution.py:20
  194.1 11.1 %collective-permute-start.23 = (bf16[1024,256]{1,0:T(8,128)(2,1)S(1)}, bf16[1024,256]{1,0:T(8,128)(2,1)S(1)}, u32[]{:S(2)}, u32[]{:S(2)}) collective-permute-start(bf16[1024,256]{1,0:T(8,128)(2,1)S(1)} %fusion.3), channel_id=1, source_target_pairs={{8,0},{10,2},{12,4},{14,6},{16,8},{18,10},{20,12},{22,14},{24,16},... | collective-permute-start | bytes 1572872 | tf_op jit(solution)/shard_map/ppermute | solution.py:25
  195.4 7.1 %collective-permute-start.30 = (bf16[256,640]{1,0:T(8,128)(2,1)S(1)}, bf16[256,640]{1,0:T(8,128)(2,1)S(1)}, u32[]{:S(2)}, u32[]{:S(2)}) collective-permute-start(bf16[256,640]{1,0:T(8,128)(2,1)S(1)} %pad_maximum_fusion.2), channel_id=1, source_target_pairs={{0,4},{2,6},{4,0},{6,2},{8,12},{10,14},{12,8},{14,10},{16,20},{18,... | collective-permute-start | bytes 983048 | tf_op jit(solution)/shard_map/ppermute | solution.py:20
  196.4 17.2 %collective-permute-start.15 = (bf16[1024,256]{1,0:T(8,128)(2,1)S(1)}, bf16[1024,256]{1,0:T(8,128)(2,1)S(1)}, u32[]{:S(2)}, u32[]{:S(2)}) collective-permute-start(bf16[1024,256]{1,0:T(8,128)(2,1)S(1)} %slice.147), channel_id=1, source_target_pairs={{0,1},{1,0},{2,3},{3,2},{4,5},{5,4},{6,7},{7,6},{8,9},{9,8},{10,11... | collective-permute-start | bytes 1572872 | tf_op jit(solution)/shard_map/ppermute | solution.py:20
  202.6 12.1 %collective-permute-start.31 = (bf16[512,640]{1,0:T(8,128)(2,1)S(1)}, bf16[512,640]{1,0:T(8,128)(2,1)S(1)}, u32[]{:S(2)}, u32[]{:S(2)}) collective-permute-start(bf16[512,640]{1,0:T(8,128)(2,1)S(1)} %pad_maximum_fusion.1.refs_1_), channel_id=1, source_target_pairs={{0,2},{2,0},{4,6},{6,4},{8,10},{10,8},{12,14},{14,12},{16,18},{18,... | collective-permute-start | bytes 1966088 | tf_op jit(solution)/shard_map/ppermute | solution.py:20
  205.9 11.3 %collective-permute-start.24 = (f32[2,1024]{1,0:T(2,128)S(1)}, f32[2,1024]{1,0:T(2,128)S(1)}, u32[]{:S(2)}, u32[]{:S(2)}) collective-permute-start(f32[2,1024]{1,0:T(2,128)S(1)} %pad_maximum_fusion.5), channel_id=1, source_target_pairs={{0,1},{1,0},{2,3},{3,2},{4,5},{5,4},{6,7},{7,6},{8,9},{9,8},{10,11... | collective-permute-start | bytes 24584 | tf_op jit(solution)/shard_map/ppermute | solution.py:20
  213.6 5.9 %copy-start.1 = (bf16[512,4,2,128]{3,2,1,0:T(2,128)(2,1)S(1)}, bf16[512,4,2,128]{3,2,1,0:T(2,128)(2,1)}, u32[]{:S(2)}) copy-start(bf16[512,4,2,128]{3,2,1,0:T(2,128)(2,1)} %param.7) | copy-start | bytes 3145732
  (5 other events, 4.1 us)

commit v3 on v2

--- a/solution.py
+++ b/solution.py
@@ -49,6 +49,12 @@
 
 def gate_of(inputs):
     return 0.5 + 0.5 * jnp.tanh(0.5 * inputs)
+
+
+def column_of(row):
+    count = row.shape[1]
+    turned = jnp.broadcast_to(row, (128, count)).T
+    return jnp.concatenate([turned] * (count // 128), axis=1)
 
 
 def aligned(start, size):
@@ -139,7 +145,7 @@
     lax.fori_loop(0, q_tiles, query_tile, 0)
 
 
-def forward_kernel(low_ref, first_ref, last_ref, q_ref, k_ref, v_ref, col_ref, row_ref, *rest, block_off, query_off, scale):
+def forward_kernel(low_ref, first_ref, last_ref, q_ref, k_ref, v_ref, row_ref, *rest, block_off, query_off, scale):
     out_ref = rest[-1]
     if len(rest) == 2:
         out_ref[...] = rest[0][...]
@@ -152,7 +158,7 @@
         if reach is not None:
             pos_q = lax.broadcasted_iota(jnp.int32, (TILE, TILE), 0)
             pos_k = lax.broadcasted_iota(jnp.int32, (TILE, TILE), 1)
-            id_q = col_ref[aligned((query_off + i) * TILE, TILE), :]
+            id_q = column_of(row_ref[:, aligned((query_off + i) * TILE, TILE)])
             id_k = row_ref[:, aligned((block_off + j) * TILE, TILE)]
             half = jnp.where((id_q == id_k) & (pos_k - pos_q <= reach), half, 0.0)
         weights = half + half * jnp.tanh(half)
@@ -163,7 +169,7 @@
     )
 
 
-def backward_kernel(low_ref, first_ref, last_ref, core_ref, q_ref, g_ref, k_ref, v_ref, col_ref, row_ref, w_ref, slope_ref, *rest, block_off, query_off, scale):
+def backward_kernel(low_ref, first_ref, last_ref, core_ref, q_ref, g_ref, k_ref, v_ref, row_ref, w_ref, slope_ref, *rest, block_off, query_off, scale):
     own = block_off == query_off
     *before, send_ref, keep_ref, grads_ref, dq_ref, dk_ref, dv_ref = rest
     width = k_ref.shape[1]
@@ -184,7 +190,7 @@
         if reach is not None:
             pos_k = lax.broadcasted_iota(jnp.int32, (TILE, TILE), 0)
             pos_q = lax.broadcasted_iota(jnp.int32, (TILE, TILE), 1)
-            id_k = col_ref[aligned((block_off + j) * TILE, TILE), :]
+            id_k = column_of(row_ref[:, aligned((block_off + j) * TILE, TILE)])
             id_q = row_ref[:, aligned((query_off + i) * TILE, TILE)]
             ok = (id_k == id_q) & (pos_k - pos_q <= reach)
             half = jnp.where(ok, half, 0.0)
@@ -225,14 +231,14 @@
     rest[-1][...] = grads if len(rest) == 1 else grads + rest[0][...]
 
 
-def weight_own_kernel(side_ref, normed_ref, grads_ref, early_ref, kv_ref, send_ref, keep_ref, sum_ref):
+def weight_own_kernel(table_ref, normed_ref, grads_ref, early_ref, kv_ref, send_ref, keep_ref, sum_ref):
     width = kv_ref.shape[1] // 2
     sum_ref[:, width : 4 * width] = dot(normed_ref[...], grads_ref[:, width:], TN)
     sum_ref[:, width : 2 * width] += kv_ref[:, :width]
     sum_ref[:, 3 * width : 4 * width] += kv_ref[:, width:]
     sum_ref[:, :width] = early_ref[:, :width]
     sum_ref[:, 4 * width :] = early_ref[:, width:]
-    side = side_ref[0]
+    side = table_ref[2]
     size = send_ref.shape[0]
     send_ref[...] = sum_ref[aligned((1 - side) * size, size), :].astype(bf16)
     keep_ref[...] = sum_ref[aligned(side * size, size), :]
@@ -242,8 +248,8 @@
     out_ref[...] = (kept_ref[...] + received_ref[...].astype(f32)).astype(bf16)
 
 
-def halve_kernel(side_ref, kept_ref, received_ref, send_ref, keep_ref):
-    side = side_ref[0]
+def halve_kernel(table_ref, kept_ref, received_ref, send_ref, keep_ref, *, step):
+    side = table_ref[2 + step]
     size = send_ref.shape[0]
     other, mine = aligned((1 - side) * size, size), aligned(side * size, size)
     send_ref[...] = (kept_ref[other, :] + received_ref[other, :].astype(f32)).astype(bf16)
@@ -283,9 +289,9 @@
     row_count, half_width = tokens.shape
     seq_count = lax.axis_size("seq")
     device_pos = lax.axis_index("seq")
-    core = device_pos % 2
-    pair = device_pos // 2
-    odd = pair % 2 == 1
+    core = device_pos & 1
+    pair = device_pos >> 1
+    odd = (device_pos & 2) != 0
     block = 2 * row_count
     width = 2 * half_width
     head_size = weight_out.shape[1]
@@ -293,12 +299,20 @@
     if (MAXLEN - 2 + block) // block != 2:
         raise ValueError("reach")
     tiles = block // TILE
-    core_table = core.astype(jnp.int32).reshape(1)
+
+    bits = []
+    while 2 << len(bits) < seq_count:
+        bits.append(2 << len(bits))
+    steps = len(bits)
+    block_place = lax.axis_index("col") << (steps - 1)
+    for i in range(steps):
+        block_place = block_place ^ (((device_pos >> (i + 1)) & 1) << (steps - 1 - i))
+    table = jnp.stack([core, block_place] + [(device_pos >> (i + 1)) & 1 for i in range(steps)]).astype(jnp.int32)
 
     def over(array, axis, bit):
         return swap(array, axis, bit)
 
-    flip = lax.axis_index("col") == 1
+    flip = lax.axis_index("col") != 0
     w_in = lax.dynamic_index_in_dim(weight_in, core, 2, keepdims=False).reshape(width, 4 * head_size)
     w_in = jnp.where(flip, jnp.roll(w_in, half_width, axis=0), w_in)
     w_out = lax.dynamic_index_in_dim(weight_out, core, 0, keepdims=False)
@@ -311,12 +325,12 @@
     first, last = by_tile[:, 0], by_tile[:, -1]
     low = jnp.sum((last[None, :] < first[2 * tiles :, None]).astype(jnp.int32), axis=1)
     tables = (low, first, last)
-    id_col, id_row = ids[:, None], ids[None, :]
+    id_row = ids[None, :]
 
     far = shift(tokens, "seq", 4)
     own_other = over(tokens, "col", 1)
-    own_other, w_in, w_kv, w_out, id_col, id_row, tables = lax.optimization_barrier(
-        (own_other, w_in, w_kv, w_out, id_col, id_row, tables)
+    own_other, w_in, w_kv, w_out, id_row, tables, table, odd = lax.optimization_barrier(
+        (own_other, w_in, w_kv, w_out, id_row, tables, table, odd)
     )
     own_set = (tokens, own_other, over(tokens, "seq", 1), over(own_other, "seq", 1))
 
@@ -326,7 +340,7 @@
     def project(token_set, weights):
         count = weights.shape[1] // head_size
         outs = (shape(block, width), shape(block, count * head_size)) + (shape(block, head_size),) * count
-        return vmem_call(project_kernel, (core_table,), (*token_set, weights), outs)
+        return vmem_call(project_kernel, (table,), (*token_set, weights), outs)
 
     normed_own, slope_own, up_part, value_own, query, key_own = project(own_set, w_in)
     near = over(jnp.where(odd, far, tokens), "seq", 2)
@@ -343,7 +357,7 @@
     values = [value_far, value_near, value_own]
 
     def forward(which, before):
-        arrays = [query, keys[which], values[which], id_col, id_row]
+        arrays = [query, keys[which], values[which], id_row]
         aliases = {}
         if before is not None:
             aliases = {3 + len(arrays): 0}
@@ -365,13 +379,13 @@
 
     grad_narrow, gated, pre_up = vmem_call(
         middle_kernel,
-        (core_table,),
+        (table,),
         (attended, up_part, slope_own, *cot_set, w_out),
         (shape(block, head_size),) * 3,
     )
     out_send, out_keep, grad_early = vmem_call(
         outer_kernel,
-        (core_table,),
+        (table,),
         (gated, pre_up, normed_own, *cot_set, w_out),
         (shape(row_count, width), shape(row_count, width), shape(width, 2 * head_size, f32)),
     )
@@ -381,7 +395,7 @@
         return keep[:, :half_width] + over(keep[:, half_width:].astype(bf16), "col", 1).astype(f32)
 
     def backward(which, weights, slope, before):
-        arrays = [query, grad_narrow, keys[which], values[which], id_col, id_row, weights, slope, *before]
+        arrays = [query, grad_narrow, keys[which], values[which], id_row, weights, slope, *before]
         outs = (
             shape(row_count, width),
             shape(row_count, width),
@@ -390,10 +404,10 @@
         )
         return vmem_call(
             backward_kernel,
-            (*tables, core_table),
+            (*tables, table),
             arrays,
             outs,
-            {4 + 8: 3} if before else None,
+            {4 + 7: 3} if before else None,
             scratch=[pltpu.VMEM((block, head_size), f32)] * 2,
             block_off=which * tiles,
             query_off=2 * tiles,
@@ -414,15 +428,11 @@
     grad_normed = own_part + jnp.where(odd, 0.0, near_back) + far_back
     out = (tokens.astype(f32) + over_heads(out_send, out_keep)).astype(bf16)
 
-    bits = []
-    while 2 << len(bits) < seq_count:
-        bits.append(2 << len(bits))
-    sides = [((device_pos // bit) % 2).astype(jnp.int32) for bit in bits]
     lanes = 5 * head_size
     size = half_width
     sent, kept = vmem_call(
         weight_own_kernel,
-        (sides[0].reshape(1),),
+        (table,),
         (normed_own, own_grads, grad_early, grad_kv),
         (shape(size, lanes), shape(size, lanes, f32)),
         scratch=[pltpu.VMEM((width, lanes), f32)],
@@ -433,28 +443,24 @@
             size = size // 2
             sent, kept = vmem_call(
                 halve_kernel,
-                (sides[i + 1].reshape(1),),
+                (table,),
                 (kept, received),
                 (shape(size, lanes), shape(size, lanes, f32)),
+                step=i + 1,
             )
         else:
             total = vmem_call(last_kernel, (), (kept, received), shape(size, lanes))
     for i, bit in reversed(list(enumerate(bits))):
         total = jnp.concatenate([total, over(total, "seq", bit)], axis=0)
 
-    blocks = 1 << len(bits)
-    block_place = lax.axis_index("col") * (blocks // 2)
-    for i, side in enumerate(sides):
-        block_place = block_place ^ (side << (len(bits) - 1 - i))
-    place = jnp.stack([core, block_place]).astype(jnp.int32)
     grad_weight_in, grad_weight_out = vmem_call(
         assemble_kernel,
-        (place,),
+        (table,),
         (total, over(total, "seq", 1)),
         (shape(8 * width, head_size, f32), jax.ShapeDtypeStruct((2, head_size, width), f32)),
         scratch=[pltpu.VMEM((width, head_size), f32)],
         scale=1.0 / math.sqrt(row_count * seq_count),
-        blocks=blocks,
+        blocks=1 << steps,
     )
     grad_weight_in = grad_weight_in.reshape(width, 4, 2, head_size)
 

time: 220 us -> 204 us (0.927)
  local copies, waits for them, and re-layouts: 21.5 us -> 5.74 us
  waiting for transfers between devices: 70.5 us -> 76 us
  other arithmetic: 12.5 us -> 8.02 us
  Pallas kernels: 55.4 us -> 52 us
  starting transfers between devices: 58.4 us -> 60.8 us
    unnamed x75 -> x11, local copies, waits for them, and re-layouts: 15.8 us -> 1.35 us
    ppermute x30, waiting for transfers between devices: 68.1 us -> 73.4 us  [swap(): lax.ppermute(block, axis, [(i, i ^ bit) for i in range(lax.axis_size(axis...]
    pallas_call x18, Pallas kernels: 55.4 us -> 52 us  [vmem_call(): pl.pallas_call(lambda *refs: kernel(*refs, **static), out_shape=outs, in_...]
    add x4, other arithmetic: 4.02 us -> 1.25 us  [over_heads(): keep = keep.astype(f32) + over(send, 'seq', 1).astype(f32)]
    ppermute x30, starting transfers between devices: 53.6 us -> 56.1 us  [swap(): lax.ppermute(block, axis, [(i, i ^ bit) for i in range(lax.axis_size(axis...]
  transfers between devices with their start and end apart: 32 -> 32, of which waited for: 11 -> 13; matrix products, arithmetic and copies ran while one was open for 8% -> 6% of each run, Pallas kernels for 22% -> 23%
where the time goes in v3:
time: 204 us
  waiting for transfers between devices  76 us (37%)
  starting transfers between devices  60.8 us (30%)
  Pallas kernels  52 us (25%)
  other arithmetic  8.02 us (4%)
  local copies, waits for them, and re-layouts  5.74 us (3%)
    ppermute x30, waiting for transfers between devices, swap(): lax.ppermute(block, axis, [(i, i ^ bit) for i in range(lax.axis_size(axis...  73.4 us
    ppermute x30, starting transfers between devices, swap(): lax.ppermute(block, axis, [(i, i ^ bit) for i in range(lax.axis_size(axis...  56.1 us
    pallas_call x18, Pallas kernels, vmem_call(): pl.pallas_call(lambda *refs: kernel(*refs, **static), out_shape=outs, in_...  52 us
    ppermute x2, starting transfers between devices, shift(): lax.ppermute(block, axis, [(i, i + distance) for i in devices if i + dist...  4.8 us
  transfers between devices with their start and end apart: 32, of which 13 were waited for; matrix products, arithmetic and copies ran while one was open for 6% of the time, Pallas kernels for 23%

profile of v3, /device:TPU:0, one launch (start us, length us, event | category | flops | bytes accessed | tf_op | source)
XLA Modules:
  0.0 203.6 jit_solution(3321572236631893039)
XLA Ops:
  0.6 3.0 %collective-permute-start = (bf16[1024,256]{1,0:T(8,128)(2,1)}, bf16[1024,256]{1,0:T(8,128)(2,1)S(1)}, u32[]{:S(2)}, u32[]{:S(2)}) collective-permute-start(bf16[1024,256]{1,0:T(8,128)(2,1)} %refs_1_.1), channel_id=1, source_target_pairs={{0,1},{1,0},{2,3},{3,2},{4,5},{5,4},{6,7},{7,6},{8,9},{9,8},{10,11... | collective-permute-start | bytes 1572872 | tf_op jit(solution)/shard_map/ppermute | solution.py:20
  3.7 3.5 %collective-permute-start.3 = (bf16[1024,256]{1,0:T(8,128)(2,1)}, bf16[1024,256]{1,0:T(8,128)(2,1)S(1)}, u32[]{:S(2)}, u32[]{:S(2)}) collective-permute-start(bf16[1024,256]{1,0:T(8,128)(2,1)} %refs_1_.1), channel_id=1, source_target_pairs={{0,8},{2,10},{4,12},{6,14},{8,16},{10,18},{12,20},{14,22},{16,24},... | collective-permute-start | bytes 1572872 | tf_op jit(solution)/shard_map/ppermute | solution.py:25
  7.2 0.7 pad_dynamic-slice_fusion
  8.2 1.1 constant_dynamic-slice_fusion
  9.3 1.3 copy.25
  10.8 0.8 copy.23
  11.9 0.6 fusion.11
  12.6 1.1 maximum_select_fusion.refs_5_.refs_9_
  14.0 1.0 maximum_select_fusion.1.refs_8_
  15.1 0.8 collective-permute-done.refs_2_
  15.8 2.5 %collective-permute-done.3.refs_1_ = bf16[1024,256]{1,0:T(8,128)(2,1)S(1)} collective-permute-done((bf16[1024,256]{1,0:T(8,128)(2,1)}, bf16[1024,256]{1,0:T(8,128)(2,1)S(1)}, u32[]{:S(2)}, u32[]{:S(2)}) %collective-permute-start.3) | collective-permute-done | bytes 524320 | tf_op jit(solution)/shard_map/ppermute | solution.py:25
  18.4 1.6 collective-permute-start.4
  20.0 0.5 collective-permute-start.2
  20.5 0.5 collective-permute-start.8
  21.1 1.5 collective-permute-start.11
  22.5 8.5 %collective-permute-done.4.refs_1_ = bf16[1024,256]{1,0:T(8,128)(2,1)S(1)} collective-permute-done((bf16[1024,256]{1,0:T(8,128)(2,1)S(1)}, bf16[1024,256]{1,0:T(8,128)(2,1)S(1)}, u32[]{:S(2)}, u32[]{:S(2)}) %collective-permute-start.4) | collective-permute-done | bytes 524320 | tf_op jit(solution)/shard_map/ppermute | solution.py:20
  31.0 0.5 collective-permute-start.5
  31.6 5.1 %shard_map.84 = (bf16[2048,512]{1,0:T(8,128)(2,1)S(1)}, bf16[2048,512]{1,0:T(8,128)(2,1)S(1)}, bf16[2048,128]{1,0:T(8,128)(2,1)S(1)}, bf16[2048,128]{1,0:T(8,128...) custom-call(s32[5]{0:T(128)S(1)} %stack.32.refs_0_.refs_3_, bf16[1024,256]{1,0:T(8,128)(2,1)S(1)} %copy-done.2, ...), custom_call_target="tpu_custom_call" | custom-call | tf_op jit(solution)/shard_map/pallas_call | solution.py:277
  36.8 0.5 collective-permute-start.10
  37.4 19.4 %collective-permute-done.5.refs_2_ = bf16[1024,256]{1,0:T(8,128)(2,1)S(1)} collective-permute-done((bf16[1024,256]{1,0:T(8,128)(2,1)S(1)}, bf16[1024,256]{1,0:T(8,128)(2,1)S(1)}, u32[]{:S(2)}, u32[]{:S(2)}) %collective-permute-start.5) | collective-permute-done | bytes 524320 | tf_op jit(solution)/shard_map/ppermute | solution.py:20
  56.8 0.5 collective-permute-start.12
  57.4 6.9 %shard_map.87.refs_7_ = f32[2048,128]{1,0:T(8,128)S(1)} custom-call(s32[4]{0:T(128)S(1)} %convert_reduce_fusion.1.refs_0_, s32[12]{0:T(128)S(1)} %get-tuple-element.56.refs_1_, s32[12]{0:T(128)S(1)} %get-tuple-element.57.refs_2_, bf16[2048,128]{1,0:T(8,128)(2,1)S(1)} %get-tuple-element.60.refs_3_.refs_4_, ...), custom_call_target="tpu_custom_call" | custom-call | tf_op jit(solution)/shard_map/pallas_call | solution.py:277
  64.3 4.0 %shard_map.86 = (bf16[2048,512]{1,0:T(8,128)(2,1)S(1)}, bf16[2048,256]{1,0:T(8,128)(2,1)S(1)}, bf16[2048,128]{1,0:T(8,128)(2,1)S(1)}, bf16[2048,128]{1,0:T(8,128)(2,1)S(1)}) custom-call(s32[5]{0:T(128)S(1)} %stack.32.refs_0_.refs_3_, bf16[1024,256]{1,0:T(8,128)(2,1)S(1)} %collective-permute-done.3.refs_1_, ...), custom_call_target="tpu_custom_call" | custom-call | tf_op jit(solution)/shard_map/pallas_call | solution.py:277
  68.3 0.7 shard_map.88.refs_7_
  69.0 4.0 %shard_map.85 = (bf16[2048,512]{1,0:T(8,128)(2,1)S(1)}, bf16[2048,256]{1,0:T(8,128)(2,1)S(1)}, bf16[2048,128]{1,0:T(8,128)(2,1)S(1)}, bf16[2048,128]{1,0:T(8,128)(2,1)S(1)}) custom-call(s32[5]{0:T(128)S(1)} %stack.32.refs_0_.refs_3_, bf16[1024,256]{1,0:T(8,128)(2,1)S(1)} %collective-permute-done.4.refs_1_, ...), custom_call_target="tpu_custom_call" | custom-call | tf_op jit(solution)/shard_map/pallas_call | solution.py:277
  73.0 0.8 shard_map.89.refs_1_
  73.8 3.3 %shard_map.90 = (bf16[2048,128]{1,0:T(8,128)(2,1)S(1)}, bf16[2048,128]{1,0:T(8,128)(2,1)S(1)}, bf16[2048,128]{1,0:T(8,128)(2,1)S(1)}) custom-call(s32[5]{0:T(128)S(1)} %stack.32.refs_0_.refs_3_, f32[2048,128]{1,0:T(8,128)S(1)} %shard_map.89.refs_1_, bf16[2048,128]{1,0:T(8,128)(2,1)S(1)} %get-tuple-element.71.refs_2_, ...), custom_call_target="tpu_custom_call" | custom-call | tf_op jit(solution)/shard_map/pallas_call | solution.py:277
  77.1 2.1 %shard_map.92 = (bf16[1024,512]{1,0:T(8,128)(2,1)S(1)}, bf16[1024,512]{1,0:T(8,128)(2,1)S(1)}, bf16[2048,256]{1,0:T(8,128)(2,1)S(1)}, f32[2048,128]{1,0:T(8,128)S(1)}) custom-call(s32[4]{0:T(128)S(1)} %convert_reduce_fusion.1.refs_0_, s32[12]{0:T(128)S(1)} %get-tuple-element.56.refs_1_, s32[12]{0:T(128)S(1)} %get-tuple-element.57.refs_2_, ...), custom_call_target="tpu_custom_call" | custom-call | tf_op jit(solution)/shard_map/pallas_call | solution.py:277
  79.2 0.5 collective-permute-start.18
  79.7 0.8 shard_map.95.refs_2_
  80.4 1.9 shard_map.93
  82.4 13.7 %shard_map.94 = (bf16[1024,512]{1,0:T(8,128)(2,1)S(1)}, bf16[1024,512]{1,0:T(8,128)(2,1)S(1)}, bf16[2048,512]{1,0:T(8,128)(2,1)S(1)}, f32[2048,128]{1,0:T(8,128)S(1)}) custom-call(s32[4]{0:T(128)S(1)} %convert_reduce_fusion.1.refs_0_, s32[12]{0:T(128)S(1)} %get-tuple-element.56.refs_1_, ...), custom_call_target="tpu_custom_call", output_to_operand_aliasing={{3}: (11, {})} | custom-call | tf_op jit(solution)/shard_map/pallas_call | solution.py:277
  96.1 0.7 shard_map.96.refs_4_
  96.9 2.3 %shard_map.91 = (bf16[1024,512]{1,0:T(8,128)(2,1)S(1)}, bf16[1024,512]{1,0:T(8,128)(2,1)S(1)}, f32[512,256]{1,0:T(8,128)S(1)}) custom-call(s32[5]{0:T(128)S(1)} %stack.32.refs_0_.refs_3_, bf16[2048,128]{1,0:T(8,128)(2,1)S(1)} %get-tuple-element.74.refs_1_, bf16[2048,128]{1,0:T(8,128)(2,1)S(1)} %get-tuple-element.75.refs_2_.refs_12_, ...), custom_call_target="tpu_custom_call" | custom-call | tf_op jit(solution)/shard_map/pallas_call | solution.py:277
  99.2 1.9 shard_map.97
  101.2 6.8 %collective-permute-start.25 = (bf16[256,640]{1,0:T(8,128)(2,1)S(1)}, bf16[256,640]{1,0:T(8,128)(2,1)S(1)}, u32[]{:S(2)}, u32[]{:S(2)}) collective-permute-start(bf16[256,640]{1,0:T(8,128)(2,1)S(1)} %get-tuple-element.97), channel_id=1, source_target_pairs={{0,4},{2,6},{4,0},{6,2},{8,12},{10,14},{12,8},{14,10},{16,20},{18,... | collective-permute-start | bytes 983048 | tf_op jit(solution)/shard_map/ppermute | solution.py:20
  108.1 7.7 %collective-permute-done.25.refs_2_ = bf16[256,640]{1,0:T(8,128)(2,1)S(1)} collective-permute-done((bf16[256,640]{1,0:T(8,128)(2,1)S(1)}, bf16[256,640]{1,0:T(8,128)(2,1)S(1)}, u32[]{:S(2)}, u32[]{:S(2)}) %collective-permute-start.25) | collective-permute-done | bytes 327712 | tf_op jit(solution)/shard_map/ppermute | solution.py:20
  115.8 0.6 shard_map.98
  116.5 29.5 %collective-permute-start.26 = (bf16[128,640]{1,0:T(8,128)(2,1)S(1)}, bf16[128,640]{1,0:T(8,128)(2,1)S(1)}, u32[]{:S(2)}, u32[]{:S(2)}) collective-permute-start(bf16[128,640]{1,0:T(8,128)(2,1)S(1)} %get-tuple-element.99), channel_id=1, source_target_pairs={{0,8},{2,10},{4,12},{6,14},{8,0},{10,2},{12,4},{14,6},{16,24},{18,... | collective-permute-start | bytes 491528 | tf_op jit(solution)/shard_map/ppermute | solution.py:20
  145.9 3.6 %collective-permute-done.26.refs_2_ = bf16[128,640]{1,0:T(8,128)(2,1)S(1)} collective-permute-done((bf16[128,640]{1,0:T(8,128)(2,1)S(1)}, bf16[128,640]{1,0:T(8,128)(2,1)S(1)}, u32[]{:S(2)}, u32[]{:S(2)}) %collective-permute-start.26) | collective-permute-done | bytes 163872 | tf_op jit(solution)/shard_map/ppermute | solution.py:20
  149.5 0.6 shard_map.99
  150.1 2.8 %collective-permute-start.27 = (bf16[64,640]{1,0:T(8,128)(2,1)S(1)}, bf16[64,640]{1,0:T(8,128)(2,1)S(1)}, u32[]{:S(2)}, u32[]{:S(2)}) collective-permute-start(bf16[64,640]{1,0:T(8,128)(2,1)S(1)} %get-tuple-element.101), channel_id=1, source_target_pairs={{0,16},{2,18},{4,20},{6,22},{8,24},{10,26},{12,28},{14,30},{16,0},... | collective-permute-start | bytes 245768 | tf_op jit(solution)/shard_map/ppermute | solution.py:20
  153.3 0.6 collective-permute-start.19
  153.9 0.5 convert_subtract_fusion
  154.5 1.0 collective-permute-done.27.refs_1_
  155.5 2.8 %collective-permute-start.28 = (bf16[64,640]{1,0:T(8,128)(2,1)S(1)}, bf16[64,640]{1,0:T(8,128)(2,1)S(1)}, u32[]{:S(2)}, u32[]{:S(2)}) collective-permute-start(bf16[64,640]{1,0:T(8,128)(2,1)S(1)} %shard_map.100), channel_id=1, source_target_pairs={{0,16},{2,18},{4,20},{6,22},{8,24},{10,26},{12,28},{14,30},{16,0},... | collective-permute-start | bytes 245768 | tf_op jit(solution)/shard_map/ppermute | solution.py:20
  158.7 0.6 collective-permute-start.22
  159.3 8.8 %collective-permute-done.19 = bf16[1024,256]{1,0:T(8,128)(2,1)S(1)} collective-permute-done((bf16[1024,256]{1,0:T(8,128)(2,1)S(1)}, bf16[1024,256]{1,0:T(8,128)(2,1)S(1)}, u32[]{:S(2)}, u32[]{:S(2)}) %collective-permute-start.19) | collective-permute-done | bytes 524320 | tf_op jit(solution)/shard_map/ppermute | solution.py:20
  168.4 0.6 collective-permute-start.20
  169.0 0.4 collective-permute-start.29
  169.8 0.6 collective-permute-start.17
  170.4 9.0 %collective-permute-done.22 = bf16[1024,256]{1,0:T(8,128)(2,1)S(1)} collective-permute-done((bf16[1024,256]{1,0:T(8,128)(2,1)S(1)}, bf16[1024,256]{1,0:T(8,128)(2,1)S(1)}, u32[]{:S(2)}, u32[]{:S(2)}) %collective-permute-start.22) | collective-permute-done | bytes 524320 | tf_op jit(solution)/shard_map/ppermute | solution.py:20
  179.7 1.3 collective-permute-start.23
  181.0 0.6 collective-permute-start.30
  181.6 0.3 convert_add_fusion.3
  182.0 0.6 collective-permute-start.15
  182.6 5.5 %collective-permute-done.30 = bf16[256,640]{1,0:T(8,128)(2,1)S(1)} collective-permute-done((bf16[256,640]{1,0:T(8,128)(2,1)S(1)}, bf16[256,640]{1,0:T(8,128)(2,1)S(1)}, u32[]{:S(2)}, u32[]{:S(2)}) %collective-permute-start.30) | collective-permute-done | bytes 327712 | tf_op jit(solution)/shard_map/ppermute | solution.py:20
  188.3 2.4 %collective-permute-done.17 = bf16[1024,256]{1,0:T(8,128)(2,1)S(1)} collective-permute-done((bf16[1024,256]{1,0:T(8,128)(2,1)S(1)}, bf16[1024,256]{1,0:T(8,128)(2,1)S(1)}, u32[]{:S(2)}, u32[]{:S(2)}) %collective-permute-start.17) | collective-permute-done | bytes 524320 | tf_op jit(solution)/shard_map/ppermute | solution.py:20
  190.7 0.7 fusion.7
  191.5 0.6 collective-permute-start.24
  192.1 6.7 %collective-permute-done.15 = bf16[1024,256]{1,0:T(8,128)(2,1)S(1)} collective-permute-done((bf16[1024,256]{1,0:T(8,128)(2,1)S(1)}, bf16[1024,256]{1,0:T(8,128)(2,1)S(1)}, u32[]{:S(2)}, u32[]{:S(2)}) %collective-permute-start.15) | collective-permute-done | bytes 524320 | tf_op jit(solution)/shard_map/ppermute | solution.py:20
  198.8 1.0 fusion.6
  199.8 2.5 %shard_map.101 = (f32[4096,128]{1,0:T(8,128)}, f32[2,128,512]{2,1,0:T(8,128)}) custom-call(s32[5]{0:T(128)S(1)} %stack.32.refs_0_.refs_3_, bf16[512,640]{1,0:T(8,128)(2,1)S(1)} %pad_maximum_fusion.1.refs_1_, bf16[512,640]{1,0:T(8,128)(2,1)S(1)} %collective-permute-done.31.refs_2_), custom_call_target="tpu_custom_call" | custom-call | tf_op jit(solution)/shard_map/pallas_call | solution.py:277
  202.4 1.3 add_convert_fusion
  (70 shorter events, 3.6 us)
Async XLA Ops:
  0.6 7.6 %copy-start = (bf16[512,4,2,128]{3,2,1,0:T(2,128)(2,1)S(1)}, bf16[512,4,2,128]{3,2,1,0:T(2,128)(2,1)}, u32[]{:S(2)}) copy-start(bf16[512,4,2,128]{3,2,1,0:T(2,128)(2,1)} %param.7) | copy-start | bytes 3145732
  0.6 15.2 %collective-permute-start = (bf16[1024,256]{1,0:T(8,128)(2,1)}, bf16[1024,256]{1,0:T(8,128)(2,1)S(1)}, u32[]{:S(2)}, u32[]{:S(2)}) collective-permute-start(bf16[1024,256]{1,0:T(8,128)(2,1)} %refs_1_.1), channel_id=1, source_target_pairs={{0,1},{1,0},{2,3},{3,2},{4,5},{5,4},{6,7},{7,6},{8,9},{9,8},{10,11... | collective-permute-start | bytes 1572872 | tf_op jit(solution)/shard_map/ppermute | solution.py:20
  3.7 14.7 %collective-permute-start.3 = (bf16[1024,256]{1,0:T(8,128)(2,1)}, bf16[1024,256]{1,0:T(8,128)(2,1)S(1)}, u32[]{:S(2)}, u32[]{:S(2)}) collective-permute-start(bf16[1024,256]{1,0:T(8,128)(2,1)} %refs_1_.1), channel_id=1, source_target_pairs={{0,8},{2,10},{4,12},{6,14},{8,16},{10,18},{12,20},{14,22},{16,24},... | collective-permute-start | bytes 1572872 | tf_op jit(solution)/shard_map/ppermute | solution.py:25
  10.6 1.3 copy-start.4
  11.7 6.7 %copy-start.2 = (bf16[1024,256]{1,0:T(8,128)(2,1)S(1)}, bf16[1024,256]{1,0:T(8,128)(2,1)}, u32[]{:S(2)}) copy-start(bf16[1024,256]{1,0:T(8,128)(2,1)} %refs_1_.1) | copy-start | bytes 1572868
  12.6 8.5 %copy-start.3 = (bf16[1024,256]{1,0:T(8,128)(2,1)S(1)}, bf16[1024,256]{1,0:T(8,128)(2,1)}, u32[]{:S(2)}) copy-start(bf16[1024,256]{1,0:T(8,128)(2,1)} %refs_4_.3) | copy-start | bytes 1572868
  18.4 12.6 %collective-permute-start.4 = (bf16[1024,256]{1,0:T(8,128)(2,1)S(1)}, bf16[1024,256]{1,0:T(8,128)(2,1)S(1)}, u32[]{:S(2)}, u32[]{:S(2)}) collective-permute-start(bf16[1024,256]{1,0:T(8,128)(2,1)S(1)} %broadcast_select_fusion), channel_id=1, source_target_pairs={{0,4},{2,6},{4,0},{6,2},{8,12},{10,14},{12,8},{14,10},{16,20},{18,... | collective-permute-start | bytes 1572872 | tf_op jit(solution)/shard_map/ppermute | solution.py:20
  20.0 11.5 %collective-permute-start.1 = (bf16[1024,256]{1,0:T(8,128)(2,1)S(1)}, bf16[1024,256]{1,0:T(8,128)(2,1)S(1)}, u32[]{:S(2)}, u32[]{:S(2)}) collective-permute-start(bf16[1024,256]{1,0:T(8,128)(2,1)S(1)} %copy-done.2), channel_id=1, source_target_pairs={{0,2},{2,0},{4,6},{6,4},{8,10},{10,8},{12,14},{14,12},{16,18},{18,... | collective-permute-start | bytes 1572872 | tf_op jit(solution)/shard_map/ppermute | solution.py:20
  20.0 11.5 %collective-permute-start.2 = (bf16[1024,256]{1,0:T(8,128)(2,1)S(1)}, bf16[1024,256]{1,0:T(8,128)(2,1)S(1)}, u32[]{:S(2)}, u32[]{:S(2)}) collective-permute-start(bf16[1024,256]{1,0:T(8,128)(2,1)S(1)} %collective-permute-done.refs_2_), channel_id=1, source_target_pairs={{0,2},{2,0},{4,6},{6,4},{8,10},{10,8},{12,14},{14,12},{16,18},{18,... | collective-permute-start | bytes 1572872 | tf_op jit(solution)/shard_map/ppermute | solution.py:20
  20.5 16.3 %collective-permute-start.8 = (bf16[1024,256]{1,0:T(8,128)(2,1)S(1)}, bf16[1024,256]{1,0:T(8,128)(2,1)S(1)}, u32[]{:S(2)}, u32[]{:S(2)}) collective-permute-start(bf16[1024,256]{1,0:T(8,128)(2,1)S(1)} %collective-permute-done.3.refs_1_), channel_id=1, source_target_pairs={{0,1},{1,0},{2,3},{3,2},{4,5},{5,4},{6,7},{7,6},{8,9},{9,8},{10,11... | collective-permute-start | bytes 1572872 | tf_op jit(solution)/shard_map/ppermute | solution.py:20
  21.1 35.8 %collective-permute-start.11 = (bf16[1024,256]{1,0:T(8,128)(2,1)S(1)}, bf16[1024,256]{1,0:T(8,128)(2,1)S(1)}, u32[]{:S(2)}, u32[]{:S(2)}) collective-permute-start(bf16[1024,256]{1,0:T(8,128)(2,1)S(1)} %copy-done.3), channel_id=1, source_target_pairs={{0,1},{1,0},{2,3},{3,2},{4,5},{5,4},{6,7},{7,6},{8,9},{9,8},{10,11... | collective-permute-start | bytes 1572872 | tf_op jit(solution)/shard_map/ppermute | solution.py:20
  31.0 25.8 %collective-permute-start.5 = (bf16[1024,256]{1,0:T(8,128)(2,1)S(1)}, bf16[1024,256]{1,0:T(8,128)(2,1)S(1)}, u32[]{:S(2)}, u32[]{:S(2)}) collective-permute-start(bf16[1024,256]{1,0:T(8,128)(2,1)S(1)} %collective-permute-done.4.refs_1_), channel_id=1, source_target_pairs={{0,1},{1,0},{2,3},{3,2},{4,5},{5,4},{6,7},{7,6},{8,9},{9,8},{10,11... | collective-permute-start | bytes 1572872 | tf_op jit(solution)/shard_map/ppermute | solution.py:20
  36.7 20.6 %collective-permute-start.9 = (bf16[1024,256]{1,0:T(8,128)(2,1)S(1)}, bf16[1024,256]{1,0:T(8,128)(2,1)S(1)}, u32[]{:S(2)}, u32[]{:S(2)}) collective-permute-start(bf16[1024,256]{1,0:T(8,128)(2,1)S(1)} %collective-permute-done.3.refs_1_), channel_id=1, source_target_pairs={{0,2},{2,0},{4,6},{6,4},{8,10},{10,8},{12,14},{14,12},{16,18},{18,... | collective-permute-start | bytes 1572872 | tf_op jit(solution)/shard_map/ppermute | solution.py:20
  36.8 27.5 %collective-permute-start.10 = (bf16[1024,256]{1,0:T(8,128)(2,1)S(1)}, bf16[1024,256]{1,0:T(8,128)(2,1)S(1)}, u32[]{:S(2)}, u32[]{:S(2)}) collective-permute-start(bf16[1024,256]{1,0:T(8,128)(2,1)S(1)} %collective-permute-done.8.refs_2_), channel_id=1, source_target_pairs={{0,2},{2,0},{4,6},{6,4},{8,10},{10,8},{12,14},{14,12},{16,18},{18,... | collective-permute-start | bytes 1572872 | tf_op jit(solution)/shard_map/ppermute | solution.py:20
  37.3 31.7 %collective-permute-start.6 = (bf16[1024,256]{1,0:T(8,128)(2,1)S(1)}, bf16[1024,256]{1,0:T(8,128)(2,1)S(1)}, u32[]{:S(2)}, u32[]{:S(2)}) collective-permute-start(bf16[1024,256]{1,0:T(8,128)(2,1)S(1)} %collective-permute-done.4.refs_1_), channel_id=1, source_target_pairs={{0,2},{2,0},{4,6},{6,4},{8,10},{10,8},{12,14},{14,12},{16,18},{18,... | collective-permute-start | bytes 1572872 | tf_op jit(solution)/shard_map/ppermute | solution.py:20
  56.8 12.2 %collective-permute-start.7 = (bf16[1024,256]{1,0:T(8,128)(2,1)S(1)}, bf16[1024,256]{1,0:T(8,128)(2,1)S(1)}, u32[]{:S(2)}, u32[]{:S(2)}) collective-permute-start(bf16[1024,256]{1,0:T(8,128)(2,1)S(1)} %collective-permute-done.5.refs_2_), channel_id=1, source_target_pairs={{0,2},{2,0},{4,6},{6,4},{8,10},{10,8},{12,14},{14,12},{16,18},{18,... | collective-permute-start | bytes 1572872 | tf_op jit(solution)/shard_map/ppermute | solution.py:20
  56.8 17.0 %collective-permute-start.12 = (bf16[1024,256]{1,0:T(8,128)(2,1)S(1)}, bf16[1024,256]{1,0:T(8,128)(2,1)S(1)}, u32[]{:S(2)}, u32[]{:S(2)}) collective-permute-start(bf16[1024,256]{1,0:T(8,128)(2,1)S(1)} %copy-done.3), channel_id=1, source_target_pairs={{0,2},{2,0},{4,6},{6,4},{8,10},{10,8},{12,14},{14,12},{16,18},{18,... | collective-permute-start | bytes 1572872 | tf_op jit(solution)/shard_map/ppermute | solution.py:20
  57.3 16.5 %collective-permute-start.13 = (bf16[1024,256]{1,0:T(8,128)(2,1)S(1)}, bf16[1024,256]{1,0:T(8,128)(2,1)S(1)}, u32[]{:S(2)}, u32[]{:S(2)}) collective-permute-start(bf16[1024,256]{1,0:T(8,128)(2,1)S(1)} %collective-permute-done.11.refs_5_), channel_id=1, source_target_pairs={{0,2},{2,0},{4,6},{6,4},{8,10},{10,8},{12,14},{14,12},{16,18},{18,... | collective-permute-start | bytes 1572872 | tf_op jit(solution)/shard_map/ppermute | solution.py:20
  79.2 73.7 %collective-permute-start.18 = (bf16[1024,512]{1,0:T(8,128)(2,1)S(1)}, bf16[1024,512]{1,0:T(8,128)(2,1)S(1)}, u32[]{:S(2)}, u32[]{:S(2)}) collective-permute-start(bf16[1024,512]{1,0:T(8,128)(2,1)S(1)} %get-tuple-element.87), channel_id=1, source_target_pairs={{0,2},{2,0},{4,6},{6,4},{8,10},{10,8},{12,14},{14,12},{16,18},{18,... | collective-permute-start | bytes 3145736 | tf_op jit(solution)/shard_map/ppermute | solution.py:20
  101.2 14.7 %collective-permute-start.25 = (bf16[256,640]{1,0:T(8,128)(2,1)S(1)}, bf16[256,640]{1,0:T(8,128)(2,1)S(1)}, u32[]{:S(2)}, u32[]{:S(2)}) collective-permute-start(bf16[256,640]{1,0:T(8,128)(2,1)S(1)} %get-tuple-element.97), channel_id=1, source_target_pairs={{0,4},{2,6},{4,0},{6,2},{8,12},{10,14},{12,8},{14,10},{16,20},{18,... | collective-permute-start | bytes 983048 | tf_op jit(solution)/shard_map/ppermute | solution.py:20
  107.9 50.4 %collective-permute-start.21 = (bf16[1024,512]{1,0:T(8,128)(2,1)S(1)}, bf16[1024,512]{1,0:T(8,128)(2,1)S(1)}, u32[]{:S(2)}, u32[]{:S(2)}) collective-permute-start(bf16[1024,512]{1,0:T(8,128)(2,1)S(1)} %get-tuple-element.89), channel_id=1, source_target_pairs={{0,2},{2,0},{4,6},{6,4},{8,10},{10,8},{12,14},{14,12},{16,18},{18,... | collective-permute-start | bytes 3145736 | tf_op jit(solution)/shard_map/ppermute | solution.py:20
  116.5 33.0 %collective-permute-start.26 = (bf16[128,640]{1,0:T(8,128)(2,1)S(1)}, bf16[128,640]{1,0:T(8,128)(2,1)S(1)}, u32[]{:S(2)}, u32[]{:S(2)}) collective-permute-start(bf16[128,640]{1,0:T(8,128)(2,1)S(1)} %get-tuple-element.99), channel_id=1, source_target_pairs={{0,8},{2,10},{4,12},{6,14},{8,0},{10,2},{12,4},{14,6},{16,24},{18,... | collective-permute-start | bytes 491528 | tf_op jit(solution)/shard_map/ppermute | solution.py:20
  145.9 23.4 %collective-permute-start.16 = (bf16[1024,512]{1,0:T(8,128)(2,1)S(1)}, bf16[1024,512]{1,0:T(8,128)(2,1)S(1)}, u32[]{:S(2)}, u32[]{:S(2)}) collective-permute-start(bf16[1024,512]{1,0:T(8,128)(2,1)S(1)} %get-tuple-element.85), channel_id=1, source_target_pairs={{0,2},{2,0},{4,6},{6,4},{8,10},{10,8},{12,14},{14,12},{16,18},{18,... | collective-permute-start | bytes 3145736 | tf_op jit(solution)/shard_map/ppermute | solution.py:20
  150.1 5.4 %collective-permute-start.27 = (bf16[64,640]{1,0:T(8,128)(2,1)S(1)}, bf16[64,640]{1,0:T(8,128)(2,1)S(1)}, u32[]{:S(2)}, u32[]{:S(2)}) collective-permute-start(bf16[64,640]{1,0:T(8,128)(2,1)S(1)} %get-tuple-element.101), channel_id=1, source_target_pairs={{0,16},{2,18},{4,20},{6,22},{8,24},{10,26},{12,28},{14,30},{16,0},... | collective-permute-start | bytes 245768 | tf_op jit(solution)/shard_map/ppermute | solution.py:20
  153.3 14.9 %collective-permute-start.19 = (bf16[1024,256]{1,0:T(8,128)(2,1)S(1)}, bf16[1024,256]{1,0:T(8,128)(2,1)S(1)}, u32[]{:S(2)}, u32[]{:S(2)}) collective-permute-start(bf16[1024,256]{1,0:T(8,128)(2,1)S(1)} %slice.145), channel_id=1, source_target_pairs={{0,1},{1,0},{2,3},{3,2},{4,5},{5,4},{6,7},{7,6},{8,9},{9,8},{10,11... | collective-permute-start | bytes 1572872 | tf_op jit(solution)/shard_map/ppermute | solution.py:20
  154.4 27.2 %collective-permute-start.14 = (bf16[1024,512]{1,0:T(8,128)(2,1)S(1)}, bf16[1024,512]{1,0:T(8,128)(2,1)S(1)}, u32[]{:S(2)}, u32[]{:S(2)}) collective-permute-start(bf16[1024,512]{1,0:T(8,128)(2,1)S(1)} %get-tuple-element.78), channel_id=1, source_target_pairs={{0,2},{2,0},{4,6},{6,4},{8,10},{10,8},{12,14},{14,12},{16,18},{18,... | collective-permute-start | bytes 3145736 | tf_op jit(solution)/shard_map/ppermute | solution.py:20
  155.5 13.5 %collective-permute-start.28 = (bf16[64,640]{1,0:T(8,128)(2,1)S(1)}, bf16[64,640]{1,0:T(8,128)(2,1)S(1)}, u32[]{:S(2)}, u32[]{:S(2)}) collective-permute-start(bf16[64,640]{1,0:T(8,128)(2,1)S(1)} %shard_map.100), channel_id=1, source_target_pairs={{0,16},{2,18},{4,20},{6,22},{8,24},{10,26},{12,28},{14,30},{16,0},... | collective-permute-start | bytes 245768 | tf_op jit(solution)/shard_map/ppermute | solution.py:20
  158.7 20.7 %collective-permute-start.22 = (bf16[1024,256]{1,0:T(8,128)(2,1)S(1)}, bf16[1024,256]{1,0:T(8,128)(2,1)S(1)}, u32[]{:S(2)}, u32[]{:S(2)}) collective-permute-start(bf16[1024,256]{1,0:T(8,128)(2,1)S(1)} %slice.144), channel_id=1, source_target_pairs={{0,1},{1,0},{2,3},{3,2},{4,5},{5,4},{6,7},{7,6},{8,9},{9,8},{10,11... | collective-permute-start | bytes 1572872 | tf_op jit(solution)/shard_map/ppermute | solution.py:20
  168.4 11.0 %collective-permute-start.20 = (bf16[1024,256]{1,0:T(8,128)(2,1)S(1)}, bf16[1024,256]{1,0:T(8,128)(2,1)S(1)}, u32[]{:S(2)}, u32[]{:S(2)}) collective-permute-start(bf16[1024,256]{1,0:T(8,128)(2,1)S(1)} %fusion.4), channel_id=1, source_target_pairs={{0,4},{2,6},{4,0},{6,2},{8,12},{10,14},{12,8},{14,10},{16,20},{18,... | collective-permute-start | bytes 1572872 | tf_op jit(solution)/shard_map/ppermute | solution.py:20
  169.0 11.9 %collective-permute-start.29 = (bf16[128,640]{1,0:T(8,128)(2,1)S(1)}, bf16[128,640]{1,0:T(8,128)(2,1)S(1)}, u32[]{:S(2)}, u32[]{:S(2)}) collective-permute-start(bf16[128,640]{1,0:T(8,128)(2,1)S(1)} %pad_maximum_fusion.4), channel_id=1, source_target_pairs={{0,8},{2,10},{4,12},{6,14},{8,0},{10,2},{12,4},{14,6},{16,24},{18,... | collective-permute-start | bytes 491528 | tf_op jit(solution)/shard_map/ppermute | solution.py:20
  169.8 20.9 %collective-permute-start.17 = (bf16[1024,256]{1,0:T(8,128)(2,1)S(1)}, bf16[1024,256]{1,0:T(8,128)(2,1)S(1)}, u32[]{:S(2)}, u32[]{:S(2)}) collective-permute-start(bf16[1024,256]{1,0:T(8,128)(2,1)S(1)} %slice.146), channel_id=1, source_target_pairs={{0,1},{1,0},{2,3},{3,2},{4,5},{5,4},{6,7},{7,6},{8,9},{9,8},{10,11... | collective-permute-start | bytes 1572872 | tf_op jit(solution)/shard_map/ppermute | solution.py:20
  179.7 11.1 %collective-permute-start.23 = (bf16[1024,256]{1,0:T(8,128)(2,1)S(1)}, bf16[1024,256]{1,0:T(8,128)(2,1)S(1)}, u32[]{:S(2)}, u32[]{:S(2)}) collective-permute-start(bf16[1024,256]{1,0:T(8,128)(2,1)S(1)} %fusion.3), channel_id=1, source_target_pairs={{8,0},{10,2},{12,4},{14,6},{16,8},{18,10},{20,12},{22,14},{24,16},... | collective-permute-start | bytes 1572872 | tf_op jit(solution)/shard_map/ppermute | solution.py:25
  181.0 7.1 %collective-permute-start.30 = (bf16[256,640]{1,0:T(8,128)(2,1)S(1)}, bf16[256,640]{1,0:T(8,128)(2,1)S(1)}, u32[]{:S(2)}, u32[]{:S(2)}) collective-permute-start(bf16[256,640]{1,0:T(8,128)(2,1)S(1)} %pad_maximum_fusion.2), channel_id=1, source_target_pairs={{0,4},{2,6},{4,0},{6,2},{8,12},{10,14},{12,8},{14,10},{16,20},{18,... | collective-permute-start | bytes 983048 | tf_op jit(solution)/shard_map/ppermute | solution.py:20
  182.0 16.7 %collective-permute-start.15 = (bf16[1024,256]{1,0:T(8,128)(2,1)S(1)}, bf16[1024,256]{1,0:T(8,128)(2,1)S(1)}, u32[]{:S(2)}, u32[]{:S(2)}) collective-permute-start(bf16[1024,256]{1,0:T(8,128)(2,1)S(1)} %slice.147), channel_id=1, source_target_pairs={{0,1},{1,0},{2,3},{3,2},{4,5},{5,4},{6,7},{7,6},{8,9},{9,8},{10,11... | collective-permute-start | bytes 1572872 | tf_op jit(solution)/shard_map/ppermute | solution.py:20
  188.2 11.6 %collective-permute-start.31 = (bf16[512,640]{1,0:T(8,128)(2,1)S(1)}, bf16[512,640]{1,0:T(8,128)(2,1)S(1)}, u32[]{:S(2)}, u32[]{:S(2)}) collective-permute-start(bf16[512,640]{1,0:T(8,128)(2,1)S(1)} %pad_maximum_fusion.1.refs_1_), channel_id=1, source_target_pairs={{0,2},{2,0},{4,6},{6,4},{8,10},{10,8},{12,14},{14,12},{16,18},{18,... | collective-permute-start | bytes 1966088 | tf_op jit(solution)/shard_map/ppermute | solution.py:20
  191.5 10.8 %collective-permute-start.24 = (f32[2,1024]{1,0:T(2,128)S(1)}, f32[2,1024]{1,0:T(2,128)S(1)}, u32[]{:S(2)}, u32[]{:S(2)}) collective-permute-start(f32[2,1024]{1,0:T(2,128)S(1)} %pad_maximum_fusion.5), channel_id=1, source_target_pairs={{0,1},{1,0},{2,3},{3,2},{4,5},{5,4},{6,7},{7,6},{8,9},{9,8},{10,11... | collective-permute-start | bytes 24584 | tf_op jit(solution)/shard_map/ppermute | solution.py:20
  198.8 4.9 %copy-start.1 = (bf16[512,4,2,128]{3,2,1,0:T(2,128)(2,1)S(1)}, bf16[512,4,2,128]{3,2,1,0:T(2,128)(2,1)}, u32[]{:S(2)}) copy-start(bf16[512,4,2,128]{3,2,1,0:T(2,128)(2,1)} %param.7) | copy-start | bytes 3145732
